TPU v7x, 32 devices: a whole 2x2x4 slice. The times are simulated.
32 devices in a mesh: rows: 16 (over z, y, x), seq: 2 (over core).
Axes of the slice: x: 2, y: 2, z: 4, core: 2. Of those that a mesh axis runs over, the one named last changes fastest.
Arguments:
- tokens: bfloat16 [64, 512, 1024], P('rows', 'seq'), may hold values from -6 to 6
- segments: int32 [64, 512], P('rows'), may hold values from -1 to 9, as said below
- pad_mask: int32 [64, 512], P('rows', 'seq'), may hold values from 0 to 1, as said below
- dest_shard: int32 [64, 10], P('rows'), may hold values from 0 to 1, as said below
- dest_slot: int32 [64, 10], P('rows'), may hold values from 0 to 19, as said below
- ln1_gain: bfloat16 [1024], P(('rows', 'seq')), may hold values from 0.5 to 1.5
- ln1_bias: bfloat16 [1024], P(('rows', 'seq')), may hold values from -1.796875 to 1.796875
- qkv_weight: bfloat16 [1024, 3072], P(('rows', 'seq')), may hold values from -0.1875 to 0.1875
- qv_bias: bfloat16 [2, 1024], P(None, ('rows', 'seq')), may hold values from -3 to 3
- out_weight: bfloat16 [1024, 1024], P(('rows', 'seq')), may hold values from -1.5 to 1.5
- out_bias: bfloat16 [1024], P(('rows', 'seq')), may hold values from -1.796875 to 1.796875
- ln2_gain: bfloat16 [1024], P(('rows', 'seq')), may hold values from 0.5 to 1.5
- ln2_bias: bfloat16 [1024], P(('rows', 'seq')), may hold values from -1.796875 to 1.796875
- fc1_weight: bfloat16 [1024, 4096], P(('rows', 'seq')), may hold values from -0.1875 to 0.1875
- fc1_bias: bfloat16 [4096], P(('rows', 'seq')), may hold values from -3 to 3
- fc2_weight: bfloat16 [4096, 1024], P(('rows', 'seq')), may hold values from -0.09375 to 0.09375
- fc2_bias: bfloat16 [1024], P(('rows', 'seq')), may hold values from -1.796875 to 1.796875
- learn_gain: bfloat16 [1024], replicated, may hold values from 0.5 to 1.5
- learn_bias: bfloat16 [1024], replicated, may hold values from -1.796875 to 1.796875
- maps_weight: bfloat16 [8, 1024], replicated, may hold values from -0.1875 to 0.1875
- maps_bias: bfloat16 [8], replicated, may hold values from -4 to 4
- out_grad: bfloat16 [16, 40, 8, 1024], P('rows', 'seq'), may hold values from -384 to 384
Outputs:
- pooled: bfloat16 [16, 40, 8, 1024], P('rows', 'seq')
- grad_tokens: float32 [64, 512, 1024], P('rows', 'seq')
- grad_ln1_gain: float32 [1024], P(('rows', 'seq'))
- grad_ln1_bias: float32 [1024], P(('rows', 'seq'))
- grad_qkv_weight: float32 [1024, 3072], P(('rows', 'seq'))
- grad_qv_bias: float32 [2, 1024], P(None, ('rows', 'seq'))
- grad_out_weight: float32 [1024, 1024], P(('rows', 'seq'))
- grad_out_bias: float32 [1024], P(('rows', 'seq'))
- grad_ln2_gain: float32 [1024], P(('rows', 'seq'))
- grad_ln2_bias: float32 [1024], P(('rows', 'seq'))
- grad_fc1_weight: float32 [1024, 4096], P(('rows', 'seq'))
- grad_fc1_bias: float32 [4096], P(('rows', 'seq'))
- grad_fc2_weight: float32 [4096, 1024], P(('rows', 'seq'))
- grad_fc2_bias: float32 [1024], P(('rows', 'seq'))
- grad_learn_gain: float32 [1024], replicated
- grad_learn_bias: float32 [1024], replicated
- grad_maps_weight: float32 [8, 1024], replicated
- grad_maps_bias: float32 [8], replicated
Inputs may be any that keep to these rules, and one draw needn't show every extreme that they name: `segments`: in each row images are runs of consecutive slots from slot 0, with ids 0, 1, 2, ... in order, each 49, 100 or 196 slots long; the slots after the last image are padding with id -1; in every draw some row holds 10 images. `pad_mask`: 1 exactly on the slots that belong to an image. `dest_shard`: over the 4 rows of one index of rows, records in order (row by row, image id within a row), the k-th existing image (k from 0) goes to seq index (k + c) mod 2 for a c drawn for that index; records without an image hold arbitrary values. `dest_slot`: the k-th existing image of an index of rows takes slot 19 - k // 2, so existing images of one index of rows have distinct (shard, slot) pairs and each device's slots fill from 19 downward; records without an image hold arbitrary slots.
All inputs are finite; a program needn't handle non-finite values.
Results may differ from a plain program's by a relative error of at most 0.0085.
Values may be sent and summed in bfloat16 or wider, within the bound.
No kernel may reach another device: no remote copies, remote signals or barrier semaphores. Data moves between devices by JAX's collectives and lax.ppermute only.
A program may use at most 256 MiB of HBM per device.

v0:
```python
import jax
import jax.numpy as jnp
from jax import lax
from jax.sharding import PartitionSpec as P

HEAD_DIM = 64
NTOK = 8
IMG_ROW = 10


EPSILON = 1e-06
NEGATIVE = -1e30
HIGHEST = lax.Precision.HIGHEST


def dot_plain(former, latter, precision=None):
    return jnp.dot(former, latter, precision=precision, preferred_element_type=jnp.float32)


def dot_first(former, latter, precision=None):
    return lax.dot_general(
        former,
        latter,
        (((0,), (0,)), ((), ())),
        precision=precision,
        preferred_element_type=jnp.float32,
    )


def dot_second(former, latter, precision=None):
    return lax.dot_general(
        former,
        latter,
        (((1,), (1,)), ((), ())),
        precision=precision,
        preferred_element_type=jnp.float32,
    )


def norm_forward(values, scale_vec, shift_vec):
    centred = values - jnp.mean(values, axis=-1, keepdims=True)
    inverse = lax.rsqrt(jnp.mean(centred * centred, axis=-1, keepdims=True) + EPSILON)
    normed = centred * inverse
    return (normed * scale_vec + shift_vec, normed, inverse)


def norm_backward(grad_out, normed, inverse, scale_vec):
    grad_unit = grad_out * scale_vec
    grad_in = inverse * (
        grad_unit
        - jnp.mean(grad_unit, axis=-1, keepdims=True)
        - normed * jnp.mean(grad_unit * normed, axis=-1, keepdims=True)
    )
    return (grad_in, jnp.sum(grad_out * normed, axis=0), jnp.sum(grad_out, axis=0))


def exact_gelu(values):
    return jax.nn.gelu(values, approximate=False)


def block_scores(queries, key_vecs, own_ids, row_ids):
    scale_factor = queries.shape[-1] ** (-0.5)
    scores = (
        jnp.einsum("bqhe,bkhe->bhqk", queries, key_vecs, preferred_element_type=jnp.float32)
        * scale_factor
    )
    allowed = (own_ids[:, :, None] == row_ids[:, None, :])[:, None]
    return jnp.where(allowed, scores, NEGATIVE)


def attend_block(block_inputs):
    queries, key_vecs, value_vecs, own_ids, row_ids = block_inputs
    scores = block_scores(queries, key_vecs, own_ids, row_ids)
    largest = jnp.max(scores, axis=-1, keepdims=True)
    exponent = jnp.exp(scores - largest)
    summed = jnp.sum(exponent, axis=-1, keepdims=True)
    probs_low = (exponent / summed).astype(jnp.bfloat16)
    mixed_out = jnp.einsum(
        "bhqk,bkhe->bqhe", probs_low, value_vecs, preferred_element_type=jnp.float32
    )
    return (mixed_out, (largest + jnp.log(summed))[..., 0])


def attend_back(block_inputs):
    queries, key_vecs, value_vecs, own_ids, row_ids, log_total, grad_mixed = block_inputs
    scale_factor = queries.shape[-1] ** (-0.5)
    scores = block_scores(queries, key_vecs, own_ids, row_ids)
    probs = jnp.exp(scores - log_total[..., None])
    grad_probs = jnp.einsum(
        "bqhe,bkhe->bhqk", grad_mixed, value_vecs, preferred_element_type=jnp.float32
    )
    inner = jnp.sum(probs * grad_probs, axis=-1, keepdims=True)
    grad_scores = (probs * (grad_probs - inner)).astype(jnp.bfloat16)
    grad_queries = (
        jnp.einsum("bhqk,bkhe->bqhe", grad_scores, key_vecs, preferred_element_type=jnp.float32)
        * scale_factor
    )
    grad_keys = (
        jnp.einsum("bhqk,bqhe->bkhe", grad_scores, queries, preferred_element_type=jnp.float32)
        * scale_factor
    )
    grad_values = jnp.einsum(
        "bhqk,bqhe->bkhe",
        probs.astype(jnp.bfloat16),
        grad_mixed,
        preferred_element_type=jnp.float32,
    )
    return (grad_queries, grad_keys, grad_values)


def shards(
    tokens,
    segments,
    pad_mask,
    dest_shard,
    dest_slot,
    ln1_gain,
    ln1_bias,
    qkv_weight,
    qv_bias,
    out_weight,
    out_bias,
    ln2_gain,
    ln2_bias,
    fc1_weight,
    fc1_bias,
    fc2_weight,
    fc2_bias,
    learn_gain,
    learn_bias,
    maps_weight,
    maps_bias,
    out_grad,
):
    (
        norm1_gain,
        norm1_shift,
        qkv_full,
        qv_full,
        out_full,
        out_shift,
        norm2_gain,
        norm2_shift,
        fc1_full,
        fc1_shift,
        fc2_full,
        fc2_shift,
    ) = (
        lax.all_gather(ln1_gain, ("rows", "seq"), axis=0, tiled=True),
        lax.all_gather(ln1_bias, ("rows", "seq"), axis=0, tiled=True),
        lax.all_gather(qkv_weight, ("rows", "seq"), axis=0, tiled=True),
        lax.all_gather(qv_bias, ("rows", "seq"), axis=1, tiled=True),
        lax.all_gather(out_weight, ("rows", "seq"), axis=0, tiled=True),
        lax.all_gather(out_bias, ("rows", "seq"), axis=0, tiled=True),
        lax.all_gather(ln2_gain, ("rows", "seq"), axis=0, tiled=True),
        lax.all_gather(ln2_bias, ("rows", "seq"), axis=0, tiled=True),
        lax.all_gather(fc1_weight, ("rows", "seq"), axis=0, tiled=True),
        lax.all_gather(fc1_bias, ("rows", "seq"), axis=0, tiled=True),
        lax.all_gather(fc2_weight, ("rows", "seq"), axis=0, tiled=True),
        lax.all_gather(fc2_bias, ("rows", "seq"), axis=0, tiled=True),
    )
    rows_here, slots_here, model_width = tokens.shape
    seq_count = lax.axis_size("seq")
    seq_place = lax.axis_index("seq")
    row_len = slots_here * seq_count
    head_count = model_width // HEAD_DIM
    count_tok = rows_here * slots_here
    records = rows_here * IMG_ROW
    capacity = records // seq_count
    seg_held = lax.dynamic_slice_in_dim(segments, seq_place * slots_here, slots_here, 1)
    group_size = 2
    per_row = tokens.shape[1]
    block_count = rows_here // group_size
    mask_flat = pad_mask.reshape(count_tok).astype(jnp.float32)
    inputs = tokens.reshape(count_tok, model_width).astype(jnp.float32)
    normed1_out, normed1, inverse1 = norm_forward(
        inputs, norm1_gain.astype(jnp.float32), norm1_shift.astype(jnp.float32)
    )
    attn_in = normed1_out.astype(jnp.bfloat16)
    qkv_out = dot_plain(attn_in, qkv_full)
    qv_vals = qv_full.astype(jnp.float32)
    queries = (qkv_out[:, :model_width] + qv_vals[0]).astype(jnp.bfloat16)
    keys_own = qkv_out[:, model_width : 2 * model_width].astype(jnp.bfloat16)
    values_own = (qkv_out[:, 2 * model_width :] + qv_vals[1]).astype(jnp.bfloat16)
    keys_row, values_row = (
        lax.all_gather(
            keys_own.reshape(rows_here, slots_here, model_width), "seq", axis=1, tiled=True
        ),
        lax.all_gather(
            values_own.reshape(rows_here, slots_here, model_width), "seq", axis=1, tiled=True
        ),
    )
    q_blocks = queries.reshape(block_count, group_size, per_row, head_count, HEAD_DIM)
    k_blocks = keys_row.reshape(block_count, group_size, row_len, head_count, HEAD_DIM)
    v_blocks = values_row.reshape(block_count, group_size, row_len, head_count, HEAD_DIM)
    own_blocks = seg_held.reshape(block_count, group_size, per_row)
    seg_blocks = segments.reshape(block_count, group_size, row_len)
    mixed_out, log_total = lax.map(
        attend_block, (q_blocks, k_blocks, v_blocks, own_blocks, seg_blocks)
    )
    mixed_low = mixed_out.reshape(count_tok, model_width).astype(jnp.bfloat16)
    resid1 = inputs + dot_plain(mixed_low, out_full) + out_shift.astype(jnp.float32)
    normed2_out, normed2, inverse2 = norm_forward(
        resid1, norm2_gain.astype(jnp.float32), norm2_shift.astype(jnp.float32)
    )
    mlp_in = normed2_out.astype(jnp.bfloat16)
    hidden = dot_plain(mlp_in, fc1_full) + fc1_shift.astype(jnp.float32)
    activated, gelu_back = jax.vjp(exact_gelu, hidden)
    activated_low = activated.astype(jnp.bfloat16)
    resid2 = resid1 + dot_plain(activated_low, fc2_full) + fc2_shift.astype(jnp.float32)
    learn_scale = learn_gain.astype(jnp.float32)
    normed3_out, normed3, inverse3 = norm_forward(
        resid2, learn_scale, learn_bias.astype(jnp.float32)
    )
    map_weight = maps_weight.astype(jnp.float32)
    logits = dot_second(normed3_out, map_weight, HIGHEST) + maps_bias.astype(jnp.float32)
    sigmas = jax.nn.sigmoid(logits)
    map_vals = sigmas * mask_flat[:, None]
    own_flat = seg_held.reshape(count_tok)
    row_index = jnp.arange(count_tok, dtype=jnp.int32) // per_row
    owner_ids = jnp.where(own_flat >= 0, row_index * IMG_ROW + own_flat, -1)
    select = (owner_ids[:, None] == jnp.arange(records, dtype=jnp.int32)[None, :]).astype(
        jnp.float32
    )
    token_weights = (select[:, :, None] * map_vals[:, None, :]).reshape(count_tok, records * NTOK)
    partial_sums = dot_first(token_weights, resid2, HIGHEST)
    counts = jnp.sum(select * mask_flat[:, None], axis=0)
    positions = (dest_shard * capacity + dest_slot).reshape(records)
    routing = (
        positions[None, :] == jnp.arange(seq_count * capacity, dtype=jnp.int32)[:, None]
    ).astype(jnp.float32)
    send_sums = dot_plain(
        routing, partial_sums.reshape(records, NTOK * model_width), HIGHEST
    ).reshape(seq_count, capacity, NTOK * model_width)
    send_counts = dot_plain(routing, counts[:, None], HIGHEST).reshape(seq_count, capacity)
    got_sums, got_counts = (
        lax.all_to_all(
            send_sums.astype(jnp.bfloat16), "seq", split_axis=0, concat_axis=0, tiled=True
        ).astype(send_sums.dtype),
        lax.all_to_all(
            send_counts.astype(jnp.bfloat16), "seq", split_axis=0, concat_axis=0, tiled=True
        ).astype(send_counts.dtype),
    )
    divisor = jnp.maximum(jnp.sum(got_counts, axis=0), 1.0)
    pooled = (
        (jnp.sum(got_sums, axis=0) / divisor[:, None])
        .astype(jnp.bfloat16)
        .reshape(1, capacity, NTOK, model_width)
    )
    grad_pooled = out_grad.reshape(capacity, NTOK * model_width).astype(jnp.float32)
    grad_sums = (grad_pooled / divisor[:, None]).astype(jnp.bfloat16)
    grad_all = lax.all_gather(grad_sums, "seq", axis=0, tiled=True)
    grad_records = dot_first(routing.astype(jnp.bfloat16), grad_all).reshape(
        records * NTOK, model_width
    )
    grad_resid2 = dot_plain(token_weights, grad_records, HIGHEST)
    grad_maps_all = dot_second(resid2, grad_records, HIGHEST).reshape(count_tok, records, NTOK)
    grad_map_vals = jnp.sum(grad_maps_all * select[:, :, None], axis=1)
    grad_logits = grad_map_vals * mask_flat[:, None] * sigmas * (1.0 - sigmas)
    grad_maps_weight = dot_first(grad_logits, normed3_out, HIGHEST)
    grad_maps_bias = jnp.sum(grad_logits, axis=0)
    grad_normed3 = dot_plain(grad_logits, map_weight, HIGHEST)
    back_three, grad_learn_gain, grad_learn_bias = norm_backward(
        grad_normed3, normed3, inverse3, learn_scale
    )
    grad_resid2 = grad_resid2 + back_three
    learner_sums = lax.psum(
        (grad_learn_gain, grad_learn_bias, grad_maps_weight, grad_maps_bias), ("rows", "seq")
    )
    grad_branch2 = grad_resid2.astype(jnp.bfloat16)
    grad_fc2 = dot_first(activated_low, grad_branch2)
    grad_fc2_shift = jnp.sum(grad_branch2.astype(jnp.float32), axis=0)
    grad_activ = dot_second(grad_branch2, fc2_full).astype(jnp.bfloat16)
    grad_hidden = gelu_back(grad_activ.astype(jnp.float32))[0].astype(jnp.bfloat16)
    grad_fc1 = dot_first(mlp_in, grad_hidden)
    grad_fc1_shift = jnp.sum(grad_hidden.astype(jnp.float32), axis=0)
    grad_normed2 = dot_second(grad_hidden, fc1_full)
    back_two, grad_norm2_gain, grad_norm2_shift = norm_backward(
        grad_normed2, normed2, inverse2, norm2_gain.astype(jnp.float32)
    )
    grad_resid1 = grad_resid2 + back_two
    grad_branch1 = grad_resid1.astype(jnp.bfloat16)
    grad_out_full = dot_first(mixed_low, grad_branch1)
    grad_out_shift = jnp.sum(grad_branch1.astype(jnp.float32), axis=0)
    grad_mixed = dot_second(grad_branch1, out_full).astype(jnp.bfloat16)
    grad_q, grad_k, grad_v = lax.map(
        attend_back,
        (
            q_blocks,
            k_blocks,
            v_blocks,
            own_blocks,
            seg_blocks,
            log_total,
            grad_mixed.reshape(block_count, group_size, per_row, head_count, HEAD_DIM),
        ),
    )
    grad_keys_own, grad_values_own = (
        lax.psum_scatter(
            grad_k.reshape(rows_here, row_len, model_width).astype(jnp.bfloat16),
            "seq",
            scatter_dimension=1,
            tiled=True,
        ).astype(jnp.float32),
        lax.psum_scatter(
            grad_v.reshape(rows_here, row_len, model_width).astype(jnp.bfloat16),
            "seq",
            scatter_dimension=1,
            tiled=True,
        ).astype(jnp.float32),
    )
    grad_q_low = grad_q.reshape(count_tok, model_width).astype(jnp.bfloat16)
    grad_v_low = grad_values_own.reshape(count_tok, model_width).astype(jnp.bfloat16)
    grad_qkv = jnp.concatenate(
        [
            grad_q_low,
            grad_keys_own.reshape(count_tok, model_width).astype(jnp.bfloat16),
            grad_v_low,
        ],
        axis=1,
    )
    grad_qkv_full = dot_first(attn_in, grad_qkv)
    grad_qv_full = jnp.stack(
        [
            jnp.sum(grad_q_low.astype(jnp.float32), axis=0),
            jnp.sum(grad_v_low.astype(jnp.float32), axis=0),
        ]
    )
    grad_normed1 = dot_second(grad_qkv, qkv_full)
    back_one, grad_norm1_gain, grad_norm1_shift = norm_backward(
        grad_normed1, normed1, inverse1, norm1_gain.astype(jnp.float32)
    )
    grad_held = (grad_resid1 + back_one).reshape(rows_here, per_row, model_width)
    block_shards = (
        lax.psum_scatter(grad_norm1_gain, ("rows", "seq"), scatter_dimension=0, tiled=True),
        lax.psum_scatter(grad_norm1_shift, ("rows", "seq"), scatter_dimension=0, tiled=True),
        lax.psum_scatter(grad_qkv_full, ("rows", "seq"), scatter_dimension=0, tiled=True),
        lax.psum_scatter(grad_qv_full, ("rows", "seq"), scatter_dimension=1, tiled=True),
        lax.psum_scatter(grad_out_full, ("rows", "seq"), scatter_dimension=0, tiled=True),
        lax.psum_scatter(grad_out_shift, ("rows", "seq"), scatter_dimension=0, tiled=True),
        lax.psum_scatter(grad_norm2_gain, ("rows", "seq"), scatter_dimension=0, tiled=True),
        lax.psum_scatter(grad_norm2_shift, ("rows", "seq"), scatter_dimension=0, tiled=True),
        lax.psum_scatter(grad_fc1, ("rows", "seq"), scatter_dimension=0, tiled=True),
        lax.psum_scatter(grad_fc1_shift, ("rows", "seq"), scatter_dimension=0, tiled=True),
        lax.psum_scatter(grad_fc2, ("rows", "seq"), scatter_dimension=0, tiled=True),
        lax.psum_scatter(grad_fc2_shift, ("rows", "seq"), scatter_dimension=0, tiled=True),
    )
    return (
        pooled,
        grad_held,
        block_shards[0],
        block_shards[1],
        block_shards[2],
        block_shards[3],
        block_shards[4],
        block_shards[5],
        block_shards[6],
        block_shards[7],
        block_shards[8],
        block_shards[9],
        block_shards[10],
        block_shards[11],
        learner_sums[0],
        learner_sums[1],
        learner_sums[2],
        learner_sums[3],
    )


def solution(mesh):
    in_specs = (
        P("rows", "seq", None),
        P("rows", None),
        P("rows", "seq"),
        P("rows", None),
        P("rows", None),
        P(("rows", "seq")),
        P(("rows", "seq")),
        P(("rows", "seq"), None),
        P(None, ("rows", "seq")),
        P(("rows", "seq"), None),
        P(("rows", "seq")),
        P(("rows", "seq")),
        P(("rows", "seq")),
        P(("rows", "seq"), None),
        P(("rows", "seq")),
        P(("rows", "seq"), None),
        P(("rows", "seq")),
        P(),
        P(),
        P(),
        P(),
        P("rows", "seq", None, None),
    )
    out_specs = (
        P("rows", "seq", None, None),
        P("rows", "seq", None),
        P(("rows", "seq")),
        P(("rows", "seq")),
        P(("rows", "seq"), None),
        P(None, ("rows", "seq")),
        P(("rows", "seq"), None),
        P(("rows", "seq")),
        P(("rows", "seq")),
        P(("rows", "seq")),
        P(("rows", "seq"), None),
        P(("rows", "seq")),
        P(("rows", "seq"), None),
        P(("rows", "seq")),
        P(),
        P(),
        P(),
        P(),
    )
    return jax.shard_map(shards, mesh=mesh, in_specs=in_specs, out_specs=out_specs, check_vma=False)
```

profile of v0, /device:TPU:0, one launch (start us, length us, event | category | flops | bytes accessed | tf_op | source)
XLA Modules:
  0.0 1577.4 jit_solution(7356794524099298934)
XLA Ops:
  13.1 42.4 %all-reduce.14 = (bf16[1024]{0:T(1024)(128)(2,1)S(1)}, bf16[1024]{0:T(1024)(128)(2,1)S(1)}, bf16[1024]{0:T(1024)(128)(2,1)S(1)}, bf16[1024]{0:T(1024)(128)(2,1)S...) all-reduce(bf16[1024]{0:T(1024)(128)(2,1)S(1)} %dynamic-update-slic, ...), channel_id=1, replica_groups=mesh['rows'=16,'seq'=2] {'rows','seq'}, use_global_device_ids=true, to_apply=%add.2 | all-reduce | flops 6144 | bytes 24576
  59.8 40.7 %all-gather = bf16[32,32,2]{1,2,0:T(2,128)(2,1)S(1)} all-gather(bf16[1,32,2]{1,2,0:T(2,128)(2,1)S(1)} %bitcast.276), channel_id=1, replica_groups=mesh['rows'=16,'seq'=2] {'rows','seq'}, dimensions={0}, use_global_device_ids=true | all-gather | bytes 4224 | tf_op jit(solution)/shard_map/all_gather | solution.py:152
  102.7 9.4 fusion.151
  129.7 36.8 %all-gather.1 = bf16[32,1,128]{2,1,0:T(2,128)(2,1)S(1)} all-gather(bf16[1,1,128]{2,1,0:T(2,128)(2,1)S(1)} %bitcast.277), channel_id=1, replica_groups=mesh['rows'=16,'seq'=2] {'rows','seq'}, dimensions={0}, use_global_device_ids=true | all-gather | bytes 8448 | tf_op jit(solution)/shard_map/all_gather | solution.py:158
  181.2 4.8 copy.99
  186.1 6.3 copy.96
  192.4 6.2 copy.98
  200.2 33.5 %while.26 = (s32[]{:T(128)}, bf16[2,2,256,16,64]{2,4,3,1,0:T(8,128)(2,1)}, f32[2,2,16,256]{3,2,1,0:T(8,128)S(1)}, bf16[2,2,512,16,64]{2,4,3,1,0:T(8,128)(2,1)}, ...) while((s32[]{:T(128)}, ...), condition=%wide.region_5.6_spmd, body=%wide.region_2.5_spmd.sunk | while | flops 1124327424 | bytes 59002992 | solution.py:198
  200.4 4.7 fusion.193
  209.6 7.3 bitcast_dynamic-update-slice_fusion.10
  217.2 4.7 fusion.193
  226.4 7.3 bitcast_dynamic-update-slice_fusion.10
  233.8 5.9 copy.100
  244.5 5.7 fusion.149
  252.7 29.9 %all-gather.18.cloned.1.call-done = bf16[1024,4096]{1,0:T(8,128)(2,1)} async-done(((bf16[32,4096]{1,0:T(8,128)(2,1)}), bf16[1024,4096]{1,0:T(8,128)(2,1)}) %all-gather.18.cloned.1.call-update) | async-done | bytes 8388624 | tf_op jit(solution)/shard_map/all_gather | solution.py:157
  282.6 51.3 %multiply_convert_fusion.1 = (bf16[1024,4096]{1,0:T(8,128)(2,1)}, f32[1024,4096]{1,0:T(8,128)}, f32[1024,4096]{1,0:T(8,128)}) fusion(f32[4096]{0:T(1024)S(1)} %bitcast.272, bf16[1024,4096]{1,0:T(8,128)(2,1)} %all-gather.18.cloned.1.call-done, f32[1024,1024]{1,0:T(8,128)} %copy-done.14, f32[1024]{0:T(1024)S(1)} %copy-done.58, f32[1024]{0:T(1024)S(1)} %copy-done.51, ...), kind=kOutput, calls=%fused_computation.75 | convolution fusion | flops 8872001536 | bytes 54558720 | tf_op jit(solution)/shard_map/dot_general | solution.py:17
  333.9 27.1 %all-gather.20.cloned.1.call-done = bf16[4096,1024]{1,0:T(8,128)(2,1)} async-done(((bf16[128,1024]{1,0:T(8,128)(2,1)}), bf16[4096,1024]{1,0:T(8,128)(2,1)}) %all-gather.20.cloned.1.call-update) | async-done | bytes 8388624 | tf_op jit(solution)/shard_map/all_gather | solution.py:159
  361.0 14.8 fusion.150
  390.1 10.1 multiply_add_fusion.1
  400.2 24.8 %convert_reduce_fusion = (f32[4096]{0:T(1024)}, bf16[1024,4096]{1,0:T(8,128)(2,1)}) fusion(f32[1024,4096]{1,0:T(8,128)} %get-tuple-element.292, bf16[4096,1024]{1,0:T(8,128)(2,1)} %all-gather.20.cloned.1.call-done, f32[1024,1024]{1,0:T(8,128)} %multiply_add_fusion.1, f32[1024,4096]{1,0:T(8,128)} %get-tuple-element.307, f32[4096]{0:T(1024)S(1)} %bitcast.273), kind=kOutput, calls=%fused_computation.74 | convolution fusion | flops 8670670848 | bytes 54558720 | tf_op jit(solution)/shard_map/dot_general | solution.py:31
  425.0 16.4 %multiply_reduce_fusion.2 = (f32[1024]{0:T(1024)}, f32[1024]{0:T(1024)S(1)}, f32[1024]{0:T(1024)S(1)}, f32[1024]{0:T(1024)}, f32[1024,1024]{1,0:T(8,128)S(1)}) fusion(f32[1024,1024]{1,0:T(8,128)} %copy-done.14, f32[1024]{0:T(1024)S(1)} %add_rsqrt_fusion.1, f32[1024]{0:T(1024)S(1)} %broadcast_multiply_fusion.9, f32[1024]{0:T(1024)S(1)} %copy-done.51, ...), kind=kOutput, calls=%fused_computation.119 | convolution fusion | flops 8599367680 | bytes 25194496 | tf_op jit(solution)/shard_map/dot_general | solution.py:31
  452.3 5.9 copy.106
  459.8 122.3 %while.27 = (s32[]{:T(128)}, bf16[2,2,256,16,64]{2,4,3,1,0:T(8,128)(2,1)}, bf16[2,2,512,16,64]{2,4,3,1,0:T(8,128)(2,1)}, bf16[2,2,512,16,64]{2,4,3,1,0:T(8,128)(...) while((s32[]{:T(128)}, ...), condition=%wide.region_20.21_spmd, body=%wide.region_18.20_spmd.sunk | while | flops 2749095936 | bytes 248765840 | solution.py:286
  460.3 10.2 fusion.203
  470.7 14.0 multiply_reduce_fusion.11
  484.7 16.0 %multiply_convert_fusion.3 = bf16[2,16,256,512]{3,2,1,0:T(8,128)(2,1)} fusion(f32[2,16,256,512]{3,2,1,0:T(8,128)} %get-tuple-element.439, f32[2,16,256,512]{3,2,1,0:T(8,128)} %fusion.203, f32[2,16,256]{2,1,0:T(8,128)S(1)} %get-tuple-element.440, f32[2,16,256]{2,1,0:T(8,128)S(1)} %dynamic-slice_bitcast_fusion.10, ...), kind=kLoop, calls=%fused_computation.22.clone.1 | loop fusion | flops 25165824 | bytes 42270720 | tf_op jit(solution)/shard_map/while/body/eval_jaxpr/convert_element_type | solution.py:93
  500.7 8.0 bitcast_dynamic-update-slice_fusion.12
  508.7 6.7 bitcast_dynamic-update-slice_fusion.13
  515.5 5.8 bitcast_dynamic-update-slice_fusion.14
  521.2 10.2 fusion.203
  531.6 14.0 multiply_reduce_fusion.11
  545.7 16.0 %multiply_convert_fusion.3 = bf16[2,16,256,512]{3,2,1,0:T(8,128)(2,1)} fusion(f32[2,16,256,512]{3,2,1,0:T(8,128)} %get-tuple-element.439, f32[2,16,256,512]{3,2,1,0:T(8,128)} %fusion.203, f32[2,16,256]{2,1,0:T(8,128)S(1)} %get-tuple-element.440, f32[2,16,256]{2,1,0:T(8,128)S(1)} %dynamic-slice_bitcast_fusion.10, ...), kind=kLoop, calls=%fused_computation.22.clone.1 | loop fusion | flops 25165824 | bytes 42270720 | tf_op jit(solution)/shard_map/while/body/eval_jaxpr/convert_element_type | solution.py:93
  561.7 8.0 bitcast_dynamic-update-slice_fusion.12
  569.7 6.7 bitcast_dynamic-update-slice_fusion.13
  576.4 5.7 bitcast_dynamic-update-slice_fusion.14
  592.4 5.5 fusion.84
  619.4 13.9 fusion.82
  633.4 7.2 fusion.137
  640.8 14.7 fusion.86
  656.2 16.8 %fusion.144 = f32[1024,4096]{1,0:T(8,128)} fusion(bf16[1024,4096]{1,0:T(8,128)(2,1)} %get-tuple-element.314, f32[1024,1024]{1,0:T(8,128)} %copy-done.14, f32[1024]{0:T(1024)S(1)} %copy-done.59, f32[1024]{0:T(1024)S(1)} %copy-done.52, f32[1024]{0:T(1024)S(1)} %copy-done.54, f32[1024]{0:T(1024)S(1)} %copy-done.45), kind=kOutput, calls=%fused_computation.228 | convolution fusion | flops 8595177472 | bytes 29376512 | tf_op jit(solution)/shard_map/dot_general | solution.py:21
  673.3 16.5 %fusion.140 = f32[4096,1024]{1,0:T(8,128)} fusion(bf16[1024,4096]{1,0:T(8,128)(2,1)} %get-tuple-element.291, f32[1024,1024]{1,0:T(8,128)} %multiply_add_fusion.1), kind=kOutput, calls=%fused_computation.224 | convolution fusion | flops 8590983168 | bytes 29360128 | tf_op jit(solution)/shard_map/dot_general | solution.py:21
  691.2 8.3 fusion.102
  712.3 44.3 %reduce-scatter.22.cloned.1.call-done = f32[32,2]{1,0:T(8,128)} async-done(((f32[1024,2]{1,0:T(8,128)}), f32[32,2]{1,0:T(8,128)}) %reduce-scatter.22.cloned.1.call-update) | async-done | bytes 272
  757.9 130.9 %all-reduce.17.cloned.1.call-done = (f32[1024]{0:T(1024)}, f32[1024]{0:T(1024)}, f32[1024]{0:T(1024)}, f32[1024]{0:T(1024)}, f32[1024]{0:T(1024)}, /*index=5*/f3...) async-done(((f32[1024]{0:T(1024)}, f32[1024]{0:T(1024)}, f32[1024]{0:T(1024)}, f32[1024]{0:T(1024)}, ...) | async-done | bytes 81968
  897.6 138.4 %reduce-scatter.16.cloned.1.call-done = f32[32,1024]{1,0:T(8,128)} async-done(((f32[1024,1024]{1,0:T(8,128)}), f32[32,1024]{1,0:T(8,128)}) %reduce-scatter.16.cloned.1.call-update) | async-done | bytes 131088 | tf_op jit(solution)/shard_map/reduce_scatter | solution.py:339
  1036.0 157.2 %reduce-scatter.14.cloned.1.call-done = f32[32,3072]{1,0:T(8,128)} async-done(((f32[1024,3072]{1,0:T(8,128)}), f32[32,3072]{1,0:T(8,128)}) %reduce-scatter.14.cloned.1.call-update) | async-done | bytes 393232 | tf_op jit(solution)/shard_map/reduce_scatter | solution.py:337
  1193.2 184.7 %reduce-scatter.18.cloned.1.call-done = f32[32,4096]{1,0:T(8,128)} async-done(((f32[1024,4096]{1,0:T(8,128)}), f32[32,4096]{1,0:T(8,128)}) %reduce-scatter.18.cloned.1.call-update) | async-done | bytes 524304 | tf_op jit(solution)/shard_map/reduce_scatter | solution.py:343
  1377.9 187.4 %reduce-scatter.20.cloned.1.call-done = f32[128,1024]{1,0:T(8,128)} async-done(((f32[4096,1024]{1,0:T(8,128)}), f32[128,1024]{1,0:T(8,128)}) %reduce-scatter.20.cloned.1.call-update) | async-done | bytes 524304 | tf_op jit(solution)/shard_map/reduce_scatter | solution.py:345
  (347 shorter events, 151.6 us)
Async XLA Ops:
  7.2 375.7 %copy-start = (bf16[8,1024]{1,0:T(8,128)(2,1)S(1)}, bf16[8,1024]{1,0:T(8,128)(2,1)}, u32[]{:S(2)}) copy-start(bf16[8,1024]{1,0:T(8,128)(2,1)} %param.45) | copy-start | bytes 49156
  7.2 93.4 %copy-start.6 = (bf16[4,256,1024]{2,1,0:T(8,128)(2,1)S(1)}, bf16[4,256,1024]{2,1,0:T(8,128)(2,1)}, u32[]{:S(2)}) copy-start(bf16[4,256,1024]{2,1,0:T(8,128)(2,1)} %param.26) | copy-start | bytes 6291460
  7.2 52.6 %copy-start.72 = (bf16[2,32]{1,0:T(2,128)(2,1)S(1)}, bf16[2,32]{1,0:T(2,128)(2,1)}, u32[]{:S(2)}) copy-start(bf16[2,32]{1,0:T(2,128)(2,1)} %param.34) | copy-start | bytes 388
  7.2 95.5 %all-gather.10.cloned.1.call-start = ((), (), s32[]{:S(2)}) async-start(), calls=%async_computation.9 | async-start | bytes 6488064 | tf_op jit(solution)/shard_map/all_gather | solution.py:151
  8.0 178.1 %all-gather.12.cloned.1.call-start = ((), (), s32[]{:S(2)}) async-start(), calls=%async_computation.10 | async-start | bytes 6291456 | tf_op jit(solution)/shard_map/all_gather | solution.py:189
  55.5 47.2 %copy-start.38 = (f32[1024]{0:T(1024)}, f32[1024]{0:T(1024)S(1)}, u32[]{:S(2)}) copy-start(f32[1024]{0:T(1024)S(1)} %convert_element_type.201) | copy-start | bytes 12292
  59.8 52.4 %copy-start.40 = (f32[1,2,4,128]{3,1,2,0:T(2,128)}, f32[1,2,4,128]{3,1,2,0:T(2,128)S(1)}, u32[]{:S(2)}) copy-start(f32[1,2,4,128]{3,1,2,0:T(2,128)S(1)} %copy.122) | copy-start | bytes 12292
  59.8 52.4 %copy-start.42 = (f32[1,2,4,128]{3,1,2,0:T(2,128)}, f32[1,2,4,128]{3,1,2,0:T(2,128)S(1)}, u32[]{:S(2)}) copy-start(f32[1,2,4,128]{3,1,2,0:T(2,128)S(1)} %copy.121) | copy-start | bytes 12292
  117.4 12.3 copy-start.73
  117.4 51.0 %copy-start.25 = (bf16[1,20,8,1024]{3,2,1,0:T(8,128)(2,1)S(1)}, bf16[1,20,8,1024]{3,2,1,0:T(8,128)(2,1)}, u32[]{:S(2)}) copy-start(bf16[1,20,8,1024]{3,2,1,0:T(8,128)(2,1)} %param.47) | copy-start | bytes 983044
  117.5 75.0 %all-gather.14.cloned.1.call-start = ((), (), s32[]{:S(2)}) async-start(), calls=%async_computation.11 | async-start | bytes 6291456 | tf_op jit(solution)/shard_map/all_gather | solution.py:186
  121.6 122.8 %all-gather.16.cloned.1.call-start = ((), (), s32[]{:S(2)}) async-start(), calls=%async_computation.12 | async-start | bytes 2162688 | tf_op jit(solution)/shard_map/all_gather | solution.py:153
  122.2 160.4 %all-gather.18.cloned.1.call-start = ((), (), s32[]{:S(2)}) async-start(), calls=%async_computation.13 | async-start | bytes 8650752 | tf_op jit(solution)/shard_map/all_gather | solution.py:157
  122.9 49.9 %copy-start.56 = (s32[40]{0:T(128)}, s32[40]{0:T(128)S(1)}, u32[]{:S(2)}) copy-start(s32[40]{0:T(128)S(1)} %eq.93) | copy-start | bytes 484
  124.0 45.1 %all-to-all-start.1 = ((bf16[2,1,20]{2,1,0:T(2,128)(2,1)}), bf16[2,1,20]{2,1,0:T(2,128)(2,1)S(1)}, u32[]{:S(2)}, u32[]{:S(2)}) async-start(bf16[2,1,20]{2,1,0:T(2,128)(2,1)} %copy.102), calls=%async_computation.1 | async-start | bytes 2048 | tf_op jit(solution)/shard_map/all_to_all | solution.py:240
  127.2 233.9 %all-gather.20.cloned.1.call-start = ((), (), s32[]{:S(2)}) async-start(), calls=%async_computation.14 | async-start | bytes 8650752 | tf_op jit(solution)/shard_map/all_gather | solution.py:159
  127.7 470.2 %reduce-scatter.12.cloned.1.call-start = ((), (), s32[]{:S(2)}) async-start(), calls=%async_computation.16 | async-start | bytes 6291456 | tf_op jit(solution)/shard_map/reduce_scatter | solution.py:305
  233.8 10.6 copy-start.3
  233.8 10.6 copy-start.61
  250.2 32.4 %copy-start.51 = (f32[1024]{0:T(1024)S(1)}, f32[1024]{0:T(1024)}, u32[]{:S(2)}) copy-start(f32[1024]{0:T(1024)} %convert_element_type.210) | copy-start | bytes 12292
  250.2 32.4 %copy-start.55 = (f32[32,1,128]{2,1,0:T(1,128)S(1)}, f32[32,1,128]{2,1,0:T(1,128)}, u32[]{:S(2)}) copy-start(f32[32,1,128]{2,1,0:T(1,128)} %convert_element_type.253) | copy-start | bytes 49156
  250.2 32.4 %copy-start.58 = (f32[1024]{0:T(1024)S(1)}, f32[1024]{0:T(1024)}, u32[]{:S(2)}) copy-start(f32[1024]{0:T(1024)} %convert_element_type.211) | copy-start | bytes 12292
  250.2 191.2 %copy-start.44 = (f32[1024]{0:T(1024)}, f32[1024]{0:T(1024)S(1)}, u32[]{:S(2)}) copy-start(f32[1024]{0:T(1024)S(1)} %broadcast_multiply_fusion.9) | copy-start | bytes 12292
  252.7 188.7 %copy-start.53 = (f32[1024]{0:T(1024)}, f32[1024]{0:T(1024)S(1)}, u32[]{:S(2)}) copy-start(f32[1024]{0:T(1024)S(1)} %add_rsqrt_fusion.1) | copy-start | bytes 12292
  282.6 78.4 %copy-start.60 = (f32[1024]{0:T(1024)S(1)}, f32[1024]{0:T(1024)}, u32[]{:S(2)}) copy-start(f32[1024]{0:T(1024)} %convert_element_type.215) | copy-start | bytes 12292
  375.9 14.2 copy-start.4
  375.9 14.1 copy-start.32
  376.5 13.5 copy-start.36
  425.0 16.4 %copy-start.13 = (f32[1024,1024]{1,0:T(8,128)S(1)}, f32[1024,1024]{1,0:T(8,128)}, u32[]{:S(2)}) copy-start(f32[1024,1024]{1,0:T(8,128)} %multiply_add_fusion.1) | copy-start | bytes 12582916
  425.0 16.4 %copy-start.15 = (f32[1024,1024]{1,0:T(8,128)S(1)}, f32[1024,1024]{1,0:T(8,128)}, u32[]{:S(2)}) copy-start(f32[1024,1024]{1,0:T(8,128)} %copy-done.14) | copy-start | bytes 12582916
  484.7 16.0 %copy-start.2 = (bf16[2,2,512,16,64]{2,4,3,1,0:T(8,128)(2,1)S(1)}, bf16[2,2,512,16,64]{2,4,3,1,0:T(8,128)(2,1)}, u32[]{:S(2)}) copy-start(bf16[2,2,512,16,64]{2,4,3,1,0:T(8,128)(2,1)} %get-tuple-element.496) | copy-start | bytes 12582916 | tf_op jit(solution)/shard_map/while
  484.7 30.7 %slice-start = ((s8[16777216]{0:T(1024)(128)(4,1)}), s8[4194304]{0:T(1024)(128)(4,1)S(1)}, s32[]{:S(2)}) async-start(s8[16777216]{0:T(1024)(128)(4,1)} %bitcast.243), calls=%async_computation.23 | async-start | bytes 8388608 | tf_op jit(solution)/shard_map/while
  484.7 30.7 %slice-start.1 = ((s8[16777216]{0:T(1024)(128)(4,1)}), s8[4194304]{0:T(1024)(128)(4,1)S(1)}, s32[]{:S(2)}) async-start(s8[16777216]{0:T(1024)(128)(4,1)} %bitcast.243), calls=%async_computation.24 | async-start | bytes 8388608 | tf_op jit(solution)/shard_map/while
  484.7 30.7 %slice-start.2 = ((s8[16777216]{0:T(1024)(128)(4,1)}), s8[4194304]{0:T(1024)(128)(4,1)S(1)}, s32[]{:S(2)}) async-start(s8[16777216]{0:T(1024)(128)(4,1)} %bitcast.243), calls=%async_computation.25 | async-start | bytes 8388608 | tf_op jit(solution)/shard_map/while
  500.7 14.7 slice-start.3
  545.7 16.0 %copy-start.2 = (bf16[2,2,512,16,64]{2,4,3,1,0:T(8,128)(2,1)S(1)}, bf16[2,2,512,16,64]{2,4,3,1,0:T(8,128)(2,1)}, u32[]{:S(2)}) copy-start(bf16[2,2,512,16,64]{2,4,3,1,0:T(8,128)(2,1)} %get-tuple-element.496) | copy-start | bytes 12582916 | tf_op jit(solution)/shard_map/while
  545.7 30.7 %slice-start = ((s8[16777216]{0:T(1024)(128)(4,1)}), s8[4194304]{0:T(1024)(128)(4,1)S(1)}, s32[]{:S(2)}) async-start(s8[16777216]{0:T(1024)(128)(4,1)} %bitcast.243), calls=%async_computation.23 | async-start | bytes 8388608 | tf_op jit(solution)/shard_map/while
  545.7 30.7 %slice-start.1 = ((s8[16777216]{0:T(1024)(128)(4,1)}), s8[4194304]{0:T(1024)(128)(4,1)S(1)}, s32[]{:S(2)}) async-start(s8[16777216]{0:T(1024)(128)(4,1)} %bitcast.243), calls=%async_computation.24 | async-start | bytes 8388608 | tf_op jit(solution)/shard_map/while
  545.7 30.7 %slice-start.2 = ((s8[16777216]{0:T(1024)(128)(4,1)}), s8[4194304]{0:T(1024)(128)(4,1)S(1)}, s32[]{:S(2)}) async-start(s8[16777216]{0:T(1024)(128)(4,1)} %bitcast.243), calls=%async_computation.25 | async-start | bytes 8388608 | tf_op jit(solution)/shard_map/while
  561.7 14.7 slice-start.3
  582.2 26.1 %reduce-scatter.10.cloned.1.call-start = ((), (), s32[]{:S(2)}) async-start(), calls=%async_computation.15 | async-start | bytes 6291456 | tf_op jit(solution)/shard_map/reduce_scatter | solution.py:299
  582.9 173.7 %reduce-scatter.22.cloned.1.call-start = ((), (), s32[]{:S(2)}) async-start(), calls=%async_computation.21 | async-start | bytes 540672
  619.4 269.5 %all-reduce.17.cloned.1.call-start = ((), (), s32[]{:S(2)}) async-start(), calls=%async_computation.22 | async-start | bytes 164864
  633.4 402.6 %reduce-scatter.16.cloned.1.call-start = ((), (), s32[]{:S(2)}) async-start(), calls=%async_computation.18 | async-start | bytes 4325376 | tf_op jit(solution)/shard_map/reduce_scatter | solution.py:339
  640.6 552.6 %reduce-scatter.14.cloned.1.call-start = ((), (), s32[]{:S(2)}) async-start(), calls=%async_computation.17 | async-start | bytes 12976128 | tf_op jit(solution)/shard_map/reduce_scatter | solution.py:337
  655.5 722.4 %reduce-scatter.18.cloned.1.call-start = ((), (), s32[]{:S(2)}) async-start(), calls=%async_computation.19 | async-start | bytes 17301504 | tf_op jit(solution)/shard_map/reduce_scatter | solution.py:343
  673.0 892.3 %reduce-scatter.20.cloned.1.call-start = ((), (), s32[]{:S(2)}) async-start(), calls=%async_computation.20 | async-start | bytes 17301504 | tf_op jit(solution)/shard_map/reduce_scatter | solution.py:345
  707.9 862.5 %copy-start.1 = (bf16[8,1024]{1,0:T(8,128)(2,1)S(1)}, bf16[8,1024]{1,0:T(8,128)(2,1)}, u32[]{:S(2)}) copy-start(bf16[8,1024]{1,0:T(8,128)(2,1)} %param.45) | copy-start | bytes 49156
  (55 other events, 319.5 us)
Sparse Core Ops, SparseCore 0:
  10.9 71.9 all-gather.9
  117.6 9.7 all-gather.11
  128.9 14.8 all-gather.13
  146.5 57.3 all-gather.15
  206.6 75.9 all-gather.17
  285.3 75.6 all-gather.19
  582.3 10.4 reduce-scatter.11
  595.1 13.1 reduce-scatter.9
  619.5 137.0 reduce-scatter.21
  764.0 124.7 all-reduce.16
  891.7 144.2 reduce-scatter.15
  1042.4 150.7 reduce-scatter.13
  1196.1 181.8 reduce-scatter.17
  1380.7 184.6 reduce-scatter.19
where the time goes:
time: 1590 us; the launch traced here: 1580 us
  waiting for transfers between devices  908 us (57%)
  matrix products  345 us (22%)
  blocking collectives  127 us (8%)
  local copies, waits for them, and re-layouts  109 us (7%)
  other arithmetic  68.4 us (4%)
    reduce_scatter x1, waiting for transfers between devices, shards(): lax.psum_scatter(grad_fc2, ('rows', 'seq'), scatter_dimension=0, tiled=True)  187 us
    reduce_scatter x1, waiting for transfers between devices, shards(): lax.psum_scatter(grad_fc1, ('rows', 'seq'), scatter_dimension=0, tiled=True)  185 us
    unnamed x16, waiting for transfers between devices  178 us
    reduce_scatter x1, waiting for transfers between devices, shards(): lax.psum_scatter(grad_qkv_full, ('rows', 'seq'), scatter_dimension=0, til...  157 us
    reduce_scatter x1, waiting for transfers between devices, shards(): lax.psum_scatter(grad_out_full, ('rows', 'seq'), scatter_dimension=0, til...  138 us
    dot_general x8, matrix products, dot_plain(): jnp.dot(former, latter, precision=precision, preferred_element_type=jnp.f...  96.1 us
    dot_general x7, matrix products, dot_first(): lax.dot_general(former, latter, (((0,), (0,)), ((), ())), precision=preci...  70.5 us
    dot_general x6, matrix products, dot_second(): lax.dot_general(former, latter, (((1,), (1,)), ((), ())), precision=preci...  65.4 us
  transfers between devices with their start and end apart: 15, of which 9 were waited for; matrix products, arithmetic and copies ran while one was open for 17% of the time, Pallas kernels for 0%

commit v1 on v0

v1 whole, which is shorter than its diff:
```python
import jax
import jax.numpy as jnp
from jax import lax
from jax.experimental import pallas as pl
from jax.experimental.pallas import tpu as pltpu
from jax.sharding import PartitionSpec as P

HEAD_DIM = 64
NTOK = 8
IMG_ROW = 10

EPSILON = 1e-06
NEGATIVE = -1e30
HIGH = lax.Precision.HIGH
BF = jnp.bfloat16
F32 = jnp.float32
SWAP = [(0, 1), (1, 0)]


def dot_plain(a, b, precision=None):
    return jnp.dot(a, b, precision=precision, preferred_element_type=F32)


def dot_first(a, b, precision=None):
    return lax.dot_general(
        a, b, (((0,), (0,)), ((), ())), precision=precision, preferred_element_type=F32
    )


def dot_second(a, b, precision=None):
    return lax.dot_general(
        a, b, (((1,), (1,)), ((), ())), precision=precision, preferred_element_type=F32
    )


def norm_stats(values):
    centred = values - jnp.mean(values, axis=-1, keepdims=True)
    inverse = lax.rsqrt(jnp.mean(centred * centred, axis=-1, keepdims=True) + EPSILON)
    return centred * inverse, inverse


def norm_backward(grad_out, normed, inverse, scale_vec):
    grad_unit = grad_out * scale_vec
    grad_in = inverse * (
        grad_unit
        - jnp.mean(grad_unit, axis=-1, keepdims=True)
        - normed * jnp.mean(grad_unit * normed, axis=-1, keepdims=True)
    )
    return (grad_in, jnp.sum(grad_out * normed, axis=0), jnp.sum(grad_out, axis=0))


def factors(count):
    if count == 16:
        return (4, 2, 2)
    if count == 128:
        return (4, 8, 4)
    return (count, 1, 1)


def rotation(dims, place, step):
    pairs = []
    for a in range(dims[0]):
        for b in range(dims[1]):
            for c in range(dims[2]):
                digits = [a, b, c]
                source = (a * dims[1] + b) * dims[2] + c
                digits[place] = (digits[place] + step) % dims[place]
                pairs.append((source, (digits[0] * dims[1] + digits[1]) * dims[2] + digits[2]))
    return pairs


def crossing(dims, place, flip):
    stride = 1
    for size in dims[place + 1 :]:
        stride *= size
    count = dims[0] * dims[1] * dims[2]
    pairs = []
    for source in range(count):
        digit = (source // stride) % dims[place]
        pairs.append((source, source + ((digit ^ flip) - digit) * stride))
    return pairs


class Wires:
    def __init__(self):
        self.count = lax.axis_size("rows")
        self.dims = factors(self.count)
        row = lax.axis_index("rows")
        self.digits = (
            row // (self.dims[1] * self.dims[2]),
            (row // self.dims[2]) % self.dims[1],
            row % self.dims[2],
        )
        self.seq = lax.axis_index("seq")

    def turn(self, value, place, step):
        return lax.ppermute(value, "rows", rotation(self.dims, place, step))

    def swap(self, value):
        return lax.ppermute(value, "seq", SWAP)


def gate(values, hold):
    return lax.optimization_barrier((values, hold))[0]


def place_kernel(n_parts, dims, chunk, half):
    k0, k1, k2 = dims

    def body(where, *refs):
        parts, out = refs[:n_parts], refs[n_parts]
        buf, sem_in, sem_out = refs[n_parts + 1 :]
        came = []
        at = 0
        for other in (0, 1):
            for colour in (0, 1):
                outer, inner = ((1, 2), (2, 1))[colour]
                for late in range(dims[outer]):
                    part = parts[at]
                    at += 1
                    for mid in range(dims[inner]):
                        for top in range(k0):
                            rel = [0, 0, 0]
                            rel[0], rel[inner], rel[outer] = top, mid, late
                            spot = [
                                lax.rem(where[i] - rel[i] + dims[i], dims[i]) for i in range(3)
                            ]
                            seat = lax.rem(where[3] + other, 2)
                            block = ((spot[0] * k1 + spot[1]) * k2 + spot[2]) * 2 + seat
                            start = pl.multiple_of(block * chunk, chunk)
                            span = (pl.ds(start, chunk), pl.ds(colour * half, half))
                            copy = pltpu.make_async_copy(
                                part.at[mid * k0 + top], buf.at[span], sem_in.at[len(came)]
                            )
                            copy.start()
                            came.append((copy, span))
        went = []
        for copy, span in came:
            copy.wait()
            back = pltpu.make_async_copy(buf.at[span], out.at[span], sem_out.at[len(went)])
            back.start()
            went.append(back)
        for back in went:
            back.wait()

    return body


class Gather:
    def __init__(self, wires, shard):
        self.wires, self.shard = wires, shard
        m, n = shard.shape
        self.plain = bool(m % 32 or n % 256)
        self.half = n // 2
        self.flight, self.held, self.sends = (), (), ()
        self.stage = 0

    def step(self, after=()):
        if self.plain:
            return
        wires, stage = self.wires, self.stage
        self.stage += 1
        if stage == 0:
            shard = gate(self.shard, after) if after else self.shard
            self.flight = [wires.turn(shard, 0, r) for r in range(1, wires.dims[0])]
            return
        pairs = ((1, 2), (2, 1))
        if stage == 1:
            tops = [self.shard] + list(self.flight)
            cuts = [
                jnp.stack([t[:, c * self.half : (c + 1) * self.half] for t in tops])
                for c in (0, 1)
            ]
        else:
            cuts = self.held
        if after:
            cuts = gate(cuts, after)
        if stage == 1:
            self.held = self.sends = cuts
            self.got = [
                [wires.turn(cuts[c], pairs[c][1], r) for r in range(1, wires.dims[pairs[c][1]])]
                for c in (0, 1)
            ]
            self.flight = self.got[0] + self.got[1]
        elif stage == 2:
            mids = [jnp.concatenate([cuts[c]] + self.got[c], axis=0) for c in (0, 1)]
            if after:
                mids = gate(mids, after)
            lists = [
                [wires.turn(mids[c], pairs[c][0], r) for r in range(1, wires.dims[pairs[c][0]])]
                for c in (0, 1)
            ]
            self.held, self.sends = (mids, lists), mids
            self.flight = lists[0] + lists[1]
        elif stage == 3:
            mids, lists = cuts
            own = [mids[0]] + lists[0] + [mids[1]] + lists[1]
            self.flight = [wires.swap(p) for p in own]
            self.held = own

    def result(self):
        wires, shard = self.wires, self.shard
        if self.plain:
            return lax.all_gather(shard, ("rows", "seq"), axis=0, tiled=True)
        m, n = shard.shape
        parts = list(self.held) + list(self.flight)
        where = jnp.stack([*wires.digits, wires.seq]).astype(jnp.int32)
        total = wires.count * 2
        return pl.pallas_call(
            place_kernel(len(parts), wires.dims, m, self.half),
            out_shape=jax.ShapeDtypeStruct((m * total, n), shard.dtype),
            grid_spec=pltpu.PrefetchScalarGridSpec(
                num_scalar_prefetch=1,
                grid=(1,),
                in_specs=[pl.BlockSpec(memory_space=pl.ANY)] * len(parts),
                out_specs=pl.BlockSpec(memory_space=pl.ANY),
                scratch_shapes=[
                    pltpu.VMEM((m * total, n), shard.dtype),
                    pltpu.SemaphoreType.DMA((2 * total,)),
                    pltpu.SemaphoreType.DMA((2 * total,)),
                ],
            ),
            name="place",
        )(where, *parts)


def pick(value, index, axis):
    return lax.dynamic_index_in_dim(value, index, axis, keepdims=False)


def total_of(terms):
    wide = [t.astype(F32) for t in terms]
    return sum(wide[1:], wide[0])


class Scatter:
    def __init__(self, wires, grad):
        self.wires, self.grad = wires, grad
        d, n = grad.shape
        self.m = d // (wires.count * 2)
        self.plain = bool(self.m % 32 or n % 256)
        self.half = n // 2
        self.stage = 0
        self.sends = ()
        self.flight = ()

    def fold(self, terms, place, axis):
        wires = self.wires
        size, spot = wires.dims[place], wires.digits[place]
        kept = [pick(t, spot, axis) for t in terms]
        away, got = [], []
        for step in range(1, size):
            index = lax.rem(spot + step, size)
            send = total_of([pick(t, index, axis) for t in terms]).astype(BF)
            away.append(send)
            got.append(wires.turn(send, place, step))
        return away, kept, got

    def step(self):
        if self.plain:
            return
        wires, stage = self.wires, self.stage
        self.stage += 1
        if stage == 0:
            d, n = self.grad.shape
            cut = self.grad.reshape(*wires.dims, 2, self.m, n)
            send = pick(cut, 1 - wires.seq, 3).astype(BF)
            got = wires.swap(send)
            self.sends, self.flight = [send], [got]
            base = [pick(cut, wires.seq, 3), got]
            half = self.half
            self.terms = [[t[..., c * half : (c + 1) * half] for t in base] for c in (0, 1)]
            return
        places = (((2, 2), (1, 1), (0, 0)), ((1, 1), (2, 1), (0, 0)))
        self.sends, self.flight, terms = [], [], []
        for c in (0, 1):
            away, kept, got = self.fold(self.terms[c], *places[c][stage - 1])
            self.sends += away
            self.flight += got
            terms.append(kept + got)
        self.terms = terms

    def result(self):
        if self.plain:
            both = ("rows", "seq")
            return lax.psum_scatter(self.grad.astype(F32), both, scatter_dimension=0, tiled=True)
        return jnp.concatenate([total_of(t) for t in self.terms], axis=1)


def sum_everywhere(wires, value):
    value = value + wires.swap(value)
    for place in (2, 1, 0):
        size = wires.dims[place]
        step = 1
        while step < size:
            value = value + lax.ppermute(value, "rows", crossing(wires.dims, place, step))
            step *= 2
    return value


def attend_kernel(seg_col, seg_row, q_ref, k_ref, v_ref, mixed_ref, log_ref, bias_ref):
    @pl.when(pl.program_id(1) == 0)
    def _():
        bias_ref[...] = jnp.where(seg_col[0] == seg_row[0], 0.0, NEGATIVE)

    scale = HEAD_DIM ** (-0.5)
    mixed = []
    for h in (0, 1):
        span = slice(h * HEAD_DIM, (h + 1) * HEAD_DIM)
        q = q_ref[:, span] * BF(scale)
        scores = dot_second(k_ref[:, span], q) + bias_ref[...]
        largest = jnp.max(scores, axis=0, keepdims=True)
        exponent = jnp.exp(scores - largest)
        summed = jnp.sum(exponent, axis=0, keepdims=True)
        probs = (exponent * (1.0 / summed)).astype(BF)
        mixed.append(dot_first(v_ref[:, span], probs))
        log_ref[0, 0, h : h + 1, :] = largest + jnp.log(summed)
    mixed_ref[...] = jnp.concatenate(mixed, axis=0).T.astype(BF)


def attend(joined, segments, first, pairs):
    rows, length = segments.shape
    lane = 2 * HEAD_DIM
    all_pairs = joined.shape[1] // (3 * lane)

    def block(start):
        return pl.BlockSpec((length, lane), lambda r, h: (r, start + h))

    return pl.pallas_call(
        attend_kernel,
        grid=(rows, pairs),
        in_specs=[
            pl.BlockSpec((1, length, 1), lambda r, h: (r, 0, 0)),
            pl.BlockSpec((1, 1, length), lambda r, h: (r, 0, 0)),
            block(first),
            block(all_pairs + first),
            block(2 * all_pairs + first),
        ],
        out_specs=[block(0), pl.BlockSpec((1, 1, 2, length), lambda r, h: (r, h, 0, 0))],
        out_shape=[
            jax.ShapeDtypeStruct((rows * length, pairs * lane), BF),
            jax.ShapeDtypeStruct((rows, pairs, 2, length), F32),
        ],
        scratch_shapes=[pltpu.VMEM((length, length), F32)],
        name="attend",
    )(segments[:, :, None], segments[:, None, :], joined, joined, joined)


def attend_back_kernel(
    seg_col, seg_row, q_ref, k_ref, v_ref, log_ref, do_ref, dq_ref, dk_ref, dv_ref, bias_ref
):
    @pl.when(pl.program_id(1) == 0)
    def _():
        bias_ref[...] = jnp.where(seg_col[0] == seg_row[0], 0.0, NEGATIVE)

    scale = HEAD_DIM ** (-0.5)
    grads = []
    for h in (0, 1):
        span = slice(h * HEAD_DIM, (h + 1) * HEAD_DIM)
        q = q_ref[:, span] * BF(scale)
        k = k_ref[:, span]
        do = do_ref[:, span]
        scores = dot_second(k, q) + bias_ref[...]
        probs = jnp.exp(scores - log_ref[0, 0, h : h + 1, :])
        grad_probs = dot_second(v_ref[:, span], do)
        inner = jnp.sum(probs * grad_probs, axis=0, keepdims=True)
        grad_scores = (probs * (grad_probs - inner)).astype(BF)
        dv_ref[:, span] = dot_plain(probs.astype(BF), do).astype(BF)
        dk_ref[:, span] = dot_plain(grad_scores, q).astype(BF)
        grads.append(dot_first(k, grad_scores) * scale)
    dq_ref[...] = jnp.concatenate(grads, axis=0).T.astype(BF)


def attend_back(joined, logs, grad_mixed, segments, first, pairs):
    rows, length = segments.shape
    lane = 2 * HEAD_DIM
    all_pairs = joined.shape[1] // (3 * lane)

    def block(start):
        return pl.BlockSpec((length, lane), lambda r, h: (r, start + h))

    out = jax.ShapeDtypeStruct((rows * length, pairs * lane), BF)
    return pl.pallas_call(
        attend_back_kernel,
        grid=(rows, pairs),
        in_specs=[
            pl.BlockSpec((1, length, 1), lambda r, h: (r, 0, 0)),
            pl.BlockSpec((1, 1, length), lambda r, h: (r, 0, 0)),
            block(first),
            block(all_pairs + first),
            block(2 * all_pairs + first),
            pl.BlockSpec((1, 1, 2, length), lambda r, h: (r, h, 0, 0)),
            block(first),
        ],
        out_specs=[block(0), block(0), block(0)],
        out_shape=[out, out, out],
        scratch_shapes=[pltpu.VMEM((length, length), F32)],
        name="attend_back",
    )(segments[:, :, None], segments[:, None, :], joined, joined, joined, logs, grad_mixed)


def exact_gelu(values):
    return jax.nn.gelu(values, approximate=False)


def shards(
    tokens,
    segments,
    pad_mask,
    dest_shard,
    dest_slot,
    ln1_gain,
    ln1_bias,
    qkv_weight,
    qv_bias,
    out_weight,
    out_bias,
    ln2_gain,
    ln2_bias,
    fc1_weight,
    fc1_bias,
    fc2_weight,
    fc2_bias,
    learn_gain,
    learn_bias,
    maps_weight,
    maps_bias,
    out_grad,
):
    wires = Wires()
    seq = wires.seq
    rows_all, slots_half, width = tokens.shape
    ff = fc1_bias.shape[0] * wires.count * 2
    devices = wires.count * 2
    m = width // devices
    wide = ff // width
    rows_here = rows_all // 2
    row_len = slots_half * 2
    count_tok = rows_here * row_len
    records = rows_here * IMG_ROW
    capacity = out_grad.shape[1]

    small = jnp.concatenate(
        [
            ln1_gain[None],
            ln1_bias[None],
            qv_bias,
            out_bias[None],
            ln2_gain[None],
            ln2_bias[None],
            fc2_bias[None],
            fc1_bias.reshape(wide, m),
        ],
        axis=0,
    )
    n_small = small.shape[0]
    pad_cols = 256
    riding = jnp.concatenate(
        [qkv_weight, jnp.pad(small.T, ((0, 0), (0, pad_cols - n_small)))], axis=1
    )

    def other_rows(value):
        return lax.dynamic_slice_in_dim(value, (1 - seq) * rows_here, rows_here, 0)

    def own_rows(value):
        return lax.dynamic_slice_in_dim(value, seq * rows_here, rows_here, 0)

    came = wires.swap(other_rows(tokens))
    mine = own_rows(tokens)
    first = jnp.where(seq == 0, mine, came)
    second = jnp.where(seq == 0, came, mine)
    inputs_low = jnp.concatenate([first, second], axis=1).reshape(count_tok, width)
    grad_came = wires.swap(out_grad)
    ga, gb, gc, gd = [Gather(wires, w) for w in (riding, out_weight, fc1_weight, fc2_weight)]
    ga.step()
    top_a = ga.flight
    ga.step()
    gb.step(top_a)
    gc.step(gb.flight)
    mid_a = ga.flight
    ga.step()
    gd.step(gc.flight)
    gb.step(mid_a)
    late_a = ga.flight
    ga.step()
    gb.step(late_a)
    qkv_all = ga.result()
    qkv_full = qkv_all[:, : 3 * width]
    small_full = qkv_all[:, 3 * width : 3 * width + 128].T[:n_small].astype(F32)
    norm1_gain, norm1_shift, q_shift, v_shift, out_shift, norm2_gain, norm2_shift, fc2_shift = [
        small_full[i] for i in range(8)
    ]
    fc1_shift = small_full[8:n_small].reshape(wide, devices, m).transpose(1, 0, 2).reshape(ff)
    seg = own_rows(segments)
    seg_flat = seg.reshape(count_tok)
    mask = (seg_flat >= 0).astype(F32)

    inputs = inputs_low.astype(F32)
    normed1, inverse1 = norm_stats(inputs)
    attn_in = (normed1 * norm1_gain + norm1_shift).astype(BF)
    qkv_out = dot_plain(attn_in, qkv_full)
    joined_shift = jnp.concatenate([q_shift, jnp.zeros_like(q_shift), v_shift])
    joined = (qkv_out + joined_shift).astype(BF)
    pairs = width // (4 * HEAD_DIM)
    gb.step()
    gc.step(gb.flight)
    joined = gate(joined, gc.sends)
    mixed_a, logs_a = attend(joined, seg, 0, pairs)
    out_full = gb.result()
    gc.step((mixed_a,))
    joined_b = gate(joined, (gc.sends, mixed_a))
    mixed_b, logs_b = attend(joined_b, seg, pairs, pairs)
    mixed = jnp.concatenate([mixed_a, mixed_b], axis=1)
    resid1 = inputs + dot_plain(mixed, out_full) + out_shift
    normed2, inverse2 = norm_stats(resid1)
    mlp_in = (normed2 * norm2_gain + norm2_shift).astype(BF)
    gc.step()
    gd.step(gc.flight)
    fc1_full = gc.result()
    fc1_full = gate(fc1_full, gd.sends)
    hidden = dot_plain(mlp_in, fc1_full) + fc1_shift
    gd.step()
    gd.step()
    fc2_full = gd.result()
    activated, gelu_back = jax.vjp(exact_gelu, hidden)
    activated_low = activated.astype(BF)
    resid2 = resid1 + dot_plain(activated_low, fc2_full) + fc2_shift

    learn_scale = learn_gain.astype(F32)
    normed3, inverse3 = norm_stats(resid2)
    normed3_out = normed3 * learn_scale + learn_bias.astype(F32)
    map_weight = maps_weight.astype(F32)
    logits = dot_second(normed3_out, map_weight, HIGH) + maps_bias.astype(F32)
    sigmas = jax.nn.sigmoid(logits)
    map_vals = sigmas * mask[:, None]
    row_index = jnp.arange(count_tok, dtype=jnp.int32) // row_len
    owner = jnp.where(seg_flat >= 0, row_index * IMG_ROW + seg_flat, -1)
    select = (owner[:, None] == jnp.arange(records, dtype=jnp.int32)[None, :]).astype(F32)
    token_weights = (select[:, :, None] * map_vals[:, None, :]).reshape(count_tok, records * NTOK)
    sums = dot_first(token_weights, resid2, HIGH)
    counts = jnp.sum(select * mask[:, None], axis=0)
    divisor = jnp.maximum(counts, 1.0)
    positions = own_rows(dest_shard * capacity + dest_slot).reshape(records)
    routing = (
        (positions[None, :] == jnp.arange(2 * capacity, dtype=jnp.int32)[:, None])
        & (counts > 0.0)[None, :]
    ).astype(BF)
    pooled_here = (sums.reshape(records, NTOK * width) / divisor[:, None]).astype(BF)
    pooled_all = dot_plain(routing, pooled_here).astype(BF).reshape(2, capacity, NTOK * width)
    pooled_came = wires.swap(pick(pooled_all, 1 - seq, 0))
    pooled = (pick(pooled_all, seq, 0).astype(F32) + pooled_came.astype(F32)).astype(BF)
    pooled = pooled.reshape(1, capacity, NTOK, width)

    grad_own = out_grad.reshape(capacity, NTOK * width)
    grad_far = grad_came.reshape(capacity, NTOK * width)
    grad_pos = jnp.where(
        seq == 0,
        jnp.concatenate([grad_own, grad_far], axis=0),
        jnp.concatenate([grad_far, grad_own], axis=0),
    )
    grad_records = (dot_first(routing, grad_pos) / divisor[:, None]).astype(BF)
    grad_records = grad_records.reshape(records * NTOK, width).astype(F32)

    grad_resid2 = dot_plain(token_weights, grad_records, HIGH)
    grad_maps_all = dot_second(resid2, grad_records, HIGH).reshape(count_tok, records, NTOK)
    grad_map_vals = jnp.sum(grad_maps_all * select[:, :, None], axis=1)
    grad_logits = grad_map_vals * mask[:, None] * sigmas * (1.0 - sigmas)
    grad_maps_weight = dot_first(grad_logits, normed3_out, HIGH)
    grad_maps_bias = jnp.sum(grad_logits, axis=0)
    grad_normed3 = dot_plain(grad_logits, map_weight, HIGH)
    back_three, grad_learn_gain, grad_learn_bias = norm_backward(
        grad_normed3, normed3, inverse3, learn_scale
    )
    grad_resid2 = grad_resid2 + back_three
    grad_branch2 = grad_resid2.astype(BF)
    s_fc2 = Scatter(wires, dot_first(activated_low, grad_branch2).astype(BF))
    s_fc2.step()
    grad_branch2 = gate(grad_branch2, s_fc2.sends)
    grad_fc2_shift = jnp.sum(grad_branch2.astype(F32), axis=0)
    grad_activ = dot_second(grad_branch2, fc2_full).astype(BF)
    grad_hidden = gelu_back(grad_activ.astype(F32))[0].astype(BF)
    s_fc2.step()
    grad_hidden = gate(grad_hidden, s_fc2.sends)
    s_fc1 = Scatter(wires, dot_first(mlp_in, grad_hidden).astype(BF))
    s_fc1.step()
    grad_hidden = gate(grad_hidden, s_fc1.sends)
    grad_fc1_shift = jnp.sum(grad_hidden.astype(F32), axis=0)
    grad_normed2 = dot_second(grad_hidden, fc1_full)
    back_two, grad_norm2_gain, grad_norm2_shift = norm_backward(
        grad_normed2, normed2, inverse2, norm2_gain
    )
    grad_resid1 = grad_resid2 + back_two
    grad_branch1 = grad_resid1.astype(BF)
    s_fc2.step()
    grad_branch1 = gate(grad_branch1, s_fc2.sends)
    s_out = Scatter(wires, dot_first(mixed, grad_branch1).astype(BF))
    s_out.step()
    grad_out_shift = jnp.sum(grad_branch1.astype(F32), axis=0)
    grad_branch1 = gate(grad_branch1, s_out.sends)
    grad_mixed = dot_second(grad_branch1, out_full).astype(BF)
    s_fc1.step()
    s_fc2.step()
    grad_mixed = gate(grad_mixed, (s_fc1.sends, s_fc2.sends))
    early = jnp.concatenate(
        [
            jnp.stack(
                [
                    grad_learn_gain,
                    grad_learn_bias,
                    grad_out_shift,
                    grad_norm2_gain,
                    grad_norm2_shift,
                    grad_fc2_shift,
                    jnp.pad(grad_maps_bias, (0, width - NTOK)),
                ]
            ),
            grad_maps_weight,
            grad_fc1_shift.reshape(wide, width),
        ],
        axis=0,
    )
    early = sum_everywhere(wires, jnp.pad(early, ((0, -early.shape[0] % 8), (0, 0))))
    dq_a, dk_a, dv_a = attend_back(joined, logs_a, grad_mixed, seg, 0, pairs)
    grad_a = jnp.concatenate([dq_a, dk_a, dv_a], axis=1)
    s_a = Scatter(wires, dot_first(attn_in, grad_a).astype(BF))
    s_a.step()
    s_fc1.step()
    s_out.step()
    grad_mixed = gate(grad_mixed, (s_a.sends, s_fc1.sends, s_out.sends))
    dq_b, dk_b, dv_b = attend_back(joined, logs_b, grad_mixed, seg, pairs, pairs)
    grad_b = jnp.concatenate([dq_b, dk_b, dv_b], axis=1)
    s_a.step()
    s_out.step()
    s_fc1.step()
    done_fc2 = s_fc2.result()
    grad_b = gate(grad_b, (s_a.sends, s_out.sends, s_fc1.sends, done_fc2))
    s_b = Scatter(wires, dot_first(attn_in, grad_b).astype(BF))
    s_b.step()
    s_a.step()
    s_out.step()
    grad_a, grad_b = gate((grad_a, grad_b), (s_a.sends, s_out.sends, s_b.sends, early))
    half = pairs * 2 * HEAD_DIM
    cuts = [slice(i * width + c * half, i * width + (c + 1) * half) for c in (0, 1) for i in range(3)]
    grad_normed1 = sum(
        dot_second(g, jnp.concatenate([qkv_full[:, c] for c in cuts[3 * i : 3 * i + 3]], axis=1))
        for i, g in enumerate((grad_a, grad_b))
    )
    s_b.step()
    grad_normed1 = gate(grad_normed1, s_b.sends)
    back_one, grad_norm1_gain, grad_norm1_shift = norm_backward(
        grad_normed1, normed1, inverse1, norm1_gain
    )
    sum_q, sum_v = [
        jnp.concatenate(
            [jnp.sum(g[:, i * half : (i + 1) * half].astype(F32), axis=0) for g in (grad_a, grad_b)]
        )
        for i in (0, 2)
    ]
    late = jnp.stack([grad_norm1_gain, grad_norm1_shift, sum_q, sum_v])
    late = sum_everywhere(wires, jnp.pad(late, ((0, 4), (0, 0))))
    s_a.step()
    s_b.step()
    s_b.step()
    done_a, done_b = s_a.result(), s_b.result()
    done_out, done_fc1 = s_out.result(), s_fc1.result()
    done_qkv = jnp.concatenate(
        [d[:, i * half : (i + 1) * half] for i in range(3) for d in (done_a, done_b)], axis=1
    )
    place = lax.axis_index("rows") * 2 + seq
    held = lax.dynamic_slice_in_dim(jnp.concatenate([early[2:6], late[:4]]), place * m, m, 1)
    held_fc1 = lax.dynamic_slice_in_dim(
        early[7 + NTOK : 7 + NTOK + wide].reshape(ff), place * wide * m, wide * m, 0
    )
    grad_rows = (grad_resid1 + back_one).reshape(rows_here, row_len, width)
    grad_away = lax.dynamic_slice_in_dim(grad_rows, (1 - seq) * slots_half, slots_half, 1)
    grad_back = wires.swap(grad_away)
    grad_kept = lax.dynamic_slice_in_dim(grad_rows, seq * slots_half, slots_half, 1)
    grad_held = jnp.where(
        seq == 0,
        jnp.concatenate([grad_kept, grad_back], axis=0),
        jnp.concatenate([grad_back, grad_kept], axis=0),
    )
    return (
        pooled,
        grad_held,
        held[4],
        held[5],
        done_qkv,
        held[6:8],
        done_out,
        held[0],
        held[1],
        held[2],
        done_fc1,
        held_fc1,
        done_fc2,
        held[3],
        early[0],
        early[1],
        early[7 : 7 + NTOK],
        early[6, :NTOK],
    )


def solution(mesh):
    both = ("rows", "seq")
    in_specs = (
        P("rows", "seq", None),
        P("rows", None),
        P("rows", "seq"),
        P("rows", None),
        P("rows", None),
        P(both),
        P(both),
        P(both, None),
        P(None, both),
        P(both, None),
        P(both),
        P(both),
        P(both),
        P(both, None),
        P(both),
        P(both, None),
        P(both),
        P(),
        P(),
        P(),
        P(),
        P("rows", "seq", None, None),
    )
    out_specs = (
        P("rows", "seq", None, None),
        P("rows", "seq", None),
        P(both),
        P(both),
        P(both, None),
        P(None, both),
        P(both, None),
        P(both),
        P(both),
        P(both),
        P(both, None),
        P(both),
        P(both, None),
        P(both),
        P(),
        P(),
        P(),
        P(),
    )
    return jax.shard_map(shards, mesh=mesh, in_specs=in_specs, out_specs=out_specs, check_vma=False)
```

time: 1590 us -> 676 us (0.43)
  waiting for transfers between devices: 908 us -> 137 us
  matrix products: 345 us -> 178 us
  blocking collectives: 127 us -> 0 us
  starting transfers between devices: 4.22 us -> 103 us
  Pallas kernels: 0 us -> 89.8 us
    reduce_scatter x6 -> x0, waiting for transfers between devices: 672 us -> none  [the longest x1 187 us: shards(): lax.psum_scatter(grad_fc2, ('rows', 'seq'), scatter_dimension=0, tiled=True)]
    unnamed x16 -> x0, waiting for transfers between devices: 178 us -> none
    dot_general x35 -> x22, matrix products: 345 us -> 178 us  [the longest x7 86.2 us: dot_plain(): return jnp.dot(a, b, precision=precision, preferred_element_type=F32)]
    ppermute x0 -> x113, waiting for transfers between devices: none -> 137 us  [the longest x78 95.8 us: turn(): return lax.ppermute(value, 'rows', rotation(self.dims, place, step))]
    ppermute x0 -> x113, starting transfers between devices: none -> 103 us  [the longest x78 92.4 us: turn(): return lax.ppermute(value, 'rows', rotation(self.dims, place, step))]
    pallas_call x0 -> x8, Pallas kernels: none -> 89.8 us  [the longest x2 35 us: attend_back(): pl.pallas_call(attend_back_kernel, grid=(rows, pairs), in_specs=[pl.Block...]
    all_gather x3 -> x0, blocking collectives: 80 us -> none  [the longest x1 40.7 us: shards(): lax.all_gather(qv_bias, ('rows', 'seq'), axis=1, tiled=True)]
    all_gather x6 -> x0, waiting for transfers between devices: 57 us -> none  [the longest x1 29.9 us: shards(): lax.all_gather(fc1_weight, ('rows', 'seq'), axis=0, tiled=True)]
  transfers between devices with their start and end apart: 15 -> 113, of which waited for: 9 -> 41; matrix products, arithmetic and copies ran while one was open for 17% -> 40% of each run, Pallas kernels for 0% -> 12%
where the time goes in v1:
time: 676 us; the launch traced here: 672 us
  matrix products  178 us (26%)
  waiting for transfers between devices  137 us (20%)
  starting transfers between devices  103 us (15%)
  local copies, waits for them, and re-layouts  94.3 us (14%)
  Pallas kernels  89.8 us (13%)
  other arithmetic  67.4 us (10%)
    ppermute x78, waiting for transfers between devices, turn(): return lax.ppermute(value, 'rows', rotation(self.dims, place, step))  95.8 us
    ppermute x78, starting transfers between devices, turn(): return lax.ppermute(value, 'rows', rotation(self.dims, place, step))  92.4 us
    dot_general x7, matrix products, dot_plain(): return jnp.dot(a, b, precision=precision, preferred_element_type=F32)  86.2 us
    dot_general x7, matrix products, dot_second(): lax.dot_general(a, b, (((1,), (1,)), ((), ())), precision=precision, pref...  50.7 us
    dot_general x8, matrix products, dot_first(): lax.dot_general(a, b, (((0,), (0,)), ((), ())), precision=precision, pref...  41.1 us
    ppermute x8, waiting for transfers between devices, sum_everywhere(): lax.ppermute(value, 'rows', crossing(wires.dims, place, step))  39.8 us
    pallas_call x2, Pallas kernels, attend_back(): pl.pallas_call(attend_back_kernel, grid=(rows, pairs), in_specs=[pl.Block...  35 us
    pallas_call x4, Pallas kernels, result(): pl.pallas_call(place_kernel(len(parts), wires.dims, m, self.half), out_sh...  28.1 us
  transfers between devices with their start and end apart: 113, of which 41 were waited for; matrix products, arithmetic and copies ran while one was open for 40% of the time, Pallas kernels for 12%

profile of v1, /device:TPU:0, one launch (start us, length us, event | category | flops | bytes accessed | tf_op | source)
XLA Modules:
  0.0 672.1 jit_solution(2263139379117127563)
XLA Ops:
  7.9 5.1 collective-permute-start.3
  27.2 3.9 collective-permute-done.2
  43.3 3.0 collective-permute-done.4
  48.7 3.3 collective-permute-done.6
  53.0 11.1 %collective-permute-done.16 = bf16[32,4096]{1,0:T(8,128)(2,1)S(1)} collective-permute-done((bf16[32,4096]{1,0:T(8,128)(2,1)S(1)}, bf16[32,4096]{1,0:T(8,128)(2,1)S(1)}, u32[]{:S(2)}, u32[]{:S(2)}) %collective-permute-start.16) | collective-permute-done | bytes 262176 | tf_op jit(solution)/shard_map/ppermute | solution.py:97
  64.7 3.4 collective-permute-done.5.refs_1_
  76.8 3.0 collective-permute-done.21.refs_1_
  80.3 3.4 collective-permute-done.24.refs_3_
  91.7 7.2 %place.4 = bf16[1024,3328]{1,0:T(8,128)(2,1)} custom-call(s32[4]{0:T(128)} %pad_add_fusion.where, bf16[8,32,1664]{2,1,0:T(8,128)(2,1)} %constant_dynamic-update-slice_fusion.refs_0_, bf16[8,32,1664]{2,1,0:T(8,128)(2,1)} %copy-done.46, bf16[8,32,1664]{2,1,0:T(8,128)(2,1)} %constant_dynamic-update-slice_fusion.5.refs_2_, bf16[8,32,1664]{2,1,0:T(8,128)(2,1)} %copy-done.47, ...), custom_call_target="tpu_custom_call" | custom-call | tf_op jit(solution)/shard_map/place/pallas_call | solution.py:209
  105.1 8.6 %add_convert_fusion.q_ref.k_ref.v_ref = bf16[1024,3072]{1,0:T(8,128)(2,1)} fusion(f32[3072]{0:T(1024)S(1)} %pad_maximum_fusion.19, bf16[1024,1024]{1,0:T(8,128)(2,1)S(1)} %fusion.28, bf16[1024,3328]{1,0:T(8,128)(2,1)S(1)} %copy-done.8), kind=kOutput, calls=%fused_computation.26 | convolution fusion | flops 6448742400 | bytes 14692352 | tf_op jit(solution)/shard_map/dot_general | solution.py:21
  113.7 13.3 %attend.2 = (bf16[1024,512]{1,0:T(8,128)(2,1)}, f32[2,4,2,512]{3,2,1,0:T(2,128)}) custom-call(s32[2,512,1]{2,1,0:T(8,128)} %copy.66.seg_col, s32[2,1,512]{2,1,0:T(1,128)} %broadcast_in_dim.20.seg_row, bf16[1024,3072]{1,0:T(8,128)(2,1)} %add_convert_fusion.q_ref.k_ref.v_ref, bf16[1024,3072]{1,0:T(8,128)(2,1)} %add_convert_fusion.q_ref.k_ref.v_ref, ...), custom_call_target="tpu_custom_call" | custom-call | tf_op jit(solution)/shard_map/attend/pallas_call | solution.py:329
  149.3 13.0 %collective-permute-done.35 = bf16[128,1024]{1,0:T(8,128)(2,1)} collective-permute-done((bf16[128,1024]{1,0:T(8,128)(2,1)}, bf16[128,1024]{1,0:T(8,128)(2,1)}, u32[]{:S(2)}, u32[]{:S(2)}) %collective-permute-start.35) | collective-permute-done | bytes 262176 | tf_op jit(solution)/shard_map/ppermute | solution.py:97
  166.3 4.0 place.5
  170.4 5.7 fusion.242
  179.6 13.4 %attend.3 = (bf16[1024,512]{1,0:T(8,128)(2,1)}, f32[2,4,2,512]{3,2,1,0:T(2,128)}) custom-call(s32[2,512,1]{2,1,0:T(8,128)} %copy.66.seg_col, s32[2,1,512]{2,1,0:T(1,128)} %broadcast_in_dim.20.seg_row, bf16[1024,3072]{1,0:T(8,128)(2,1)} %add_convert_fusion.q_ref.k_ref.v_ref, bf16[1024,3072]{1,0:T(8,128)(2,1)} %add_convert_fusion.q_ref.k_ref.v_ref, ...), custom_call_target="tpu_custom_call" | custom-call | tf_op jit(solution)/shard_map/attend/pallas_call | solution.py:329
  208.4 8.4 %place.6 = bf16[1024,4096]{1,0:T(8,128)(2,1)} custom-call(s32[4]{0:T(128)} %pad_add_fusion.where, bf16[8,32,2048]{2,1,0:T(8,128)(2,1)} %pad_maximum_fusion.2.refs_0_, bf16[8,32,2048]{2,1,0:T(8,128)(2,1)} %collective-permute-done.28.refs_1_, bf16[8,32,2048]{2,1,0:T(8,128)(2,1)} %pad_maximum_fusion.3.refs_2_, ...), custom_call_target="tpu_custom_call" | custom-call | tf_op jit(solution)/shard_map/place/pallas_call | solution.py:209
  217.4 7.0 %collective-permute-done.40.refs_3_ = bf16[8,128,512]{2,1,0:T(8,128)(2,1)} collective-permute-done((bf16[8,128,512]{2,1,0:T(8,128)(2,1)}, bf16[8,128,512]{2,1,0:T(8,128)(2,1)}, u32[]{:S(2)}, u32[]{:S(2)}) %collective-permute-start.40) | collective-permute-done | bytes 1048608 | tf_op jit(solution)/shard_map/ppermute | solution.py:97
  227.3 51.1 %multiply_convert_fusion = (bf16[1024,4096]{1,0:T(8,128)(2,1)}, f32[1024,4096]{1,0:T(8,128)}, f32[1024,4096]{1,0:T(8,128)}) fusion(f32[4096]{0:T(1024)S(1)} %add.2062, bf16[1024,4096]{1,0:T(8,128)(2,1)} %place.6, f32[1024,1024]{1,0:T(8,128)} %copy-done.10, f32[1024]{0:T(1024)S(1)} %get-tuple-element.118, f32[1024]{0:T(1024)S(1)} %get-tuple-element.116, ...), kind=kOutput, calls=%fused_computation.12 | convolution fusion | flops 8872001536 | bytes 54558720 | tf_op jit(solution)/shard_map/dot_general | solution.py:21
  278.5 8.4 %place.7 = bf16[4096,1024]{1,0:T(8,128)(2,1)} custom-call(s32[4]{0:T(128)} %pad_add_fusion.where, bf16[8,128,512]{2,1,0:T(8,128)(2,1)} %constant_dynamic-update-slice_fusion.12.refs_0_, bf16[8,128,512]{2,1,0:T(8,128)(2,1)} %collective-permute-done.38.refs_1_, bf16[8,128,512]{2,1,0:T(8,128)(2,1)} %constant_dynamic-update-slice_fusion.14.refs_2_, ...), custom_call_target="tpu_custom_call" | custom-call | tf_op jit(solution)/shard_map/place/pallas_call | solution.py:209
  286.9 14.6 %fusion.255 = (f32[1024]{0:T(1024)S(1)}, f32[1024,1024]{1,0:T(8,128)S(1)}) fusion(f32[1024]{0:T(1024)S(1)} %copy-done.94, f32[1024,1024]{1,0:T(8,128)} %copy-done.10, bf16[1024,4096]{1,0:T(8,128)(2,1)} %get-tuple-element.128, bf16[4096,1024]{1,0:T(8,128)(2,1)} %place.7), kind=kOutput, calls=%fused_computation.643 | convolution fusion | flops 8593079296 | bytes 25174016 | tf_op jit(solution)/shard_map/dot_general | solution.py:21
  308.3 3.1 multiply_reduce_fusion.1
  311.5 4.3 fusion.256
  315.9 9.8 %convolution_convert_fusion.2 = bf16[4096,1024]{1,0:T(8,128)(2,1)S(1)} fusion(bf16[1024,4096]{1,0:T(8,128)(2,1)S(1)} %bitcast.819, bf16[1024,1024]{1,0:T(8,128)(2,1)S(1)} %get-tuple-element.81), kind=kOutput, calls=%fused_computation.31 | convolution fusion | flops 8594128896 | bytes 18874368 | tf_op jit(solution)/shard_map/dot_general | solution.py:25
  325.7 4.7 dynamic-slice_bitcast_fusion.2
  335.6 23.0 %fusion.5 = bf16[1024,4096]{1,0:T(8,128)(2,1)} fusion(f32[1024,4096]{1,0:T(8,128)} %get-tuple-element.129, f32[1024,4096]{1,0:T(8,128)} %get-tuple-element.251, f32[4096]{0:T(1024)S(1)} %copy-done.84, bf16[1024,1024]{1,0:T(8,128)(2,1)S(1)} %get-tuple-element.81, bf16[4096,1024]{1,0:T(8,128)(2,1)} %place.7), kind=kOutput, calls=%fused_computation.8 | convolution fusion | flops 8661237760 | bytes 52445184 | tf_op jit(solution)/shard_map/dot_general | solution.py:31
  371.7 16.1 %convolution_convert_fusion.1 = bf16[1024,4096]{1,0:T(8,128)(2,1)} fusion(bf16[1024,4096]{1,0:T(8,128)(2,1)} %fusion.5, f32[1024,1024]{1,0:T(8,128)S(1)} %copy-done.11, f32[1024]{0:T(1024)S(1)} %copy-done.93, f32[1024]{0:T(1024)S(1)} %copy-done.87, f32[1024]{0:T(1024)S(1)} %copy-done.82, f32[1024]{0:T(1024)S(1)} %copy-done.76), kind=kOutput, calls=%fused_computation.30 | convolution fusion | flops 8599371776 | bytes 20987904 | tf_op jit(solution)/shard_map/dot_general | solution.py:25
  387.9 7.8 %dynamic-slice_bitcast_fusion = (bf16[4,2,2,32,4096]{4,3,2,1,0:T(8,128)(2,1)}, bf16[4,2,2,32,4096]{4,3,2,1,0:T(8,128)(2,1)}) fusion(bf16[4,2,2,2,32,4096]{5,4,3,2,1,0:T(8,128)(2,1)} %bitcast.767, s32[]{:T(128)S(6)} %select_n.423, s32[]{:T(128)S(6)} %select_n.424), kind=kLoop, calls=%fused_computation.60 | loop fusion | bytes 16777224 | tf_op jit(solution)/shard_map/jit(dynamic_index_in_dim)/squeeze | solution.py:228
  395.7 13.5 %multiply_reduce_fusion = (f32[1024]{0:T(1024)S(1)}, f32[1024]{0:T(1024)S(1)}, f32[1024]{0:T(1024)S(1)}, f32[1024]{0:T(1024)S(1)}, f32[1024,1024]{1,0:T(8,128)}) fusion(f32[1024,1024]{1,0:T(8,128)S(1)} %copy-done.11, f32[1024]{0:T(1024)S(1)} %copy-done.82, f32[1024]{0:T(1024)S(1)} %copy-done.76, f32[1024]{0:T(1024)S(1)} %copy-done.87, ...), kind=kOutput, calls=%fused_computation.57 | convolution fusion | flops 8599367680 | bytes 25194496 | tf_op jit(solution)/shard_map/dot_general | solution.py:31
  409.2 4.6 convert_reduce_fusion
  414.3 7.0 %fusion.240 = (bf16[1024,1024]{1,0:T(8,128)(2,1)S(1)}, f32[1024,1024]{1,0:T(8,128)}) fusion(f32[1024,1024]{1,0:T(8,128)} %get-tuple-element.256, f32[1024]{0:T(1024)S(1)} %broadcast_multiply_fusion.4, f32[1024,1024]{1,0:T(8,128)} %copy-done.10, f32[1024]{0:T(1024)S(1)} %copy-done.76, f32[1024]{0:T(1024)S(1)} %broadcast_multiply_fusion.5, ...), kind=kLoop, calls=%fused_computation.629 | loop fusion | flops 9437184 | bytes 18894848 | tf_op jit(solution)/shard_map/convert_element_type | solution.py:593
  434.0 11.6 %collective-permute-done.72 = f32[24,1024]{1,0:T(8,128)S(1)} collective-permute-done((f32[24,1024]{1,0:T(8,128)S(1)}, f32[24,1024]{1,0:T(8,128)S(1)}, u32[]{:S(2)}, u32[]{:S(2)}) %collective-permute-start.72) | collective-permute-done | bytes 98336 | tf_op jit(solution)/shard_map/ppermute | solution.py:296
  446.9 3.4 collective-permute-done.73
  450.4 3.8 convolution_convert_fusion.5.do_ref
  455.2 6.4 collective-permute-done.75
  472.7 6.1 collective-permute-done.62
  483.0 3.0 collective-permute-done.65
  514.3 17.6 %attend_back.2 = (bf16[1024,512]{1,0:T(8,128)(2,1)}, bf16[1024,512]{1,0:T(8,128)(2,1)}, bf16[1024,512]{1,0:T(8,128)(2,1)}) custom-call(s32[2,512,1]{2,1,0:T(8,128)} %copy.66.seg_col, s32[2,1,512]{2,1,0:T(1,128)} %broadcast_in_dim.20.seg_row, bf16[1024,3072]{1,0:T(8,128)(2,1)} %add_convert_fusion.q_ref.k_ref.v_ref, ...), custom_call_target="tpu_custom_call" | custom-call | tf_op jit(solution)/shard_map/attend_back/pallas_call | solution.py:383
  534.7 3.8 convolution_convert_fusion.4
  548.8 17.4 %attend_back.3 = (bf16[1024,512]{1,0:T(8,128)(2,1)}, bf16[1024,512]{1,0:T(8,128)(2,1)}, bf16[1024,512]{1,0:T(8,128)(2,1)}) custom-call(s32[2,512,1]{2,1,0:T(8,128)} %copy.66.seg_col, s32[2,1,512]{2,1,0:T(1,128)} %broadcast_in_dim.20.seg_row, bf16[1024,3072]{1,0:T(8,128)(2,1)} %add_convert_fusion.q_ref.k_ref.v_ref, ...), custom_call_target="tpu_custom_call" | custom-call | tf_op jit(solution)/shard_map/attend_back/pallas_call | solution.py:383
  578.8 3.8 convolution_convert_fusion.3
  587.8 6.7 collective-permute-done.111
  599.0 3.4 fusion.43
  602.5 3.5 fusion.57
  610.1 3.0 collective-permute-start.85
  613.3 3.8 collective-permute-start.95
  628.7 8.7 %collective-permute-done.79 = f32[8,1024]{1,0:T(8,128)S(1)} collective-permute-done((f32[8,1024]{1,0:T(8,128)S(1)}, f32[8,1024]{1,0:T(8,128)S(1)}, u32[]{:S(2)}, u32[]{:S(2)}) %collective-permute-start.79) | collective-permute-done | bytes 32800 | tf_op jit(solution)/shard_map/ppermute | solution.py:296
  646.2 3.9 collective-permute-done.82
  656.2 3.8 collective-permute-start.91
  (647 shorter events, 270.1 us)
Async XLA Ops:
  7.9 19.4 %collective-permute-start.3 = (bf16[32,3328]{1,0:T(8,128)(2,1)S(1)}, bf16[32,3328]{1,0:T(8,128)(2,1)S(1)}, u32[]{:S(2)}, u32[]{:S(2)}) collective-permute-start(bf16[32,3328]{1,0:T(8,128)(2,1)S(1)} %fusion.130), channel_id=1, source_target_pairs={{0,24},{2,26},{4,28},{6,30},{8,0},{10,2},{12,4},{14,6},{16,8},{18,... | collective-permute-start | bytes 638984 | tf_op jit(solution)/shard_map/ppermute | solution.py:97
  13.0 18.1 %collective-permute-start.2 = (bf16[32,3328]{1,0:T(8,128)(2,1)S(1)}, bf16[32,3328]{1,0:T(8,128)(2,1)S(1)}, u32[]{:S(2)}, u32[]{:S(2)}) collective-permute-start(bf16[32,3328]{1,0:T(8,128)(2,1)S(1)} %fusion.130), channel_id=1, source_target_pairs={{0,16},{2,18},{4,20},{6,22},{8,24},{10,26},{12,28},{14,30},{16,0},... | collective-permute-start | bytes 638984 | tf_op jit(solution)/shard_map/ppermute | solution.py:97
  13.0 18.1 %collective-permute-start.1 = (bf16[32,3328]{1,0:T(8,128)(2,1)S(1)}, bf16[32,3328]{1,0:T(8,128)(2,1)S(1)}, u32[]{:S(2)}, u32[]{:S(2)}) collective-permute-start(bf16[32,3328]{1,0:T(8,128)(2,1)S(1)} %fusion.130), channel_id=1, source_target_pairs={{0,8},{2,10},{4,12},{6,14},{8,16},{10,18},{12,20},{14,22},{16,24},... | collective-permute-start | bytes 638984 | tf_op jit(solution)/shard_map/ppermute | solution.py:97
  15.3 61.2 %collective-permute-start = (bf16[2,256,1024]{2,1,0:T(8,128)(2,1)S(1)}, bf16[2,256,1024]{2,1,0:T(8,128)(2,1)S(1)}, u32[]{:S(2)}, u32[]{:S(2)}) collective-permute-start(bf16[2,256,1024]{2,1,0:T(8,128)(2,1)S(1)} %constant_dynamic-slice_fusion.100), channel_id=1, source_target_pairs={{0,1},{1,0},{2,3},{3,2},{4,5},{5,4},{6,7},{7,6},{8,9},{9,8},{10,11... | collective-permute-start | bytes 3145736 | tf_op jit(solution)/shard_map/ppermute | solution.py:100
  43.3 20.9 %collective-permute-start.16 = (bf16[32,4096]{1,0:T(8,128)(2,1)S(1)}, bf16[32,4096]{1,0:T(8,128)(2,1)S(1)}, u32[]{:S(2)}, u32[]{:S(2)}) collective-permute-start(bf16[32,4096]{1,0:T(8,128)(2,1)S(1)} %copy-done.59), channel_id=1, source_target_pairs={{0,16},{2,18},{4,20},{6,22},{8,24},{10,26},{12,28},{14,30},{16,0},... | collective-permute-start | bytes 786440 | tf_op jit(solution)/shard_map/ppermute | solution.py:97
  47.2 20.9 %collective-permute-start.5 = (bf16[8,32,1664]{2,1,0:T(8,128)(2,1)}, bf16[8,32,1664]{2,1,0:T(8,128)(2,1)S(1)}, u32[]{:S(2)}, u32[]{:S(2)}) collective-permute-start(bf16[8,32,1664]{2,1,0:T(8,128)(2,1)} %constant_dynamic-update-slice_fusion.refs_0_), channel_id=1, source_target_pairs={{0,4},{2,6},{4,0},{6,2},{8,12},{10,14},{12,8},{14,10},{16,20},{18,... | collective-permute-start | bytes 2555912 | tf_op jit(solution)/shard_map/ppermute | solution.py:97
  52.0 23.3 %collective-permute-start.15 = (bf16[32,4096]{1,0:T(8,128)(2,1)S(1)}, bf16[32,4096]{1,0:T(8,128)(2,1)S(1)}, u32[]{:S(2)}, u32[]{:S(2)}) collective-permute-start(bf16[32,4096]{1,0:T(8,128)(2,1)S(1)} %copy-done.59), channel_id=1, source_target_pairs={{0,8},{2,10},{4,12},{6,14},{8,16},{10,18},{12,20},{14,22},{16,24},... | collective-permute-start | bytes 786440 | tf_op jit(solution)/shard_map/ppermute | solution.py:97
  53.0 17.8 %collective-permute-start.7 = (bf16[8,32,1664]{2,1,0:T(8,128)(2,1)}, bf16[8,32,1664]{2,1,0:T(8,128)(2,1)S(1)}, u32[]{:S(2)}, u32[]{:S(2)}) collective-permute-start(bf16[8,32,1664]{2,1,0:T(8,128)(2,1)} %constant_dynamic-update-slice_fusion.5.refs_2_), channel_id=1, source_target_pairs={{0,2},{2,0},{4,6},{6,4},{8,10},{10,8},{12,14},{14,12},{16,18},{18,... | collective-permute-start | bytes 2555912 | tf_op jit(solution)/shard_map/ppermute | solution.py:97
  89.0 52.5 %collective-permute-start.46 = (bf16[1,20,8,1024]{3,2,1,0:T(8,128)(2,1)}, bf16[1,20,8,1024]{3,2,1,0:T(8,128)(2,1)}, u32[]{:S(2)}, u32[]{:S(2)}) collective-permute-start(bf16[1,20,8,1024]{3,2,1,0:T(8,128)(2,1)} %param.42), channel_id=1, source_target_pairs={{0,1},{1,0},{2,3},{3,2},{4,5},{5,4},{6,7},{7,6},{8,9},{9,8},{10,11... | collective-permute-start | bytes 983048 | tf_op jit(solution)/shard_map/ppermute | solution.py:100
  89.4 37.7 %collective-permute-start.26 = (bf16[4,32,2048]{2,1,0:T(8,128)(2,1)}, bf16[4,32,2048]{2,1,0:T(8,128)(2,1)}, u32[]{:S(2)}, u32[]{:S(2)}) collective-permute-start(bf16[4,32,2048]{2,1,0:T(8,128)(2,1)} %get-tuple-element.71), channel_id=1, source_target_pairs={{0,2},{2,0},{4,6},{6,4},{8,10},{10,8},{12,14},{14,12},{16,18},{18,... | collective-permute-start | bytes 1572872 | tf_op jit(solution)/shard_map/ppermute | solution.py:97
  89.8 39.6 %collective-permute-start.27 = (bf16[4,32,2048]{2,1,0:T(8,128)(2,1)S(1)}, bf16[4,32,2048]{2,1,0:T(8,128)(2,1)}, u32[]{:S(2)}, u32[]{:S(2)}) collective-permute-start(bf16[4,32,2048]{2,1,0:T(8,128)(2,1)S(1)} %get-tuple-element.72), channel_id=1, source_target_pairs={{0,4},{2,6},{4,0},{6,2},{8,12},{10,14},{12,8},{14,10},{16,20},{18,... | collective-permute-start | bytes 1572872 | tf_op jit(solution)/shard_map/ppermute | solution.py:97
  131.5 30.8 %collective-permute-start.28 = (bf16[8,32,2048]{2,1,0:T(8,128)(2,1)}, bf16[8,32,2048]{2,1,0:T(8,128)(2,1)}, u32[]{:S(2)}, u32[]{:S(2)}) collective-permute-start(bf16[8,32,2048]{2,1,0:T(8,128)(2,1)} %pad_maximum_fusion.2.refs_0_), channel_id=1, source_target_pairs={{0,4},{2,6},{4,0},{6,2},{8,12},{10,14},{12,8},{14,10},{16,20},{18,... | collective-permute-start | bytes 3145736 | tf_op jit(solution)/shard_map/ppermute | solution.py:97
  132.7 30.1 %collective-permute-start.29 = (bf16[8,32,2048]{2,1,0:T(8,128)(2,1)}, bf16[8,32,2048]{2,1,0:T(8,128)(2,1)}, u32[]{:S(2)}, u32[]{:S(2)}) collective-permute-start(bf16[8,32,2048]{2,1,0:T(8,128)(2,1)} %pad_maximum_fusion.3.refs_2_), channel_id=1, source_target_pairs={{0,2},{2,0},{4,6},{6,4},{8,10},{10,8},{12,14},{14,12},{16,18},{18,... | collective-permute-start | bytes 3145736 | tf_op jit(solution)/shard_map/ppermute | solution.py:97
  142.8 19.5 %collective-permute-start.35 = (bf16[128,1024]{1,0:T(8,128)(2,1)}, bf16[128,1024]{1,0:T(8,128)(2,1)}, u32[]{:S(2)}, u32[]{:S(2)}) collective-permute-start(bf16[128,1024]{1,0:T(8,128)(2,1)} %param.36), channel_id=1, source_target_pairs={{0,16},{2,18},{4,20},{6,22},{8,24},{10,26},{12,28},{14,30},{16,0},... | collective-permute-start | bytes 786440 | tf_op jit(solution)/shard_map/ppermute | solution.py:97
  148.0 15.9 %collective-permute-start.34 = (bf16[128,1024]{1,0:T(8,128)(2,1)}, bf16[128,1024]{1,0:T(8,128)(2,1)S(1)}, u32[]{:S(2)}, u32[]{:S(2)}) collective-permute-start(bf16[128,1024]{1,0:T(8,128)(2,1)} %param.36), channel_id=1, source_target_pairs={{0,8},{2,10},{4,12},{6,14},{8,16},{10,18},{12,20},{14,22},{16,24},... | collective-permute-start | bytes 786440 | tf_op jit(solution)/shard_map/ppermute | solution.py:97
  149.2 26.9 %collective-permute-start.30 = (bf16[8,32,2048]{2,1,0:T(8,128)(2,1)}, bf16[8,32,2048]{2,1,0:T(8,128)(2,1)}, u32[]{:S(2)}, u32[]{:S(2)}) collective-permute-start(bf16[8,32,2048]{2,1,0:T(8,128)(2,1)} %pad_maximum_fusion.2.refs_0_), channel_id=1, source_target_pairs={{0,1},{1,0},{2,3},{3,2},{4,5},{5,4},{6,7},{7,6},{8,9},{9,8},{10,11... | collective-permute-start | bytes 3145736 | tf_op jit(solution)/shard_map/ppermute | solution.py:100
  162.3 13.8 %collective-permute-start.32 = (bf16[8,32,2048]{2,1,0:T(8,128)(2,1)}, bf16[8,32,2048]{2,1,0:T(8,128)(2,1)}, u32[]{:S(2)}, u32[]{:S(2)}) collective-permute-start(bf16[8,32,2048]{2,1,0:T(8,128)(2,1)} %pad_maximum_fusion.3.refs_2_), channel_id=1, source_target_pairs={{0,1},{1,0},{2,3},{3,2},{4,5},{5,4},{6,7},{7,6},{8,9},{9,8},{10,11... | collective-permute-start | bytes 3145736 | tf_op jit(solution)/shard_map/ppermute | solution.py:100
  176.1 24.3 %collective-permute-start.37 = (bf16[4,128,512]{2,1,0:T(8,128)(2,1)S(1)}, bf16[4,128,512]{2,1,0:T(8,128)(2,1)}, u32[]{:S(2)}, u32[]{:S(2)}) collective-permute-start(bf16[4,128,512]{2,1,0:T(8,128)(2,1)S(1)} %get-tuple-element.78), channel_id=1, source_target_pairs={{0,2},{2,0},{4,6},{6,4},{8,10},{10,8},{12,14},{14,12},{16,18},{18,... | collective-permute-start | bytes 1572872 | tf_op jit(solution)/shard_map/ppermute | solution.py:97
  176.7 20.5 %collective-permute-start.39 = (bf16[4,128,512]{2,1,0:T(8,128)(2,1)S(1)}, bf16[4,128,512]{2,1,0:T(8,128)(2,1)}, u32[]{:S(2)}, u32[]{:S(2)}) collective-permute-start(bf16[4,128,512]{2,1,0:T(8,128)(2,1)S(1)} %copy-done.32), channel_id=1, source_target_pairs={{0,4},{2,6},{4,0},{6,2},{8,12},{10,14},{12,8},{14,10},{16,20},{18,... | collective-permute-start | bytes 1572872 | tf_op jit(solution)/shard_map/ppermute | solution.py:97
  199.1 25.3 %collective-permute-start.40 = (bf16[8,128,512]{2,1,0:T(8,128)(2,1)}, bf16[8,128,512]{2,1,0:T(8,128)(2,1)}, u32[]{:S(2)}, u32[]{:S(2)}) collective-permute-start(bf16[8,128,512]{2,1,0:T(8,128)(2,1)} %constant_dynamic-update-slice_fusion.14.refs_2_), channel_id=1, source_target_pairs={{0,2},{2,0},{4,6},{6,4},{8,10},{10,8},{12,14},{14,12},{16,18},{18,... | collective-permute-start | bytes 3145736 | tf_op jit(solution)/shard_map/ppermute | solution.py:97
  202.2 25.0 %collective-permute-start.38 = (bf16[8,128,512]{2,1,0:T(8,128)(2,1)}, bf16[8,128,512]{2,1,0:T(8,128)(2,1)}, u32[]{:S(2)}, u32[]{:S(2)}) collective-permute-start(bf16[8,128,512]{2,1,0:T(8,128)(2,1)} %constant_dynamic-update-slice_fusion.12.refs_0_), channel_id=1, source_target_pairs={{0,4},{2,6},{4,0},{6,2},{8,12},{10,14},{12,8},{14,10},{16,20},{18,... | collective-permute-start | bytes 3145736 | tf_op jit(solution)/shard_map/ppermute | solution.py:97
  216.8 61.6 %collective-permute-start.43 = (bf16[8,128,512]{2,1,0:T(8,128)(2,1)}, bf16[8,128,512]{2,1,0:T(8,128)(2,1)}, u32[]{:S(2)}, u32[]{:S(2)}) collective-permute-start(bf16[8,128,512]{2,1,0:T(8,128)(2,1)} %constant_dynamic-update-slice_fusion.14.refs_2_), channel_id=1, source_target_pairs={{0,1},{1,0},{2,3},{3,2},{4,5},{5,4},{6,7},{7,6},{8,9},{9,8},{10,11... | collective-permute-start | bytes 3145736 | tf_op jit(solution)/shard_map/ppermute | solution.py:100
  216.9 61.5 %collective-permute-start.41 = (bf16[8,128,512]{2,1,0:T(8,128)(2,1)}, bf16[8,128,512]{2,1,0:T(8,128)(2,1)}, u32[]{:S(2)}, u32[]{:S(2)}) collective-permute-start(bf16[8,128,512]{2,1,0:T(8,128)(2,1)} %constant_dynamic-update-slice_fusion.12.refs_0_), channel_id=1, source_target_pairs={{0,1},{1,0},{2,3},{3,2},{4,5},{5,4},{6,7},{7,6},{8,9},{9,8},{10,11... | collective-permute-start | bytes 3145736 | tf_op jit(solution)/shard_map/ppermute | solution.py:100
  224.4 54.0 %collective-permute-start.44 = (bf16[8,128,512]{2,1,0:T(8,128)(2,1)}, bf16[8,128,512]{2,1,0:T(8,128)(2,1)}, u32[]{:S(2)}, u32[]{:S(2)}) collective-permute-start(bf16[8,128,512]{2,1,0:T(8,128)(2,1)} %collective-permute-done.40.refs_3_), channel_id=1, source_target_pairs={{0,1},{1,0},{2,3},{3,2},{4,5},{5,4},{6,7},{7,6},{8,9},{9,8},{10,11... | collective-permute-start | bytes 3145736 | tf_op jit(solution)/shard_map/ppermute | solution.py:100
  227.2 51.2 %collective-permute-start.42 = (bf16[8,128,512]{2,1,0:T(8,128)(2,1)}, bf16[8,128,512]{2,1,0:T(8,128)(2,1)}, u32[]{:S(2)}, u32[]{:S(2)}) collective-permute-start(bf16[8,128,512]{2,1,0:T(8,128)(2,1)} %collective-permute-done.38.refs_1_), channel_id=1, source_target_pairs={{0,1},{1,0},{2,3},{3,2},{4,5},{5,4},{6,7},{7,6},{8,9},{9,8},{10,11... | collective-permute-start | bytes 3145736 | tf_op jit(solution)/shard_map/ppermute | solution.py:100
  330.3 34.8 %collective-permute-start.47 = (bf16[4,2,2,128,1024]{4,3,2,1,0:T(8,128)(2,1)}, bf16[4,2,2,128,1024]{4,3,2,1,0:T(8,128)(2,1)}, u32[]{:S(2)}, u32[]{:S(2)}) collective-permute-start(bf16[4,2,2,128,1024]{4,3,2,1,0:T(8,128)(2,1)} %get-tuple-element.133), channel_id=1, source_target_pairs={{0,1},{1,0},{2,3},{3,2},{4,5},{5,4},{6,7},{7,6},{8,9},{9,8},{10,11... | collective-permute-start | bytes 12582920 | tf_op jit(solution)/shard_map/ppermute | solution.py:100
  335.6 28.5 %collective-permute-start.45 = (bf16[20,8192]{1,0:T(8,128)(2,1)}, bf16[20,8192]{1,0:T(8,128)(2,1)S(1)}, u32[]{:S(2)}, u32[]{:S(2)}) collective-permute-start(bf16[20,8192]{1,0:T(8,128)(2,1)} %dynamic-slice_bitcast_fusion.10), channel_id=1, source_target_pairs={{0,1},{1,0},{2,3},{3,2},{4,5},{5,4},{6,7},{7,6},{8,9},{9,8},{10,11... | collective-permute-start | bytes 983048 | tf_op jit(solution)/shard_map/ppermute | solution.py:100
  368.1 53.3 %collective-permute-start.48 = (bf16[4,2,128,512]{3,2,1,0:T(8,128)(2,1)S(1)}, bf16[4,2,128,512]{3,2,1,0:T(8,128)(2,1)}, u32[]{:S(2)}, u32[]{:S(2)}) collective-permute-start(bf16[4,2,128,512]{3,2,1,0:T(8,128)(2,1)S(1)} %fusion.71), channel_id=1, source_target_pairs={{0,2},{2,0},{4,6},{6,4},{8,10},{10,8},{12,14},{14,12},{16,18},{18,... | collective-permute-start | bytes 3145736 | tf_op jit(solution)/shard_map/ppermute | solution.py:97
  370.3 52.6 %collective-permute-start.49 = (bf16[4,2,128,512]{3,2,1,0:T(8,128)(2,1)}, bf16[4,2,128,512]{3,2,1,0:T(8,128)(2,1)}, u32[]{:S(2)}, u32[]{:S(2)}) collective-permute-start(bf16[4,2,128,512]{3,2,1,0:T(8,128)(2,1)} %fusion.72), channel_id=1, source_target_pairs={{0,4},{2,6},{4,0},{6,2},{8,12},{10,14},{12,8},{14,10},{16,20},{18,... | collective-permute-start | bytes 3145736 | tf_op jit(solution)/shard_map/ppermute | solution.py:97
  413.8 92.8 %collective-permute-start.50 = (bf16[4,2,2,32,4096]{4,3,2,1,0:T(8,128)(2,1)}, bf16[4,2,2,32,4096]{4,3,2,1,0:T(8,128)(2,1)}, u32[]{:S(2)}, u32[]{:S(2)}) collective-permute-start(bf16[4,2,2,32,4096]{4,3,2,1,0:T(8,128)(2,1)} %get-tuple-element.131), channel_id=1, source_target_pairs={{0,1},{1,0},{2,3},{3,2},{4,5},{5,4},{6,7},{7,6},{8,9},{9,8},{10,11... | collective-permute-start | bytes 12582920 | tf_op jit(solution)/shard_map/ppermute | solution.py:100
  428.3 34.0 %collective-permute-start.51 = (bf16[4,128,512]{2,1,0:T(8,128)(2,1)S(1)}, bf16[4,128,512]{2,1,0:T(8,128)(2,1)S(1)}, u32[]{:S(2)}, u32[]{:S(2)}) collective-permute-start(bf16[4,128,512]{2,1,0:T(8,128)(2,1)S(1)} %fusion.78), channel_id=1, source_target_pairs={{0,4},{2,6},{4,0},{6,2},{8,12},{10,14},{12,8},{14,10},{16,20},{18,... | collective-permute-start | bytes 1572872 | tf_op jit(solution)/shard_map/ppermute | solution.py:97
  429.4 36.1 %collective-permute-start.52 = (bf16[4,128,512]{2,1,0:T(8,128)(2,1)S(1)}, bf16[4,128,512]{2,1,0:T(8,128)(2,1)S(1)}, u32[]{:S(2)}, u32[]{:S(2)}) collective-permute-start(bf16[4,128,512]{2,1,0:T(8,128)(2,1)S(1)} %fusion.77), channel_id=1, source_target_pairs={{0,2},{2,0},{4,6},{6,4},{8,10},{10,8},{12,14},{14,12},{16,18},{18,... | collective-permute-start | bytes 1572872 | tf_op jit(solution)/shard_map/ppermute | solution.py:97
  430.2 15.4 %collective-permute-start.72 = (f32[24,1024]{1,0:T(8,128)S(1)}, f32[24,1024]{1,0:T(8,128)S(1)}, u32[]{:S(2)}, u32[]{:S(2)}) collective-permute-start(f32[24,1024]{1,0:T(8,128)S(1)} %pad_add_fusion.1), channel_id=1, source_target_pairs={{0,2},{2,0},{4,6},{6,4},{8,10},{10,8},{12,14},{14,12},{16,18},{18,... | collective-permute-start | bytes 294920 | tf_op jit(solution)/shard_map/ppermute | solution.py:296
  446.8 34.0 %collective-permute-start.55 = (bf16[4,2,2,32,1024]{4,3,2,1,0:T(8,128)(2,1)S(1)}, bf16[4,2,2,32,1024]{4,3,2,1,0:T(8,128)(2,1)S(1)}, u32[]{:S(2)}, u32[]{:S(2)}) collective-permute-start(bf16[4,2,2,32,1024]{4,3,2,1,0:T(8,128)(2,1)S(1)} %get-tuple-element.181), channel_id=1, source_target_pairs={{0,1},{1,0},{2,3},{3,2},{4,5},{5,4},{6,7},{7,6},{8,9},{9,8},{10,11... | collective-permute-start | bytes 3145736 | tf_op jit(solution)/shard_map/ppermute | solution.py:100
  464.5 14.3 %collective-permute-start.62 = (bf16[128,512]{1,0:T(8,128)(2,1)S(1)}, bf16[128,512]{1,0:T(8,128)(2,1)S(1)}, u32[]{:S(2)}, u32[]{:S(2)}) collective-permute-start(bf16[128,512]{1,0:T(8,128)(2,1)S(1)} %get-tuple-element.150), channel_id=1, source_target_pairs={{0,16},{2,18},{4,20},{6,22},{8,24},{10,26},{12,28},{14,30},{16,0},... | collective-permute-start | bytes 393224 | tf_op jit(solution)/shard_map/ppermute | solution.py:97
  511.2 30.5 %collective-permute-start.53 = (bf16[4,2,32,2048]{3,2,1,0:T(8,128)(2,1)}, bf16[4,2,32,2048]{3,2,1,0:T(8,128)(2,1)}, u32[]{:S(2)}, u32[]{:S(2)}) collective-permute-start(bf16[4,2,32,2048]{3,2,1,0:T(8,128)(2,1)} %fusion.73), channel_id=1, source_target_pairs={{0,2},{2,0},{4,6},{6,4},{8,10},{10,8},{12,14},{14,12},{16,18},{18,... | collective-permute-start | bytes 3145736 | tf_op jit(solution)/shard_map/ppermute | solution.py:97
  513.0 31.9 %collective-permute-start.54 = (bf16[4,2,32,2048]{3,2,1,0:T(8,128)(2,1)}, bf16[4,2,32,2048]{3,2,1,0:T(8,128)(2,1)}, u32[]{:S(2)}, u32[]{:S(2)}) collective-permute-start(bf16[4,2,32,2048]{3,2,1,0:T(8,128)(2,1)} %fusion.74), channel_id=1, source_target_pairs={{0,4},{2,6},{4,0},{6,2},{8,12},{10,14},{12,8},{14,10},{16,20},{18,... | collective-permute-start | bytes 3145736 | tf_op jit(solution)/shard_map/ppermute | solution.py:97
  540.0 36.6 %collective-permute-start.56 = (bf16[4,2,2,32,1536]{4,3,2,1,0:T(8,128)(2,1)}, bf16[4,2,2,32,1536]{4,3,2,1,0:T(8,128)(2,1)}, u32[]{:S(2)}, u32[]{:S(2)}) collective-permute-start(bf16[4,2,2,32,1536]{4,3,2,1,0:T(8,128)(2,1)} %get-tuple-element.165), channel_id=1, source_target_pairs={{0,1},{1,0},{2,3},{3,2},{4,5},{5,4},{6,7},{7,6},{8,9},{9,8},{10,11... | collective-permute-start | bytes 4718600 | tf_op jit(solution)/shard_map/ppermute | solution.py:100
  544.2 24.1 %collective-permute-start.59 = (bf16[4,32,2048]{2,1,0:T(8,128)(2,1)}, bf16[4,32,2048]{2,1,0:T(8,128)(2,1)}, u32[]{:S(2)}, u32[]{:S(2)}) collective-permute-start(bf16[4,32,2048]{2,1,0:T(8,128)(2,1)} %fusion.76), channel_id=1, source_target_pairs={{0,4},{2,6},{4,0},{6,2},{8,12},{10,14},{12,8},{14,10},{16,20},{18,... | collective-permute-start | bytes 1572872 | tf_op jit(solution)/shard_map/ppermute | solution.py:97
  547.1 26.0 %collective-permute-start.60 = (bf16[4,32,2048]{2,1,0:T(8,128)(2,1)}, bf16[4,32,2048]{2,1,0:T(8,128)(2,1)S(1)}, u32[]{:S(2)}, u32[]{:S(2)}) collective-permute-start(bf16[4,32,2048]{2,1,0:T(8,128)(2,1)} %fusion.75), channel_id=1, source_target_pairs={{0,2},{2,0},{4,6},{6,4},{8,10},{10,8},{12,14},{14,12},{16,18},{18,... | collective-permute-start | bytes 1572872 | tf_op jit(solution)/shard_map/ppermute | solution.py:97
  570.6 14.2 %collective-permute-start.108 = (bf16[32,2048]{1,0:T(8,128)(2,1)S(1)}, bf16[32,2048]{1,0:T(8,128)(2,1)S(1)}, u32[]{:S(2)}, u32[]{:S(2)}) collective-permute-start(bf16[32,2048]{1,0:T(8,128)(2,1)S(1)} %get-tuple-element.144), channel_id=1, source_target_pairs={{0,16},{2,18},{4,20},{6,22},{8,24},{10,26},{12,28},{14,30},{16,0},... | collective-permute-start | bytes 393224 | tf_op jit(solution)/shard_map/ppermute | solution.py:97
  571.2 13.9 %collective-permute-start.107 = (bf16[32,2048]{1,0:T(8,128)(2,1)S(1)}, bf16[32,2048]{1,0:T(8,128)(2,1)S(1)}, u32[]{:S(2)}, u32[]{:S(2)}) collective-permute-start(bf16[32,2048]{1,0:T(8,128)(2,1)S(1)} %get-tuple-element.145), channel_id=1, source_target_pairs={{0,8},{2,10},{4,12},{6,14},{8,16},{10,18},{12,20},{14,22},{16,24},... | collective-permute-start | bytes 393224 | tf_op jit(solution)/shard_map/ppermute | solution.py:97
  576.6 17.9 %collective-permute-start.111 = (bf16[32,2048]{1,0:T(8,128)(2,1)S(1)}, bf16[32,2048]{1,0:T(8,128)(2,1)S(1)}, u32[]{:S(2)}, u32[]{:S(2)}) collective-permute-start(bf16[32,2048]{1,0:T(8,128)(2,1)S(1)} %get-tuple-element.141), channel_id=1, source_target_pairs={{0,16},{2,18},{4,20},{6,22},{8,24},{10,26},{12,28},{14,30},{16,0},... | collective-permute-start | bytes 393224 | tf_op jit(solution)/shard_map/ppermute | solution.py:97
  587.7 34.5 %collective-permute-start.76 = (bf16[4,2,2,32,1536]{4,3,2,1,0:T(8,128)(2,1)S(1)}, bf16[4,2,2,32,1536]{4,3,2,1,0:T(8,128)(2,1)S(1)}, u32[]{:S(2)}, u32[]{:S(2)}) collective-permute-start(bf16[4,2,2,32,1536]{4,3,2,1,0:T(8,128)(2,1)S(1)} %get-tuple-element.163), channel_id=1, source_target_pairs={{0,1},{1,0},{2,3},{3,2},{4,5},{5,4},{6,7},{7,6},{8,9},{9,8},{10,11... | collective-permute-start | bytes 4718600 | tf_op jit(solution)/shard_map/ppermute | solution.py:100
  597.5 15.6 %collective-permute-start.92 = (bf16[4,32,768]{2,1,0:T(8,128)(2,1)S(1)}, bf16[4,32,768]{2,1,0:T(8,128)(2,1)S(1)}, u32[]{:S(2)}, u32[]{:S(2)}) collective-permute-start(bf16[4,32,768]{2,1,0:T(8,128)(2,1)S(1)} %fusion.98), channel_id=1, source_target_pairs={{0,2},{2,0},{4,6},{6,4},{8,10},{10,8},{12,14},{14,12},{16,18},{18,... | collective-permute-start | bytes 589832 | tf_op jit(solution)/shard_map/ppermute | solution.py:97
  625.2 25.0 %collective-permute-start.87 = (bf16[4,2,32,768]{3,2,1,0:T(8,128)(2,1)S(1)}, bf16[4,2,32,768]{3,2,1,0:T(8,128)(2,1)S(1)}, u32[]{:S(2)}, u32[]{:S(2)}) collective-permute-start(bf16[4,2,32,768]{3,2,1,0:T(8,128)(2,1)S(1)} %fusion.94), channel_id=1, source_target_pairs={{0,2},{2,0},{4,6},{6,4},{8,10},{10,8},{12,14},{14,12},{16,18},{18,... | collective-permute-start | bytes 1179656 | tf_op jit(solution)/shard_map/ppermute | solution.py:97
  626.9 24.7 %collective-permute-start.96 = (bf16[4,2,32,768]{3,2,1,0:T(8,128)(2,1)S(1)}, bf16[4,2,32,768]{3,2,1,0:T(8,128)(2,1)S(1)}, u32[]{:S(2)}, u32[]{:S(2)}) collective-permute-start(bf16[4,2,32,768]{3,2,1,0:T(8,128)(2,1)S(1)} %fusion.95), channel_id=1, source_target_pairs={{0,4},{2,6},{4,0},{6,2},{8,12},{10,14},{12,8},{14,10},{16,20},{18,... | collective-permute-start | bytes 1179656 | tf_op jit(solution)/shard_map/ppermute | solution.py:97
  646.2 23.2 %collective-permute-start.77 = (f32[2,256,1024]{2,1,0:T(8,128)S(1)}, f32[2,256,1024]{2,1,0:T(8,128)S(1)}, u32[]{:S(2)}, u32[]{:S(2)}) collective-permute-start(f32[2,256,1024]{2,1,0:T(8,128)S(1)} %get-tuple-element.153), channel_id=1, source_target_pairs={{0,1},{1,0},{2,3},{3,2},{4,5},{5,4},{6,7},{7,6},{8,9},{9,8},{10,11... | collective-permute-start | bytes 6291464 | tf_op jit(solution)/shard_map/ppermute | solution.py:100
  (175 other events, 2389.6 us)

commit v2 on v1

--- a/solution.py
+++ b/solution.py
@@ -57,15 +57,14 @@
     return (count, 1, 1)
 
 
-def rotation(dims, place, step):
+def rotation(dims, steps):
     pairs = []
     for a in range(dims[0]):
         for b in range(dims[1]):
             for c in range(dims[2]):
-                digits = [a, b, c]
+                up = [(d + s) % size for d, s, size in zip((a, b, c), steps, dims)]
                 source = (a * dims[1] + b) * dims[2] + c
-                digits[place] = (digits[place] + step) % dims[place]
-                pairs.append((source, (digits[0] * dims[1] + digits[1]) * dims[2] + digits[2]))
+                pairs.append((source, (up[0] * dims[1] + up[1]) * dims[2] + up[2]))
     return pairs
 
 
@@ -92,9 +91,12 @@
             row % self.dims[2],
         )
         self.seq = lax.axis_index("seq")
-
-    def turn(self, value, place, step):
-        return lax.ppermute(value, "rows", rotation(self.dims, place, step))
+        self.where = jnp.stack([*self.digits, self.seq]).astype(jnp.int32)
+
+        self.planes = [(y, x) for y in range(self.dims[1]) for x in range(self.dims[2])]
+
+    def turn(self, value, z, y, x):
+        return lax.ppermute(value, "rows", rotation(self.dims, (z, y, x)))
 
     def swap(self, value):
         return lax.ppermute(value, "seq", SWAP)
@@ -104,42 +106,53 @@
     return lax.optimization_barrier((values, hold))[0]
 
 
-def place_kernel(n_parts, dims, chunk, half):
+def spans(widths, low, high):
+    found, start = [], 0
+    for i, width in enumerate(widths):
+        a, b = max(low, start), min(high, start + width)
+        if a < b:
+            found.append((i, a - start, b - start, a))
+        start += width
+    return found
+
+
+def stack_kernel(*refs):
+    for i, ref in enumerate(refs[:-1]):
+        refs[-1][i] = ref[...]
+
+
+def place_kernel(n_parts, dims, chunk, widths):
     k0, k1, k2 = dims
+    planes = [(y, x) for y in range(k1) for x in range(k2)]
 
     def body(where, *refs):
-        parts, out = refs[:n_parts], refs[n_parts]
-        buf, sem_in, sem_out = refs[n_parts + 1 :]
+        parts, outs = refs[:n_parts], refs[n_parts : n_parts + len(widths)]
+        buf, sem_in, sem_out = refs[n_parts + len(widths) :]
         came = []
-        at = 0
         for other in (0, 1):
-            for colour in (0, 1):
-                outer, inner = ((1, 2), (2, 1))[colour]
-                for late in range(dims[outer]):
-                    part = parts[at]
-                    at += 1
-                    for mid in range(dims[inner]):
-                        for top in range(k0):
-                            rel = [0, 0, 0]
-                            rel[0], rel[inner], rel[outer] = top, mid, late
-                            spot = [
-                                lax.rem(where[i] - rel[i] + dims[i], dims[i]) for i in range(3)
-                            ]
-                            seat = lax.rem(where[3] + other, 2)
-                            block = ((spot[0] * k1 + spot[1]) * k2 + spot[2]) * 2 + seat
-                            start = pl.multiple_of(block * chunk, chunk)
-                            span = (pl.ds(start, chunk), pl.ds(colour * half, half))
-                            copy = pltpu.make_async_copy(
-                                part.at[mid * k0 + top], buf.at[span], sem_in.at[len(came)]
-                            )
-                            copy.start()
-                            came.append((copy, span))
+            for i, (y, x) in enumerate(planes):
+                part = parts[other * len(planes) + i]
+                for z in range(k0):
+                    spot = [
+                        lax.rem(where[j] - r + dims[j], dims[j]) for j, r in enumerate((z, y, x))
+                    ]
+                    seat = lax.rem(where[3] + other, 2)
+                    block = ((spot[0] * k1 + spot[1]) * k2 + spot[2]) * 2 + seat
+                    rows = pl.ds(pl.multiple_of(block * chunk, chunk), chunk)
+                    copy = pltpu.make_async_copy(part.at[z], buf.at[rows], sem_in.at[len(came)])
+                    copy.start()
+                    came.append((copy, rows))
         went = []
-        for copy, span in came:
+        for copy, rows in came:
             copy.wait()
-            back = pltpu.make_async_copy(buf.at[span], out.at[span], sem_out.at[len(went)])
-            back.start()
-            went.append(back)
+            start = 0
+            for out, width in zip(outs, widths):
+                back = pltpu.make_async_copy(
+                    buf.at[rows, pl.ds(start, width)], out.at[rows], sem_out.at[len(went)]
+                )
+                back.start()
+                went.append(back)
+                start += width
         for back in went:
             back.wait()
 
@@ -147,13 +160,15 @@
 
 
 class Gather:
-    def __init__(self, wires, shard):
-        self.wires, self.shard = wires, shard
-        m, n = shard.shape
-        self.plain = bool(m % 32 or n % 256)
-        self.half = n // 2
-        self.flight, self.held, self.sends = (), (), ()
+    def __init__(self, wires, shards):
+        self.wires, self.shards = wires, shards
+        self.widths = [s.shape[1] for s in shards]
+        m, n = shards[0].shape[0], sum(self.widths)
+        self.plain = bool(m % 32 or n % 128)
+        self.flight, self.sends = (), ()
         self.stage = 0
+        if not self.plain:
+            self.shard = jnp.concatenate(shards, axis=1) if len(shards) > 1 else shards[0]
 
     def step(self, after=()):
         if self.plain:
@@ -161,71 +176,50 @@
         wires, stage = self.wires, self.stage
         self.stage += 1
         if stage == 0:
-            shard = gate(self.shard, after) if after else self.shard
-            self.flight = [wires.turn(shard, 0, r) for r in range(1, wires.dims[0])]
-            return
-        pairs = ((1, 2), (2, 1))
-        if stage == 1:
-            tops = [self.shard] + list(self.flight)
-            cuts = [
-                jnp.stack([t[:, c * self.half : (c + 1) * self.half] for t in tops])
-                for c in (0, 1)
-            ]
+            sends = [self.shard]
+        elif stage == 1:
+            tops = [self.shard, *self.flight]
+            out = jax.ShapeDtypeStruct((len(tops), *self.shard.shape), self.shard.dtype)
+            sends = [pl.pallas_call(stack_kernel, out_shape=out, name="stack")(*tops)]
         else:
-            cuts = self.held
+            sends = [self.held, *self.flight]
         if after:
-            cuts = gate(cuts, after)
-        if stage == 1:
-            self.held = self.sends = cuts
-            self.got = [
-                [wires.turn(cuts[c], pairs[c][1], r) for r in range(1, wires.dims[pairs[c][1]])]
-                for c in (0, 1)
-            ]
-            self.flight = self.got[0] + self.got[1]
-        elif stage == 2:
-            mids = [jnp.concatenate([cuts[c]] + self.got[c], axis=0) for c in (0, 1)]
-            if after:
-                mids = gate(mids, after)
-            lists = [
-                [wires.turn(mids[c], pairs[c][0], r) for r in range(1, wires.dims[pairs[c][0]])]
-                for c in (0, 1)
-            ]
-            self.held, self.sends = (mids, lists), mids
-            self.flight = lists[0] + lists[1]
-        elif stage == 3:
-            mids, lists = cuts
-            own = [mids[0]] + lists[0] + [mids[1]] + lists[1]
-            self.flight = [wires.swap(p) for p in own]
-            self.held = own
+            sends = gate(sends, after)
+        if stage == 0:
+            self.flight = [wires.turn(sends[0], r, 0, 0) for r in range(1, wires.dims[0])]
+        elif stage == 1:
+            (self.held,) = sends
+            self.flight = [wires.turn(sends[0], 0, y, x) for y, x in wires.planes[1:]]
+        else:
+            self.held = sends
+            self.flight = [wires.swap(p) for p in sends]
+        self.sends = sends
 
     def result(self):
-        wires, shard = self.wires, self.shard
+        wires = self.wires
         if self.plain:
-            return lax.all_gather(shard, ("rows", "seq"), axis=0, tiled=True)
-        m, n = shard.shape
-        parts = list(self.held) + list(self.flight)
-        where = jnp.stack([*wires.digits, wires.seq]).astype(jnp.int32)
+            both = ("rows", "seq")
+            return [lax.all_gather(s, both, axis=0, tiled=True) for s in self.shards]
+        m, n = self.shard.shape
+        kind = self.shard.dtype
+        parts = [*self.held, *self.flight]
         total = wires.count * 2
         return pl.pallas_call(
-            place_kernel(len(parts), wires.dims, m, self.half),
-            out_shape=jax.ShapeDtypeStruct((m * total, n), shard.dtype),
+            place_kernel(len(parts), wires.dims, m, self.widths),
+            out_shape=[jax.ShapeDtypeStruct((m * total, w), kind) for w in self.widths],
             grid_spec=pltpu.PrefetchScalarGridSpec(
                 num_scalar_prefetch=1,
                 grid=(1,),
                 in_specs=[pl.BlockSpec(memory_space=pl.ANY)] * len(parts),
-                out_specs=pl.BlockSpec(memory_space=pl.ANY),
+                out_specs=[pl.BlockSpec(memory_space=pl.ANY)] * len(self.widths),
                 scratch_shapes=[
-                    pltpu.VMEM((m * total, n), shard.dtype),
-                    pltpu.SemaphoreType.DMA((2 * total,)),
-                    pltpu.SemaphoreType.DMA((2 * total,)),
+                    pltpu.VMEM((m * total, n), kind),
+                    pltpu.SemaphoreType.DMA((total,)),
+                    pltpu.SemaphoreType.DMA((len(self.widths) * total,)),
                 ],
             ),
             name="place",
-        )(where, *parts)
-
-
-def pick(value, index, axis):
-    return lax.dynamic_index_in_dim(value, index, axis, keepdims=False)
+        )(wires.where, *parts)
 
 
 def total_of(terms):
@@ -233,58 +227,126 @@
     return sum(wide[1:], wide[0])
 
 
+def halves(wires, values):
+    width = values.shape[1]
+    m = width // (wires.count * 2)
+    column = jnp.arange(width, dtype=jnp.int32)
+    inside = column % (width // 2)
+    seat = jnp.where(column < width // 2, wires.seq, 1 - wires.seq)
+    source = (inside // m * 2 + seat) * m + inside % m
+    chosen = (jnp.arange(width, dtype=jnp.int32)[:, None] == source[None, :]).astype(BF)
+    both = dot_plain(values, chosen).astype(BF)
+    return both[:, : width // 2], both[:, width // 2 :]
+
+
+def inner_fold_kernel(dims, widths):
+    n = len(widths)
+
+    def body(where, *refs):
+        for at, (up, right) in enumerate(
+            (a, b) for a in range(dims[1]) for b in range(dims[2])
+        ):
+            y = lax.rem(where[1] + up, dims[1])
+            x = lax.rem(where[2] + right, dims[2])
+            start = 0
+            for i, width in enumerate(widths):
+                kept, came = refs[i][0, y, x], refs[n + i][0, y, x]
+                refs[2 * n + at][0, :, start : start + width] = kept + came
+                start += width
+
+    return body
+
+
+def outer_fold_kernel(dims, n):
+    def body(where, *refs):
+        for step in range(dims[0]):
+            spot = lax.rem(where[0] + step, dims[0])
+            refs[n + step][...] = total_of([r[spot] for r in refs[:n]]).astype(BF)
+
+    return body
+
+
 class Scatter:
-    def __init__(self, wires, grad):
-        self.wires, self.grad = wires, grad
-        d, n = grad.shape
-        self.m = d // (wires.count * 2)
-        self.plain = bool(self.m % 32 or n % 256)
-        self.half = n // 2
+    def __init__(self, wires, products):
+        self.wires = wires
+        self.widths = [p[3].shape[1] for p in products]
+        self.m = products[0][0].shape[1] // (wires.count * 2)
+        self.plain = bool(self.m % 32 or sum(self.widths) % 128)
         self.stage = 0
         self.sends = ()
-        self.flight = ()
-
-    def fold(self, terms, place, axis):
-        wires = self.wires
-        size, spot = wires.dims[place], wires.digits[place]
-        kept = [pick(t, spot, axis) for t in terms]
-        away, got = [], []
-        for step in range(1, size):
-            index = lax.rem(spot + step, size)
-            send = total_of([pick(t, index, axis) for t in terms]).astype(BF)
-            away.append(send)
-            got.append(wires.turn(send, place, step))
-        return away, kept, got
+        if self.plain:
+            self.whole = [dot_first(p[0], p[3]) for p in products]
+            return
+        shape = (*wires.dims, self.m)
+        self.sends = [
+            dot_first(p[2], p[3]).astype(BF).reshape(*shape, p[3].shape[1]) for p in products
+        ]
+        right = gate([p[3] for p in products], self.sends)
+        self.kept = [
+            dot_first(p[1], r).astype(BF).reshape(*shape, r.shape[1])
+            for p, r in zip(products, right)
+        ]
+        self.got = [wires.swap(s) for s in self.sends]
+
+    def call(self, body, grid, in_specs, out_specs, out_shape, args, name):
+        return pl.pallas_call(
+            body,
+            out_shape=out_shape,
+            grid_spec=pltpu.PrefetchScalarGridSpec(
+                num_scalar_prefetch=1, grid=grid, in_specs=in_specs, out_specs=out_specs
+            ),
+            name=name,
+        )(self.wires.where, *args)
 
     def step(self):
         if self.plain:
             return
-        wires, stage = self.wires, self.stage
+        wires, stage, m = self.wires, self.stage, self.m
+        dims = wires.dims
+        k0, k1, k2 = dims
         self.stage += 1
+        n = sum(self.widths)
         if stage == 0:
-            d, n = self.grad.shape
-            cut = self.grad.reshape(*wires.dims, 2, self.m, n)
-            send = pick(cut, 1 - wires.seq, 3).astype(BF)
-            got = wires.swap(send)
-            self.sends, self.flight = [send], [got]
-            base = [pick(cut, wires.seq, 3), got]
-            half = self.half
-            self.terms = [[t[..., c * half : (c + 1) * half] for t in base] for c in (0, 1)]
-            return
-        places = (((2, 2), (1, 1), (0, 0)), ((1, 1), (2, 1), (0, 0)))
-        self.sends, self.flight, terms = [], [], []
-        for c in (0, 1):
-            away, kept, got = self.fold(self.terms[c], *places[c][stage - 1])
-            self.sends += away
-            self.flight += got
-            terms.append(kept + got)
-        self.terms = terms
+            outs = self.call(
+                inner_fold_kernel(dims, self.widths),
+                (k0,),
+                [pl.BlockSpec((1, k1, k2, m, w), lambda z, p: (z, 0, 0, 0, 0)) for w in self.widths]
+                * 2,
+                [pl.BlockSpec((1, m, n), lambda z, p: (z, 0, 0))] * (k1 * k2),
+                [jax.ShapeDtypeStruct((k0, m, n), BF)] * (k1 * k2),
+                [*self.kept, *self.got],
+                "fold_inner",
+            )
+            self.sends = outs[1:]
+            self.terms = [outs[0]] + [
+                wires.turn(o, 0, y, x) for o, (y, x) in zip(outs[1:], wires.planes[1:])
+            ]
+        elif stage == 1:
+            outs = self.call(
+                outer_fold_kernel(dims, len(self.terms)),
+                (1,),
+                [pl.BlockSpec((k0, m, n), lambda z, p: (0, 0, 0))] * len(self.terms),
+                [pl.BlockSpec((m, n), lambda z, p: (0, 0))] * k0,
+                [jax.ShapeDtypeStruct((m, n), BF)] * k0,
+                self.terms,
+                "fold_outer",
+            )
+            self.sends = outs[1:]
+            self.terms = [outs[0]] + [wires.turn(outs[r], r, 0, 0) for r in range(1, k0)]
 
     def result(self):
         if self.plain:
             both = ("rows", "seq")
-            return lax.psum_scatter(self.grad.astype(F32), both, scatter_dimension=0, tiled=True)
-        return jnp.concatenate([total_of(t) for t in self.terms], axis=1)
+            return [lax.psum_scatter(g, both, scatter_dimension=0, tiled=True) for g in self.whole]
+        done, outs, start = total_of(self.terms), [], 0
+        for w in self.widths:
+            outs.append(done[:, start : start + w])
+            start += w
+        return outs
+
+
+def pick(value, index, axis):
+    return lax.dynamic_index_in_dim(value, index, axis, keepdims=False)
 
 
 def sum_everywhere(wires, value):
@@ -399,8 +461,90 @@
     )(segments[:, :, None], segments[:, None, :], joined, joined, joined, logs, grad_mixed)
 
 
-def exact_gelu(values):
-    return jax.nn.gelu(values, approximate=False)
+ERF_TOP = (
+    0.00022905065861350646,
+    0.0034082910107109506,
+    0.050955695062380861,
+    0.18520832239976145,
+    1.128379143519084,
+)
+ERF_LOW = (
+    -1.1791602954361697e-7,
+    0.000023547966471313185,
+    0.0010179625278914885,
+    0.014070470171167667,
+    0.11098505178285362,
+    0.49746925110067538,
+    1.0,
+)
+ROOT_HALF = 0.7071067811865476
+ERF_LIMIT = 3.832506856900711 / ROOT_HALF
+
+
+def polynomial(coefficients, value, outer):
+    last = len(coefficients) - 1
+    scaled = [c * outer * 0.5 ** (last - i) for i, c in enumerate(coefficients)]
+    total = jnp.full_like(value, scaled[0])
+    for c in scaled[1:]:
+        total = total * value + c
+    return total
+
+
+def gelu_both(values):
+    kept = jnp.clip(values, -ERF_LIMIT, ERF_LIMIT)
+    square = kept * kept
+    top = kept * polynomial(ERF_TOP, square, 0.5 * ROOT_HALF)
+    phi = 0.5 + top / polynomial(ERF_LOW, square, 1.0)
+    density = jnp.exp2(values * values * -0.7213475204444817 - 1.3257480647361593)
+    return values * phi, phi + values * density
+
+
+def widen_kernel(tile, chunk):
+    def body(where, x_ref, w_ref, shift_ref, act_ref, slope_ref, stay_ref, go_ref):
+        first = where[3] == 0
+        for start in range(0, x_ref.shape[0], tile):
+            rows = slice(start, start + tile)
+            hidden = dot_plain(x_ref[rows, :], w_ref[...]) + shift_ref[...]
+            act, slope = gelu_both(hidden)
+            act = act.astype(BF)
+            act_ref[rows, :] = act
+            slope_ref[rows, :] = slope.astype(BF)
+            for i in range(act.shape[1] // (2 * chunk)):
+                even = act[:, 2 * i * chunk : (2 * i + 1) * chunk]
+                odd = act[:, (2 * i + 1) * chunk : (2 * i + 2) * chunk]
+                span = slice(i * chunk, (i + 1) * chunk)
+                stay_ref[rows, span] = jnp.where(first, even, odd)
+                go_ref[rows, span] = jnp.where(first, odd, even)
+
+    return body
+
+
+def widen(wires, values, weight, shift):
+    count, width = values.shape
+    ff = weight.shape[1]
+    chunk = ff // (wires.count * 2)
+    cols = 512
+
+    def block(size):
+        return pl.BlockSpec((count, size), lambda j, p: (0, j))
+
+    out = jax.ShapeDtypeStruct((count, ff), BF)
+    part = jax.ShapeDtypeStruct((count, ff // 2), BF)
+    return pl.pallas_call(
+        widen_kernel(128, chunk),
+        out_shape=[out, out, part, part],
+        grid_spec=pltpu.PrefetchScalarGridSpec(
+            num_scalar_prefetch=1,
+            grid=(ff // cols,),
+            in_specs=[
+                pl.BlockSpec((count, width), lambda j, p: (0, 0)),
+                pl.BlockSpec((width, cols), lambda j, p: (0, j)),
+                pl.BlockSpec((1, cols), lambda j, p: (0, j)),
+            ],
+            out_specs=[block(cols), block(cols), block(cols // 2), block(cols // 2)],
+        ),
+        name="widen",
+    )(wires.where, values, weight, shift[None])
 
 
 def shards(
@@ -455,9 +599,7 @@
     )
     n_small = small.shape[0]
     pad_cols = 256
-    riding = jnp.concatenate(
-        [qkv_weight, jnp.pad(small.T, ((0, 0), (0, pad_cols - n_small)))], axis=1
-    )
+    small_cols = jnp.pad(small.T, ((0, 0), (0, pad_cols - n_small)))
 
     def other_rows(value):
         return lax.dynamic_slice_in_dim(value, (1 - seq) * rows_here, rows_here, 0)
@@ -471,22 +613,17 @@
     second = jnp.where(seq == 0, came, mine)
     inputs_low = jnp.concatenate([first, second], axis=1).reshape(count_tok, width)
     grad_came = wires.swap(out_grad)
-    ga, gb, gc, gd = [Gather(wires, w) for w in (riding, out_weight, fc1_weight, fc2_weight)]
+    ga = Gather(wires, [qkv_weight, small_cols])
+    gc = Gather(wires, [out_weight, fc1_weight])
+    gd = Gather(wires, [fc2_weight])
     ga.step()
-    top_a = ga.flight
-    ga.step()
-    gb.step(top_a)
-    gc.step(gb.flight)
-    mid_a = ga.flight
+    gc.step(ga.flight)
     ga.step()
     gd.step(gc.flight)
-    gb.step(mid_a)
-    late_a = ga.flight
-    ga.step()
-    gb.step(late_a)
-    qkv_all = ga.result()
-    qkv_full = qkv_all[:, : 3 * width]
-    small_full = qkv_all[:, 3 * width : 3 * width + 128].T[:n_small].astype(F32)
+    gc.step(ga.sends)
+    ga.step(gc.sends)
+    qkv_full, small_all = ga.result()
+    small_full = small_all[:, :128].T[:n_small].astype(F32)
     norm1_gain, norm1_shift, q_shift, v_shift, out_shift, norm2_gain, norm2_shift, fc2_shift = [
         small_full[i] for i in range(8)
     ]
@@ -502,28 +639,17 @@
     joined_shift = jnp.concatenate([q_shift, jnp.zeros_like(q_shift), v_shift])
     joined = (qkv_out + joined_shift).astype(BF)
     pairs = width // (4 * HEAD_DIM)
-    gb.step()
-    gc.step(gb.flight)
-    joined = gate(joined, gc.sends)
-    mixed_a, logs_a = attend(joined, seg, 0, pairs)
-    out_full = gb.result()
-    gc.step((mixed_a,))
-    joined_b = gate(joined, (gc.sends, mixed_a))
-    mixed_b, logs_b = attend(joined_b, seg, pairs, pairs)
-    mixed = jnp.concatenate([mixed_a, mixed_b], axis=1)
+    mixed, logs = attend(joined, seg, 0, 2 * pairs)
+    gc.step((mixed,))
+    gd.step(gc.sends)
+    out_full, fc1_full = gc.result()
+    mixed = gate(mixed, gd.sends)
     resid1 = inputs + dot_plain(mixed, out_full) + out_shift
     normed2, inverse2 = norm_stats(resid1)
     mlp_in = (normed2 * norm2_gain + norm2_shift).astype(BF)
-    gc.step()
-    gd.step(gc.flight)
-    fc1_full = gc.result()
-    fc1_full = gate(fc1_full, gd.sends)
-    hidden = dot_plain(mlp_in, fc1_full) + fc1_shift
-    gd.step()
-    gd.step()
-    fc2_full = gd.result()
-    activated, gelu_back = jax.vjp(exact_gelu, hidden)
-    activated_low = activated.astype(BF)
+    activated_low, slope, act_stay, act_go = widen(wires, mlp_in, fc1_full, fc1_shift)
+    gd.step((slope,))
+    (fc2_full,) = gd.result()
     resid2 = resid1 + dot_plain(activated_low, fc2_full) + fc2_shift
 
     learn_scale = learn_gain.astype(F32)
@@ -573,16 +699,14 @@
     )
     grad_resid2 = grad_resid2 + back_three
     grad_branch2 = grad_resid2.astype(BF)
-    s_fc2 = Scatter(wires, dot_first(activated_low, grad_branch2).astype(BF))
-    s_fc2.step()
+    s_fc2 = Scatter(wires, [(activated_low, act_stay, act_go, grad_branch2)])
     grad_branch2 = gate(grad_branch2, s_fc2.sends)
     grad_fc2_shift = jnp.sum(grad_branch2.astype(F32), axis=0)
     grad_activ = dot_second(grad_branch2, fc2_full).astype(BF)
-    grad_hidden = gelu_back(grad_activ.astype(F32))[0].astype(BF)
+    grad_hidden = (grad_activ.astype(F32) * slope.astype(F32)).astype(BF)
     s_fc2.step()
     grad_hidden = gate(grad_hidden, s_fc2.sends)
-    s_fc1 = Scatter(wires, dot_first(mlp_in, grad_hidden).astype(BF))
-    s_fc1.step()
+    s_fc1 = Scatter(wires, [(mlp_in, *halves(wires, mlp_in), grad_hidden)])
     grad_hidden = gate(grad_hidden, s_fc1.sends)
     grad_fc1_shift = jnp.sum(grad_hidden.astype(F32), axis=0)
     grad_normed2 = dot_second(grad_hidden, fc1_full)
@@ -591,26 +715,60 @@
     )
     grad_resid1 = grad_resid2 + back_two
     grad_branch1 = grad_resid1.astype(BF)
+    s_fc1.step()
     s_fc2.step()
-    grad_branch1 = gate(grad_branch1, s_fc2.sends)
-    s_out = Scatter(wires, dot_first(mixed, grad_branch1).astype(BF))
-    s_out.step()
+    grad_branch1 = gate(grad_branch1, (s_fc1.sends, s_fc2.sends))
+    s_out = Scatter(wires, [(mixed, *halves(wires, mixed), grad_branch1)])
     grad_out_shift = jnp.sum(grad_branch1.astype(F32), axis=0)
     grad_branch1 = gate(grad_branch1, s_out.sends)
     grad_mixed = dot_second(grad_branch1, out_full).astype(BF)
+    s_out.step()
+    grad_mixed = gate(grad_mixed, s_out.sends)
+    dq_a, dk_a, dv_a = attend_back(joined, logs[:, :pairs], grad_mixed, seg, 0, pairs)
+    grad_a = jnp.concatenate([dq_a, dk_a, dv_a], axis=1)
+    attn_stay, attn_go = halves(wires, attn_in)
+    s_a = Scatter(wires, [(attn_in, attn_stay, attn_go, grad_a)])
     s_fc1.step()
-    s_fc2.step()
-    grad_mixed = gate(grad_mixed, (s_fc1.sends, s_fc2.sends))
-    early = jnp.concatenate(
+    grad_mixed = gate(grad_mixed, (s_a.sends, s_fc1.sends))
+    dq_b, dk_b, dv_b = attend_back(joined, logs[:, pairs:], grad_mixed, seg, pairs, pairs)
+    grad_b = jnp.concatenate([dq_b, dk_b, dv_b], axis=1)
+    s_a.step()
+    s_out.step()
+    (done_fc2,) = s_fc2.result()
+    grad_b = gate(grad_b, (s_a.sends, s_out.sends, done_fc2))
+    s_b = Scatter(wires, [(attn_in, attn_stay, attn_go, grad_b)])
+    grad_a, grad_b = gate((grad_a, grad_b), s_b.sends)
+    half = pairs * 2 * HEAD_DIM
+    cuts = [slice(i * width + c * half, i * width + (c + 1) * half) for c in (0, 1) for i in range(3)]
+    grad_normed1 = sum(
+        dot_second(g, jnp.concatenate([qkv_full[:, c] for c in cuts[3 * i : 3 * i + 3]], axis=1))
+        for i, g in enumerate((grad_a, grad_b))
+    )
+    s_b.step()
+    grad_normed1 = gate(grad_normed1, s_b.sends)
+    back_one, grad_norm1_gain, grad_norm1_shift = norm_backward(
+        grad_normed1, normed1, inverse1, norm1_gain
+    )
+    sum_q, sum_v = [
+        jnp.concatenate(
+            [jnp.sum(g[:, i * half : (i + 1) * half].astype(F32), axis=0) for g in (grad_a, grad_b)]
+        )
+        for i in (0, 2)
+    ]
+    little = jnp.concatenate(
         [
             jnp.stack(
                 [
-                    grad_learn_gain,
-                    grad_learn_bias,
+                    grad_norm1_gain,
+                    grad_norm1_shift,
+                    sum_q,
+                    sum_v,
                     grad_out_shift,
                     grad_norm2_gain,
                     grad_norm2_shift,
                     grad_fc2_shift,
+                    grad_learn_gain,
+                    grad_learn_bias,
                     jnp.pad(grad_maps_bias, (0, width - NTOK)),
                 ]
             ),
@@ -619,57 +777,18 @@
         ],
         axis=0,
     )
-    early = sum_everywhere(wires, jnp.pad(early, ((0, -early.shape[0] % 8), (0, 0))))
-    dq_a, dk_a, dv_a = attend_back(joined, logs_a, grad_mixed, seg, 0, pairs)
-    grad_a = jnp.concatenate([dq_a, dk_a, dv_a], axis=1)
-    s_a = Scatter(wires, dot_first(attn_in, grad_a).astype(BF))
-    s_a.step()
-    s_fc1.step()
-    s_out.step()
-    grad_mixed = gate(grad_mixed, (s_a.sends, s_fc1.sends, s_out.sends))
-    dq_b, dk_b, dv_b = attend_back(joined, logs_b, grad_mixed, seg, pairs, pairs)
-    grad_b = jnp.concatenate([dq_b, dk_b, dv_b], axis=1)
-    s_a.step()
-    s_out.step()
-    s_fc1.step()
-    done_fc2 = s_fc2.result()
-    grad_b = gate(grad_b, (s_a.sends, s_out.sends, s_fc1.sends, done_fc2))
-    s_b = Scatter(wires, dot_first(attn_in, grad_b).astype(BF))
-    s_b.step()
-    s_a.step()
-    s_out.step()
-    grad_a, grad_b = gate((grad_a, grad_b), (s_a.sends, s_out.sends, s_b.sends, early))
-    half = pairs * 2 * HEAD_DIM
-    cuts = [slice(i * width + c * half, i * width + (c + 1) * half) for c in (0, 1) for i in range(3)]
-    grad_normed1 = sum(
-        dot_second(g, jnp.concatenate([qkv_full[:, c] for c in cuts[3 * i : 3 * i + 3]], axis=1))
-        for i, g in enumerate((grad_a, grad_b))
-    )
-    s_b.step()
-    grad_normed1 = gate(grad_normed1, s_b.sends)
-    back_one, grad_norm1_gain, grad_norm1_shift = norm_backward(
-        grad_normed1, normed1, inverse1, norm1_gain
-    )
-    sum_q, sum_v = [
-        jnp.concatenate(
-            [jnp.sum(g[:, i * half : (i + 1) * half].astype(F32), axis=0) for g in (grad_a, grad_b)]
-        )
-        for i in (0, 2)
-    ]
-    late = jnp.stack([grad_norm1_gain, grad_norm1_shift, sum_q, sum_v])
-    late = sum_everywhere(wires, jnp.pad(late, ((0, 4), (0, 0))))
+    little = sum_everywhere(wires, jnp.pad(little, ((0, -little.shape[0] % 8), (0, 0))))
     s_a.step()
     s_b.step()
-    s_b.step()
-    done_a, done_b = s_a.result(), s_b.result()
-    done_out, done_fc1 = s_out.result(), s_fc1.result()
+    (done_a,), (done_b,) = s_a.result(), s_b.result()
+    (done_fc1,), (done_out,) = s_fc1.result(), s_out.result()
     done_qkv = jnp.concatenate(
         [d[:, i * half : (i + 1) * half] for i in range(3) for d in (done_a, done_b)], axis=1
     )
     place = lax.axis_index("rows") * 2 + seq
-    held = lax.dynamic_slice_in_dim(jnp.concatenate([early[2:6], late[:4]]), place * m, m, 1)
+    held = lax.dynamic_slice_in_dim(little[:8], place * m, m, 1)
     held_fc1 = lax.dynamic_slice_in_dim(
-        early[7 + NTOK : 7 + NTOK + wide].reshape(ff), place * wide * m, wide * m, 0
+        little[11 + NTOK : 11 + NTOK + wide].reshape(ff), place * wide * m, wide * m, 0
     )
     grad_rows = (grad_resid1 + back_one).reshape(rows_here, row_len, width)
     grad_away = lax.dynamic_slice_in_dim(grad_rows, (1 - seq) * slots_half, slots_half, 1)
@@ -683,22 +802,22 @@
     return (
         pooled,
         grad_held,
+        held[0],
+        held[1],
+        done_qkv,
+        held[2:4],
+        done_out,
         held[4],
         held[5],
-        done_qkv,
-        held[6:8],
-        done_out,
-        held[0],
-        held[1],
-        held[2],
+        held[6],
         done_fc1,
         held_fc1,
         done_fc2,
-        held[3],
-        early[0],
-        early[1],
-        early[7 : 7 + NTOK],
-        early[6, :NTOK],
+        held[7],
+        little[8],
+        little[9],
+        little[11 : 11 + NTOK],
+        little[10, :NTOK],
     )
 
 

time: 676 us -> 610 us (0.902)
  Pallas kernels: 89.8 us -> 165 us
  local copies, waits for them, and re-layouts: 94.3 us -> 44.5 us
  waiting for transfers between devices: 137 us -> 109 us
  other arithmetic: 67.4 us -> 42.6 us
  matrix products: 178 us -> 154 us
  starting transfers between devices: 103 us -> 82.4 us
    pallas_call x4 -> x17, Pallas kernels: 28.1 us -> 105 us  [the longest x10 43.6 us: call(): pl.pallas_call(body, out_shape=out_shape, grid_spec=pltpu.PrefetchScalarG...]
    dot_general x7 -> x9, matrix products: 86.2 us -> 47.8 us  [dot_plain(): return jnp.dot(a, b, precision=precision, preferred_element_type=F32)]
    ppermute x8 -> x4, waiting for transfers between devices: 39.8 us -> 17.4 us  [sum_everywhere(): lax.ppermute(value, 'rows', crossing(wires.dims, place, step))]
    ppermute x78 -> x48, starting transfers between devices: 92.4 us -> 71.8 us  [turn(): return lax.ppermute(value, 'rows', rotation(self.dims, (z, y, x)))]
    convert_element_type x31 -> x2, other arithmetic: 20.5 us -> 2.08 us  [the longest x1 2.04 us: shards(): mlp_in = (normed2 * norm2_gain + norm2_shift).astype(BF)]
    dot_general x8 -> x13, matrix products: 41.1 us -> 59.3 us  [dot_first(): lax.dot_general(a, b, (((0,), (0,)), ((), ())), precision=precision, pref...]
    squeeze x6 -> x1, local copies, waits for them, and re-layouts: 15.1 us -> 0.78 us  [pick(): return lax.dynamic_index_in_dim(value, index, axis, keepdims=False)]
    slice x13 -> x4, local copies, waits for them, and re-layouts: 15.7 us -> 2.42 us  [the longest x1 0.63 us: shards(): logs[:, pairs:]]
  transfers between devices with their start and end apart: 113 -> 74, of which waited for: 41 -> 24; matrix products, arithmetic and copies ran while one was open for 40% -> 30% of each run, Pallas kernels for 12% -> 22%
where the time goes in v2:
time: 610 us; the launch traced here: 600 us
  Pallas kernels  165 us (27%)
  matrix products  154 us (25%)
  waiting for transfers between devices  109 us (18%)
  starting transfers between devices  82.4 us (14%)
  local copies, waits for them, and re-layouts  44.5 us (7%)
  other arithmetic  42.6 us (7%)
    ppermute x48, waiting for transfers between devices, turn(): return lax.ppermute(value, 'rows', rotation(self.dims, (z, y, x)))  90.7 us
    ppermute x48, starting transfers between devices, turn(): return lax.ppermute(value, 'rows', rotation(self.dims, (z, y, x)))  71.8 us
    dot_general x13, matrix products, dot_first(): lax.dot_general(a, b, (((0,), (0,)), ((), ())), precision=precision, pref...  59.3 us
    dot_general x9, matrix products, dot_plain(): return jnp.dot(a, b, precision=precision, preferred_element_type=F32)  47.8 us
    dot_general x7, matrix products, dot_second(): lax.dot_general(a, b, (((1,), (1,)), ((), ())), precision=precision, pref...  46.8 us
    pallas_call x10, Pallas kernels, call(): pl.pallas_call(body, out_shape=out_shape, grid_spec=pltpu.PrefetchScalarG...  43.6 us
    pallas_call x2, Pallas kernels, attend_back(): pl.pallas_call(attend_back_kernel, grid=(rows, pairs), in_specs=[pl.Block...  35.1 us
    pallas_call x1, Pallas kernels, widen(): pl.pallas_call(widen_kernel(128, chunk), out_shape=[out, out, part, part]...  30.7 us
  transfers between devices with their start and end apart: 74, of which 24 were waited for; matrix products, arithmetic and copies ran while one was open for 30% of the time, Pallas kernels for 22%

profile of v2, /device:TPU:0, one launch (start us, length us, event | category | flops | bytes accessed | tf_op | source)
XLA Modules:
  0.0 600.2 jit_solution(14477330376084623102)
XLA Ops:
  27.7 5.0 collective-permute-start.7
  42.6 14.0 %collective-permute-done.8.refs_2_ = bf16[32,5120]{1,0:T(8,128)(2,1)S(1)} collective-permute-done((bf16[32,5120]{1,0:T(8,128)(2,1)S(1)}, bf16[32,5120]{1,0:T(8,128)(2,1)S(1)}, u32[]{:S(2)}, u32[]{:S(2)}) %collective-permute-start.8) | collective-permute-done | bytes 327712 | tf_op jit(solution)/shard_map/ppermute | solution.py:99
  68.8 5.6 collective-permute-done.5.refs_2_
  85.9 7.0 %place.3 = (bf16[1024,3072]{1,0:T(8,128)(2,1)}, bf16[1024,256]{1,0:T(8,128)(2,1)}) custom-call(s32[4]{0:T(128)} %pad_add_fusion.where, bf16[4,32,3328]{2,1,0:T(8,128)(2,1)} %stack.67.refs_0_, bf16[4,32,3328]{2,1,0:T(8,128)(2,1)} %collective-permute-done.4.refs_1_, bf16[4,32,3328]{2,1,0:T(8,128)(2,1)} %collective-permute-done.5.refs_2_, ...), custom_call_target="tpu_custom_call" | custom-call | tf_op jit(solution)/shard_map/place/pallas_call | solution.py:207
  97.3 6.3 %collective-permute-done.17.refs_1_ = bf16[4,32,5120]{2,1,0:T(8,128)(2,1)} collective-permute-done((bf16[4,32,5120]{2,1,0:T(8,128)(2,1)}, bf16[4,32,5120]{2,1,0:T(8,128)(2,1)}, u32[]{:S(2)}, u32[]{:S(2)}) %collective-permute-start.17) | collective-permute-done | bytes 1310752 | tf_op jit(solution)/shard_map/ppermute | solution.py:99
  104.6 8.5 %add_convert_fusion.q_ref.k_ref.v_ref = bf16[1024,3072]{1,0:T(8,128)(2,1)} fusion(f32[3072]{0:T(1024)S(1)} %pad_maximum_fusion.2, bf16[1024,1024]{1,0:T(8,128)(2,1)S(1)} %fusion.11, bf16[1024,3072]{1,0:T(8,128)(2,1)S(1)} %copy-done.11), kind=kOutput, calls=%fused_computation.2 | convolution fusion | flops 6448742400 | bytes 14692352 | tf_op jit(solution)/shard_map/dot_general | solution.py:21
  113.2 24.8 %attend.1 = (bf16[1024,1024]{1,0:T(8,128)(2,1)}, f32[2,8,2,512]{3,2,1,0:T(2,128)}) custom-call(s32[2,512,1]{2,1,0:T(8,128)} %copy.57.seg_col, s32[2,1,512]{2,1,0:T(1,128)} %broadcast_in_dim.31.seg_row, bf16[1024,3072]{1,0:T(8,128)(2,1)} %add_convert_fusion.q_ref.k_ref.v_ref, bf16[1024,3072]{1,0:T(8,128)(2,1)} %add_convert_fusion.q_ref.k_ref.v_ref, ...), custom_call_target="tpu_custom_call" | custom-call | tf_op jit(solution)/shard_map/attend/pallas_call | solution.py:391
  150.2 5.7 fusion.123
  155.9 3.7 fusion.50
  161.6 9.2 %place.4 = (bf16[1024,1024]{1,0:T(8,128)(2,1)}, bf16[1024,4096]{1,0:T(8,128)(2,1)}) custom-call(s32[4]{0:T(128)} %pad_add_fusion.where, bf16[4,32,5120]{2,1,0:T(8,128)(2,1)} %stack.68.refs_0_, bf16[4,32,5120]{2,1,0:T(8,128)(2,1)} %collective-permute-done.17.refs_1_, bf16[4,32,5120]{2,1,0:T(8,128)(2,1)} %collective-permute-done.18.refs_2_, ...), custom_call_target="tpu_custom_call" | custom-call | tf_op jit(solution)/shard_map/place/pallas_call | solution.py:207
  170.8 4.7 fusion.127
  178.2 30.7 %widen.1 = (bf16[1024,4096]{1,0:T(8,128)(2,1)}, bf16[1024,4096]{1,0:T(8,128)(2,1)}, bf16[1024,2048]{1,0:T(8,128)(2,1)}, bf16[1024,2048]{1,0:T(8,128)(2,1)}) custom-call(s32[4]{0:T(128)} %pad_add_fusion.where, bf16[1024,1024]{1,0:T(8,128)(2,1)} %add_convert_fusion.1.x_ref, bf16[1024,4096]{1,0:T(8,128)(2,1)} %get-tuple-element.121.w_ref, ...), custom_call_target="tpu_custom_call" | custom-call | tf_op jit(solution)/shard_map/widen/pallas_call | solution.py:533
  210.7 3.7 fusion.51
  214.4 3.7 fusion.49
  218.1 7.7 %place.5 = bf16[4096,1024]{1,0:T(8,128)(2,1)} custom-call(s32[4]{0:T(128)} %pad_add_fusion.where, bf16[4,128,1024]{2,1,0:T(8,128)(2,1)} %stack.69.refs_0_, bf16[4,128,1024]{2,1,0:T(8,128)(2,1)} %collective-permute-done.24.refs_1_, bf16[4,128,1024]{2,1,0:T(8,128)(2,1)} %collective-permute-done.25.refs_2_, ...), custom_call_target="tpu_custom_call" | custom-call | tf_op jit(solution)/shard_map/place/pallas_call | solution.py:207
  225.8 14.6 %fusion.128 = (f32[1024]{0:T(1024)S(1)}, f32[1024,1024]{1,0:T(8,128)S(1)}) fusion(f32[1024]{0:T(1024)S(1)} %get-tuple-element.207, f32[1024,1024]{1,0:T(8,128)} %copy-done.7, bf16[1024,4096]{1,0:T(8,128)(2,1)} %get-tuple-element.122, bf16[4096,1024]{1,0:T(8,128)(2,1)} %place.5), kind=kOutput, calls=%fused_computation.252 | convolution fusion | flops 8593079296 | bytes 25174016 | tf_op jit(solution)/shard_map/dot_general | solution.py:21
  248.0 4.3 fusion.129
  252.3 6.1 %convolution_convert_fusion.4 = bf16[2048,1024]{1,0:T(8,128)(2,1)} fusion(bf16[1024,2048]{1,0:T(8,128)(2,1)S(1)} %copy-done.79, bf16[1024,1024]{1,0:T(8,128)(2,1)S(1)} %get-tuple-element.129), kind=kOutput, calls=%fused_computation.50 | convolution fusion | flops 4297064448 | bytes 10485760 | tf_op jit(solution)/shard_map/dot_general | solution.py:25
  261.4 6.4 %convolution_convert_fusion.3 = bf16[2048,1024]{1,0:T(8,128)(2,1)} fusion(bf16[1024,2048]{1,0:T(8,128)(2,1)S(1)} %copy-done.78, bf16[1024,1024]{1,0:T(8,128)(2,1)S(1)} %get-tuple-element.129), kind=kOutput, calls=%fused_computation.49 | convolution fusion | flops 4297064448 | bytes 10485760 | tf_op jit(solution)/shard_map/dot_general | solution.py:25
  272.3 15.2 %multiply_convert_fusion = bf16[1024,4096]{1,0:T(8,128)(2,1)} fusion(bf16[1024,4096]{1,0:T(8,128)(2,1)} %get-tuple-element.123, bf16[1024,1024]{1,0:T(8,128)(2,1)S(1)} %get-tuple-element.129, bf16[4096,1024]{1,0:T(8,128)(2,1)} %place.5), kind=kOutput, calls=%fused_computation.1 | convolution fusion | flops 8610906112 | bytes 27262976 | tf_op jit(solution)/shard_map/dot_general | solution.py:31
  287.5 4.4 fusion.21
  293.0 6.5 %fold_inner.5 = (bf16[4,128,1024]{2,1,0:T(8,128)(2,1)}, bf16[4,128,1024]{2,1,0:T(8,128)(2,1)}, bf16[4,128,1024]{2,1,0:T(8,128)(2,1)}, bf16[4,128,1024]{2,1,0:T(8,128)(2,1)}) custom-call(s32[4]{0:T(128)} %pad_add_fusion.where, bf16[4,2,2,128,1024]{4,3,2,1,0:T(8,128)(2,1)} %bitcast.170, bf16[4,2,2,128,1024]{4,3,2,1,0:T(8,128)(2,1)} %collective-permute-done.33.refs_1_), custom_call_target="tpu_custom_call" | custom-call | tf_op jit(solution)/shard_map/fold_inner/pallas_call | solution.py:292
  299.6 9.8 %convolution_convert_fusion.2 = bf16[512,4096]{1,0:T(8,128)(2,1)} fusion(bf16[1024,4096]{1,0:T(8,128)(2,1)} %multiply_convert_fusion, bf16[1024,1024]{1,0:T(8,128)(2,1)S(1)} %copy-done.91), kind=kOutput, calls=%fused_computation.7 | convolution fusion | flops 4297064448 | bytes 13631488 | tf_op jit(solution)/shard_map/dot_general | solution.py:25
  312.9 16.0 %multiply_reduce_fusion.1 = (f32[1024]{0:T(1024)}, f32[1024]{0:T(1024)S(1)}, f32[1024]{0:T(1024)S(1)}, f32[1024]{0:T(1024)}, f32[1024,1024]{1,0:T(8,128)S(1)}) fusion(f32[1024,1024]{1,0:T(8,128)S(1)} %copy-done.8, f32[1024]{0:T(1024)S(1)} %copy-done.60, f32[1024]{0:T(1024)S(1)} %copy-done.48, f32[1024]{0:T(1024)S(1)} %copy-done.62, ...), kind=kOutput, calls=%fused_computation.32 | convolution fusion | flops 8599367680 | bytes 25194496 | tf_op jit(solution)/shard_map/dot_general | solution.py:31
  331.8 9.5 %convolution_convert_fusion.1 = bf16[512,4096]{1,0:T(8,128)(2,1)} fusion(bf16[1024,4096]{1,0:T(8,128)(2,1)} %multiply_convert_fusion, bf16[1024,1024]{1,0:T(8,128)(2,1)S(1)} %copy-done.92), kind=kOutput, calls=%fused_computation.6 | convolution fusion | flops 4297064448 | bytes 13631488 | tf_op jit(solution)/shard_map/dot_general | solution.py:25
  341.3 17.4 %collective-permute-done.36.refs_2_ = bf16[4,128,1024]{2,1,0:T(8,128)(2,1)} collective-permute-done((bf16[4,128,1024]{2,1,0:T(8,128)(2,1)S(1)}, bf16[4,128,1024]{2,1,0:T(8,128)(2,1)}, u32[]{:S(2)}, u32[]{:S(2)}) %collective-permute-start.36) | collective-permute-done | bytes 1048608 | tf_op jit(solution)/shard_map/ppermute | solution.py:99
  358.7 4.2 fold_outer.5
  367.5 4.6 convert_reduce_fusion
  374.2 9.6 %collective-permute-done.47 = bf16[128,1024]{1,0:T(8,128)(2,1)S(1)} collective-permute-done((bf16[128,1024]{1,0:T(8,128)(2,1)}, bf16[128,1024]{1,0:T(8,128)(2,1)S(1)}, u32[]{:S(2)}, u32[]{:S(2)}) %collective-permute-start.47) | collective-permute-done | bytes 262176 | tf_op jit(solution)/shard_map/ppermute | solution.py:99
  384.8 6.6 %fold_inner.6 = (bf16[4,32,4096]{2,1,0:T(8,128)(2,1)}, bf16[4,32,4096]{2,1,0:T(8,128)(2,1)}, bf16[4,32,4096]{2,1,0:T(8,128)(2,1)}, bf16[4,32,4096]{2,1,0:T(8,128)(2,1)}) custom-call(s32[4]{0:T(128)} %pad_add_fusion.where, bf16[4,2,2,32,4096]{4,3,2,1,0:T(8,128)(2,1)} %bitcast.169, bf16[4,2,2,32,4096]{4,3,2,1,0:T(8,128)(2,1)} %collective-permute-done.34.refs_1_), custom_call_target="tpu_custom_call" | custom-call | tf_op jit(solution)/shard_map/fold_inner/pallas_call | solution.py:292
  399.9 3.7 convolution_convert_fusion.9.do_ref
  405.5 4.2 fold_inner.7
  411.8 17.4 %attend_back.2 = (bf16[1024,512]{1,0:T(8,128)(2,1)}, bf16[1024,512]{1,0:T(8,128)(2,1)}, bf16[1024,512]{1,0:T(8,128)(2,1)}) custom-call(s32[2,512,1]{2,1,0:T(8,128)} %copy.57.seg_col, s32[2,1,512]{2,1,0:T(1,128)} %broadcast_in_dim.31.seg_row, bf16[1024,3072]{1,0:T(8,128)(2,1)} %add_convert_fusion.q_ref.k_ref.v_ref, ...), custom_call_target="tpu_custom_call" | custom-call | tf_op jit(solution)/shard_map/attend_back/pallas_call | solution.py:445
  435.0 5.0 collective-permute-done.40.refs_2_
  440.3 4.3 fold_outer.6
  444.6 5.7 collective-permute-start.71
  451.4 4.2 convolution_convert_fusion.7
  455.6 17.7 %attend_back.3 = (bf16[1024,512]{1,0:T(8,128)(2,1)}, bf16[1024,512]{1,0:T(8,128)(2,1)}, bf16[1024,512]{1,0:T(8,128)(2,1)}) custom-call(s32[2,512,1]{2,1,0:T(8,128)} %copy.57.seg_col, s32[2,1,512]{2,1,0:T(1,128)} %broadcast_in_dim.31.seg_row, bf16[1024,3072]{1,0:T(8,128)(2,1)} %add_convert_fusion.q_ref.k_ref.v_ref, ...), custom_call_target="tpu_custom_call" | custom-call | tf_op jit(solution)/shard_map/attend_back/pallas_call | solution.py:445
  478.1 4.2 collective-permute-done.45.refs_3_
  493.9 4.5 fold_inner.8
  498.5 4.4 convolution_convert_fusion.6
  510.3 5.1 fusion.46
  531.0 3.9 collective-permute-done.59
  539.5 4.8 fold_inner.9
  547.9 3.7 fusion.16
  553.9 12.2 %collective-permute-done.52 = f32[24,1024]{1,0:T(8,128)S(1)} collective-permute-done((f32[24,1024]{1,0:T(8,128)S(1)}, f32[24,1024]{1,0:T(8,128)S(1)}, u32[]{:S(2)}, u32[]{:S(2)}) %collective-permute-start.52) | collective-permute-done | bytes 98336 | tf_op jit(solution)/shard_map/ppermute | solution.py:358
  566.6 5.5 fusion.15
  588.6 5.2 collective-permute-done.55
  (459 shorter events, 206.4 us)
Async XLA Ops:
  7.9 16.8 %collective-permute-start.1 = (bf16[32,3328]{1,0:T(8,128)(2,1)S(1)}, bf16[32,3328]{1,0:T(8,128)(2,1)}, u32[]{:S(2)}, u32[]{:S(2)}) collective-permute-start(bf16[32,3328]{1,0:T(8,128)(2,1)S(1)} %fusion.86.refs_0_), channel_id=1, source_target_pairs={{0,8},{2,10},{4,12},{6,14},{8,16},{10,18},{12,20},{14,22},{16,24},... | collective-permute-start | bytes 638984 | tf_op jit(solution)/shard_map/ppermute | solution.py:99
  11.0 16.6 %collective-permute-start.2 = (bf16[32,3328]{1,0:T(8,128)(2,1)S(1)}, bf16[32,3328]{1,0:T(8,128)(2,1)}, u32[]{:S(2)}, u32[]{:S(2)}) collective-permute-start(bf16[32,3328]{1,0:T(8,128)(2,1)S(1)} %fusion.86.refs_0_), channel_id=1, source_target_pairs={{0,16},{2,18},{4,20},{6,22},{8,24},{10,26},{12,28},{14,30},{16,0},... | collective-permute-start | bytes 638984 | tf_op jit(solution)/shard_map/ppermute | solution.py:99
  13.6 14.1 %collective-permute-start.3 = (bf16[32,3328]{1,0:T(8,128)(2,1)S(1)}, bf16[32,3328]{1,0:T(8,128)(2,1)}, u32[]{:S(2)}, u32[]{:S(2)}) collective-permute-start(bf16[32,3328]{1,0:T(8,128)(2,1)S(1)} %fusion.86.refs_0_), channel_id=1, source_target_pairs={{0,24},{2,26},{4,28},{6,30},{8,0},{10,2},{12,4},{14,6},{16,8},{18,... | collective-permute-start | bytes 638984 | tf_op jit(solution)/shard_map/ppermute | solution.py:99
  16.3 60.7 %collective-permute-start = (bf16[2,256,1024]{2,1,0:T(8,128)(2,1)S(1)}, bf16[2,256,1024]{2,1,0:T(8,128)(2,1)S(1)}, u32[]{:S(2)}, u32[]{:S(2)}) collective-permute-start(bf16[2,256,1024]{2,1,0:T(8,128)(2,1)S(1)} %constant_dynamic-slice_fusion.3), channel_id=1, source_target_pairs={{0,1},{1,0},{2,3},{3,2},{4,5},{5,4},{6,7},{7,6},{8,9},{9,8},{10,11... | collective-permute-start | bytes 3145736 | tf_op jit(solution)/shard_map/ppermute | solution.py:102
  16.3 21.7 %collective-permute-start.32 = (bf16[1,20,8,1024]{3,2,1,0:T(8,128)(2,1)}, bf16[1,20,8,1024]{3,2,1,0:T(8,128)(2,1)}, u32[]{:S(2)}, u32[]{:S(2)}) collective-permute-start(bf16[1,20,8,1024]{3,2,1,0:T(8,128)(2,1)} %param.42), channel_id=1, source_target_pairs={{0,1},{1,0},{2,3},{3,2},{4,5},{5,4},{6,7},{7,6},{8,9},{9,8},{10,11... | collective-permute-start | bytes 983048 | tf_op jit(solution)/shard_map/ppermute | solution.py:102
  27.7 12.9 %collective-permute-start.7 = (bf16[32,5120]{1,0:T(8,128)(2,1)S(1)}, bf16[32,5120]{1,0:T(8,128)(2,1)S(1)}, u32[]{:S(2)}, u32[]{:S(2)}) collective-permute-start(bf16[32,5120]{1,0:T(8,128)(2,1)S(1)} %constant_dynamic-update-slice_fusion.refs_0_), channel_id=1, source_target_pairs={{0,8},{2,10},{4,12},{6,14},{8,16},{10,18},{12,20},{14,22},{16,24},... | collective-permute-start | bytes 983048 | tf_op jit(solution)/shard_map/ppermute | solution.py:99
  35.1 33.7 %collective-permute-start.4 = (bf16[4,32,3328]{2,1,0:T(8,128)(2,1)}, bf16[4,32,3328]{2,1,0:T(8,128)(2,1)}, u32[]{:S(2)}, u32[]{:S(2)}) collective-permute-start(bf16[4,32,3328]{2,1,0:T(8,128)(2,1)} %stack.67.refs_0_), channel_id=1, source_target_pairs={{0,2},{2,0},{4,6},{6,4},{8,10},{10,8},{12,14},{14,12},{16,18},{18,... | collective-permute-start | bytes 2555912 | tf_op jit(solution)/shard_map/ppermute | solution.py:99
  36.6 37.9 %collective-permute-start.5 = (bf16[4,32,3328]{2,1,0:T(8,128)(2,1)}, bf16[4,32,3328]{2,1,0:T(8,128)(2,1)}, u32[]{:S(2)}, u32[]{:S(2)}) collective-permute-start(bf16[4,32,3328]{2,1,0:T(8,128)(2,1)} %stack.67.refs_0_), channel_id=1, source_target_pairs={{0,4},{2,6},{4,0},{6,2},{8,12},{10,14},{12,8},{14,10},{16,20},{18,... | collective-permute-start | bytes 2555912 | tf_op jit(solution)/shard_map/ppermute | solution.py:99
  38.1 38.4 %collective-permute-start.6 = (bf16[4,32,3328]{2,1,0:T(8,128)(2,1)}, bf16[4,32,3328]{2,1,0:T(8,128)(2,1)}, u32[]{:S(2)}, u32[]{:S(2)}) collective-permute-start(bf16[4,32,3328]{2,1,0:T(8,128)(2,1)} %stack.67.refs_0_), channel_id=1, source_target_pairs={{0,6},{2,4},{4,2},{6,0},{8,14},{10,12},{12,10},{14,8},{16,22},{18,... | collective-permute-start | bytes 2555912 | tf_op jit(solution)/shard_map/ppermute | solution.py:99
  40.6 16.0 %collective-permute-start.8 = (bf16[32,5120]{1,0:T(8,128)(2,1)S(1)}, bf16[32,5120]{1,0:T(8,128)(2,1)S(1)}, u32[]{:S(2)}, u32[]{:S(2)}) collective-permute-start(bf16[32,5120]{1,0:T(8,128)(2,1)S(1)} %constant_dynamic-update-slice_fusion.refs_0_), channel_id=1, source_target_pairs={{0,16},{2,18},{4,20},{6,22},{8,24},{10,26},{12,28},{14,30},{16,0},... | collective-permute-start | bytes 983048 | tf_op jit(solution)/shard_map/ppermute | solution.py:99
  67.3 36.3 %collective-permute-start.17 = (bf16[4,32,5120]{2,1,0:T(8,128)(2,1)}, bf16[4,32,5120]{2,1,0:T(8,128)(2,1)}, u32[]{:S(2)}, u32[]{:S(2)}) collective-permute-start(bf16[4,32,5120]{2,1,0:T(8,128)(2,1)} %stack.68.refs_0_), channel_id=1, source_target_pairs={{0,2},{2,0},{4,6},{6,4},{8,10},{10,8},{12,14},{14,12},{16,18},{18,... | collective-permute-start | bytes 3932168 | tf_op jit(solution)/shard_map/ppermute | solution.py:99
  81.3 59.2 %collective-permute-start.18 = (bf16[4,32,5120]{2,1,0:T(8,128)(2,1)}, bf16[4,32,5120]{2,1,0:T(8,128)(2,1)}, u32[]{:S(2)}, u32[]{:S(2)}) collective-permute-start(bf16[4,32,5120]{2,1,0:T(8,128)(2,1)} %stack.68.refs_0_), channel_id=1, source_target_pairs={{0,4},{2,6},{4,0},{6,2},{8,12},{10,14},{12,8},{14,10},{16,20},{18,... | collective-permute-start | bytes 3932168 | tf_op jit(solution)/shard_map/ppermute | solution.py:99
  81.9 58.6 %collective-permute-start.19 = (bf16[4,32,5120]{2,1,0:T(8,128)(2,1)}, bf16[4,32,5120]{2,1,0:T(8,128)(2,1)}, u32[]{:S(2)}, u32[]{:S(2)}) collective-permute-start(bf16[4,32,5120]{2,1,0:T(8,128)(2,1)} %stack.68.refs_0_), channel_id=1, source_target_pairs={{0,6},{2,4},{4,2},{6,0},{8,14},{10,12},{12,10},{14,8},{16,22},{18,... | collective-permute-start | bytes 3932168 | tf_op jit(solution)/shard_map/ppermute | solution.py:99
  84.3 56.7 %collective-permute-start.14 = (bf16[128,1024]{1,0:T(8,128)(2,1)}, bf16[128,1024]{1,0:T(8,128)(2,1)S(1)}, u32[]{:S(2)}, u32[]{:S(2)}) collective-permute-start(bf16[128,1024]{1,0:T(8,128)(2,1)} %refs_0_.1), channel_id=1, source_target_pairs={{0,8},{2,10},{4,12},{6,14},{8,16},{10,18},{12,20},{14,22},{16,24},... | collective-permute-start | bytes 786440 | tf_op jit(solution)/shard_map/ppermute | solution.py:99
  84.3 56.8 %collective-permute-start.15 = (bf16[128,1024]{1,0:T(8,128)(2,1)}, bf16[128,1024]{1,0:T(8,128)(2,1)}, u32[]{:S(2)}, u32[]{:S(2)}) collective-permute-start(bf16[128,1024]{1,0:T(8,128)(2,1)} %refs_0_.1), channel_id=1, source_target_pairs={{0,16},{2,18},{4,20},{6,22},{8,24},{10,26},{12,28},{14,30},{16,0},... | collective-permute-start | bytes 786440 | tf_op jit(solution)/shard_map/ppermute | solution.py:99
  103.6 40.2 %collective-permute-start.16 = (bf16[128,1024]{1,0:T(8,128)(2,1)}, bf16[128,1024]{1,0:T(8,128)(2,1)}, u32[]{:S(2)}, u32[]{:S(2)}) collective-permute-start(bf16[128,1024]{1,0:T(8,128)(2,1)} %refs_0_.1), channel_id=1, source_target_pairs={{0,24},{2,26},{4,28},{6,30},{8,0},{10,2},{12,4},{14,6},{16,8},{18,... | collective-permute-start | bytes 786440 | tf_op jit(solution)/shard_map/ppermute | solution.py:99
  140.4 19.1 %collective-permute-start.20 = (bf16[4,32,5120]{2,1,0:T(8,128)(2,1)}, bf16[4,32,5120]{2,1,0:T(8,128)(2,1)}, u32[]{:S(2)}, u32[]{:S(2)}) collective-permute-start(bf16[4,32,5120]{2,1,0:T(8,128)(2,1)} %stack.68.refs_0_), channel_id=1, source_target_pairs={{0,1},{1,0},{2,3},{3,2},{4,5},{5,4},{6,7},{7,6},{8,9},{9,8},{10,11... | collective-permute-start | bytes 3932168 | tf_op jit(solution)/shard_map/ppermute | solution.py:102
  140.4 19.7 %collective-permute-start.21 = (bf16[4,32,5120]{2,1,0:T(8,128)(2,1)}, bf16[4,32,5120]{2,1,0:T(8,128)(2,1)}, u32[]{:S(2)}, u32[]{:S(2)}) collective-permute-start(bf16[4,32,5120]{2,1,0:T(8,128)(2,1)} %collective-permute-done.17.refs_1_), channel_id=1, source_target_pairs={{0,1},{1,0},{2,3},{3,2},{4,5},{5,4},{6,7},{7,6},{8,9},{9,8},{10,11... | collective-permute-start | bytes 3932168 | tf_op jit(solution)/shard_map/ppermute | solution.py:102
  141.0 20.7 %collective-permute-start.22 = (bf16[4,32,5120]{2,1,0:T(8,128)(2,1)}, bf16[4,32,5120]{2,1,0:T(8,128)(2,1)}, u32[]{:S(2)}, u32[]{:S(2)}) collective-permute-start(bf16[4,32,5120]{2,1,0:T(8,128)(2,1)} %collective-permute-done.18.refs_2_), channel_id=1, source_target_pairs={{0,1},{1,0},{2,3},{3,2},{4,5},{5,4},{6,7},{7,6},{8,9},{9,8},{10,11... | collective-permute-start | bytes 3932168 | tf_op jit(solution)/shard_map/ppermute | solution.py:102
  141.0 20.6 %collective-permute-start.23 = (bf16[4,32,5120]{2,1,0:T(8,128)(2,1)}, bf16[4,32,5120]{2,1,0:T(8,128)(2,1)}, u32[]{:S(2)}, u32[]{:S(2)}) collective-permute-start(bf16[4,32,5120]{2,1,0:T(8,128)(2,1)} %collective-permute-done.19.refs_3_), channel_id=1, source_target_pairs={{0,1},{1,0},{2,3},{3,2},{4,5},{5,4},{6,7},{7,6},{8,9},{9,8},{10,11... | collective-permute-start | bytes 3932168 | tf_op jit(solution)/shard_map/ppermute | solution.py:102
  147.7 61.2 %collective-permute-start.24 = (bf16[4,128,1024]{2,1,0:T(8,128)(2,1)}, bf16[4,128,1024]{2,1,0:T(8,128)(2,1)}, u32[]{:S(2)}, u32[]{:S(2)}) collective-permute-start(bf16[4,128,1024]{2,1,0:T(8,128)(2,1)} %stack.69.refs_0_), channel_id=1, source_target_pairs={{0,2},{2,0},{4,6},{6,4},{8,10},{10,8},{12,14},{14,12},{16,18},{18,... | collective-permute-start | bytes 3145736 | tf_op jit(solution)/shard_map/ppermute | solution.py:99
  159.6 49.4 %collective-permute-start.25 = (bf16[4,128,1024]{2,1,0:T(8,128)(2,1)}, bf16[4,128,1024]{2,1,0:T(8,128)(2,1)}, u32[]{:S(2)}, u32[]{:S(2)}) collective-permute-start(bf16[4,128,1024]{2,1,0:T(8,128)(2,1)} %stack.69.refs_0_), channel_id=1, source_target_pairs={{0,4},{2,6},{4,0},{6,2},{8,12},{10,14},{12,8},{14,10},{16,20},{18,... | collective-permute-start | bytes 3145736 | tf_op jit(solution)/shard_map/ppermute | solution.py:99
  160.1 48.8 %collective-permute-start.26 = (bf16[4,128,1024]{2,1,0:T(8,128)(2,1)}, bf16[4,128,1024]{2,1,0:T(8,128)(2,1)}, u32[]{:S(2)}, u32[]{:S(2)}) collective-permute-start(bf16[4,128,1024]{2,1,0:T(8,128)(2,1)} %stack.69.refs_0_), channel_id=1, source_target_pairs={{0,6},{2,4},{4,2},{6,0},{8,14},{10,12},{12,10},{14,8},{16,22},{18,... | collective-permute-start | bytes 3145736 | tf_op jit(solution)/shard_map/ppermute | solution.py:99
  258.5 34.5 %collective-permute-start.33 = (bf16[4,2,2,128,1024]{4,3,2,1,0:T(8,128)(2,1)}, bf16[4,2,2,128,1024]{4,3,2,1,0:T(8,128)(2,1)}, u32[]{:S(2)}, u32[]{:S(2)}) collective-permute-start(bf16[4,2,2,128,1024]{4,3,2,1,0:T(8,128)(2,1)} %bitcast.20), channel_id=1, source_target_pairs={{0,1},{1,0},{2,3},{3,2},{4,5},{5,4},{6,7},{7,6},{8,9},{9,8},{10,11... | collective-permute-start | bytes 12582920 | tf_op jit(solution)/shard_map/ppermute | solution.py:102
  271.8 20.1 %collective-permute-start.31 = (bf16[20,8192]{1,0:T(8,128)(2,1)}, bf16[20,8192]{1,0:T(8,128)(2,1)S(1)}, u32[]{:S(2)}, u32[]{:S(2)}) collective-permute-start(bf16[20,8192]{1,0:T(8,128)(2,1)} %dynamic-slice_bitcast_fusion), channel_id=1, source_target_pairs={{0,1},{1,0},{2,3},{3,2},{4,5},{5,4},{6,7},{7,6},{8,9},{9,8},{10,11... | collective-permute-start | bytes 983048 | tf_op jit(solution)/shard_map/ppermute | solution.py:102
  309.4 75.4 %collective-permute-start.34 = (bf16[4,2,2,32,4096]{4,3,2,1,0:T(8,128)(2,1)}, bf16[4,2,2,32,4096]{4,3,2,1,0:T(8,128)(2,1)}, u32[]{:S(2)}, u32[]{:S(2)}) collective-permute-start(bf16[4,2,2,32,4096]{4,3,2,1,0:T(8,128)(2,1)} %bitcast.22), channel_id=1, source_target_pairs={{0,1},{1,0},{2,3},{3,2},{4,5},{5,4},{6,7},{7,6},{8,9},{9,8},{10,11... | collective-permute-start | bytes 12582920 | tf_op jit(solution)/shard_map/ppermute | solution.py:102
  309.4 31.9 %collective-permute-start.35 = (bf16[4,128,1024]{2,1,0:T(8,128)(2,1)S(1)}, bf16[4,128,1024]{2,1,0:T(8,128)(2,1)S(1)}, u32[]{:S(2)}, u32[]{:S(2)}) collective-permute-start(bf16[4,128,1024]{2,1,0:T(8,128)(2,1)S(1)} %copy-done.84), channel_id=1, source_target_pairs={{0,2},{2,0},{4,6},{6,4},{8,10},{10,8},{12,14},{14,12},{16,18},{18,... | collective-permute-start | bytes 3145736 | tf_op jit(solution)/shard_map/ppermute | solution.py:99
  310.9 47.8 %collective-permute-start.36 = (bf16[4,128,1024]{2,1,0:T(8,128)(2,1)S(1)}, bf16[4,128,1024]{2,1,0:T(8,128)(2,1)}, u32[]{:S(2)}, u32[]{:S(2)}) collective-permute-start(bf16[4,128,1024]{2,1,0:T(8,128)(2,1)S(1)} %copy-done.83), channel_id=1, source_target_pairs={{0,4},{2,6},{4,0},{6,2},{8,12},{10,14},{12,8},{14,10},{16,20},{18,... | collective-permute-start | bytes 3145736 | tf_op jit(solution)/shard_map/ppermute | solution.py:99
  311.4 47.2 %collective-permute-start.37 = (bf16[4,128,1024]{2,1,0:T(8,128)(2,1)S(1)}, bf16[4,128,1024]{2,1,0:T(8,128)(2,1)}, u32[]{:S(2)}, u32[]{:S(2)}) collective-permute-start(bf16[4,128,1024]{2,1,0:T(8,128)(2,1)S(1)} %copy-done.82), channel_id=1, source_target_pairs={{0,6},{2,4},{4,2},{6,0},{8,14},{10,12},{12,10},{14,8},{16,22},{18,... | collective-permute-start | bytes 3145736 | tf_op jit(solution)/shard_map/ppermute | solution.py:99
  362.9 20.9 %collective-permute-start.47 = (bf16[128,1024]{1,0:T(8,128)(2,1)}, bf16[128,1024]{1,0:T(8,128)(2,1)S(1)}, u32[]{:S(2)}, u32[]{:S(2)}) collective-permute-start(bf16[128,1024]{1,0:T(8,128)(2,1)} %get-tuple-element.142), channel_id=1, source_target_pairs={{0,16},{2,18},{4,20},{6,22},{8,24},{10,26},{12,28},{14,30},{16,0},... | collective-permute-start | bytes 786440 | tf_op jit(solution)/shard_map/ppermute | solution.py:99
  364.6 19.3 %collective-permute-start.48 = (bf16[128,1024]{1,0:T(8,128)(2,1)}, bf16[128,1024]{1,0:T(8,128)(2,1)S(1)}, u32[]{:S(2)}, u32[]{:S(2)}) collective-permute-start(bf16[128,1024]{1,0:T(8,128)(2,1)} %get-tuple-element.143), channel_id=1, source_target_pairs={{0,24},{2,26},{4,28},{6,30},{8,0},{10,2},{12,4},{14,6},{16,8},{18,... | collective-permute-start | bytes 786440 | tf_op jit(solution)/shard_map/ppermute | solution.py:99
  391.4 43.6 %collective-permute-start.39 = (bf16[4,32,4096]{2,1,0:T(8,128)(2,1)}, bf16[4,32,4096]{2,1,0:T(8,128)(2,1)}, u32[]{:S(2)}, u32[]{:S(2)}) collective-permute-start(bf16[4,32,4096]{2,1,0:T(8,128)(2,1)} %get-tuple-element.137), channel_id=1, source_target_pairs={{0,2},{2,0},{4,6},{6,4},{8,10},{10,8},{12,14},{14,12},{16,18},{18,... | collective-permute-start | bytes 3145736 | tf_op jit(solution)/shard_map/ppermute | solution.py:99
  392.0 47.9 %collective-permute-start.40 = (bf16[4,32,4096]{2,1,0:T(8,128)(2,1)}, bf16[4,32,4096]{2,1,0:T(8,128)(2,1)}, u32[]{:S(2)}, u32[]{:S(2)}) collective-permute-start(bf16[4,32,4096]{2,1,0:T(8,128)(2,1)} %get-tuple-element.138), channel_id=1, source_target_pairs={{0,4},{2,6},{4,0},{6,2},{8,12},{10,14},{12,8},{14,10},{16,20},{18,... | collective-permute-start | bytes 3145736 | tf_op jit(solution)/shard_map/ppermute | solution.py:99
  393.4 46.9 %collective-permute-start.41 = (bf16[4,32,4096]{2,1,0:T(8,128)(2,1)}, bf16[4,32,4096]{2,1,0:T(8,128)(2,1)}, u32[]{:S(2)}, u32[]{:S(2)}) collective-permute-start(bf16[4,32,4096]{2,1,0:T(8,128)(2,1)} %get-tuple-element.139), channel_id=1, source_target_pairs={{0,6},{2,4},{4,2},{6,0},{8,14},{10,12},{12,10},{14,8},{16,22},{18,... | collective-permute-start | bytes 3145736 | tf_op jit(solution)/shard_map/ppermute | solution.py:99
  409.7 63.6 %collective-permute-start.43 = (bf16[4,32,1024]{2,1,0:T(8,128)(2,1)}, bf16[4,32,1024]{2,1,0:T(8,128)(2,1)S(1)}, u32[]{:S(2)}, u32[]{:S(2)}) collective-permute-start(bf16[4,32,1024]{2,1,0:T(8,128)(2,1)} %get-tuple-element.146), channel_id=1, source_target_pairs={{0,2},{2,0},{4,6},{6,4},{8,10},{10,8},{12,14},{14,12},{16,18},{18,... | collective-permute-start | bytes 786440 | tf_op jit(solution)/shard_map/ppermute | solution.py:99
  410.4 64.3 %collective-permute-start.44 = (bf16[4,32,1024]{2,1,0:T(8,128)(2,1)}, bf16[4,32,1024]{2,1,0:T(8,128)(2,1)}, u32[]{:S(2)}, u32[]{:S(2)}) collective-permute-start(bf16[4,32,1024]{2,1,0:T(8,128)(2,1)} %get-tuple-element.147), channel_id=1, source_target_pairs={{0,4},{2,6},{4,0},{6,2},{8,12},{10,14},{12,8},{14,10},{16,20},{18,... | collective-permute-start | bytes 786440 | tf_op jit(solution)/shard_map/ppermute | solution.py:99
  435.0 58.9 %collective-permute-start.42 = (bf16[4,2,2,32,1536]{4,3,2,1,0:T(8,128)(2,1)}, bf16[4,2,2,32,1536]{4,3,2,1,0:T(8,128)(2,1)}, u32[]{:S(2)}, u32[]{:S(2)}) collective-permute-start(bf16[4,2,2,32,1536]{4,3,2,1,0:T(8,128)(2,1)} %bitcast.26), channel_id=1, source_target_pairs={{0,1},{1,0},{2,3},{3,2},{4,5},{5,4},{6,7},{7,6},{8,9},{9,8},{10,11... | collective-permute-start | bytes 4718600 | tf_op jit(solution)/shard_map/ppermute | solution.py:102
  444.6 41.0 %collective-permute-start.71 = (bf16[32,4096]{1,0:T(8,128)(2,1)}, bf16[32,4096]{1,0:T(8,128)(2,1)}, u32[]{:S(2)}, u32[]{:S(2)}) collective-permute-start(bf16[32,4096]{1,0:T(8,128)(2,1)} %get-tuple-element.154), channel_id=1, source_target_pairs={{0,8},{2,10},{4,12},{6,14},{8,16},{10,18},{12,20},{14,22},{16,24},... | collective-permute-start | bytes 786440 | tf_op jit(solution)/shard_map/ppermute | solution.py:99
  450.3 37.2 %collective-permute-start.72 = (bf16[32,4096]{1,0:T(8,128)(2,1)}, bf16[32,4096]{1,0:T(8,128)(2,1)}, u32[]{:S(2)}, u32[]{:S(2)}) collective-permute-start(bf16[32,4096]{1,0:T(8,128)(2,1)} %get-tuple-element.155), channel_id=1, source_target_pairs={{0,16},{2,18},{4,20},{6,22},{8,24},{10,26},{12,28},{14,30},{16,0},... | collective-permute-start | bytes 786440 | tf_op jit(solution)/shard_map/ppermute | solution.py:99
  473.3 15.4 %collective-permute-start.73 = (bf16[32,4096]{1,0:T(8,128)(2,1)}, bf16[32,4096]{1,0:T(8,128)(2,1)}, u32[]{:S(2)}, u32[]{:S(2)}) collective-permute-start(bf16[32,4096]{1,0:T(8,128)(2,1)} %get-tuple-element.156), channel_id=1, source_target_pairs={{0,24},{2,26},{4,28},{6,30},{8,0},{10,2},{12,4},{14,6},{16,8},{18,... | collective-permute-start | bytes 786440 | tf_op jit(solution)/shard_map/ppermute | solution.py:99
  502.9 36.5 %collective-permute-start.49 = (bf16[4,2,2,32,1536]{4,3,2,1,0:T(8,128)(2,1)}, bf16[4,2,2,32,1536]{4,3,2,1,0:T(8,128)(2,1)}, u32[]{:S(2)}, u32[]{:S(2)}) collective-permute-start(bf16[4,2,2,32,1536]{4,3,2,1,0:T(8,128)(2,1)} %bitcast.28), channel_id=1, source_target_pairs={{0,1},{1,0},{2,3},{3,2},{4,5},{5,4},{6,7},{7,6},{8,9},{9,8},{10,11... | collective-permute-start | bytes 4718600 | tf_op jit(solution)/shard_map/ppermute | solution.py:102
  502.9 16.4 %collective-permute-start.56 = (bf16[4,32,1536]{2,1,0:T(8,128)(2,1)}, bf16[4,32,1536]{2,1,0:T(8,128)(2,1)S(1)}, u32[]{:S(2)}, u32[]{:S(2)}) collective-permute-start(bf16[4,32,1536]{2,1,0:T(8,128)(2,1)} %get-tuple-element.162), channel_id=1, source_target_pairs={{0,2},{2,0},{4,6},{6,4},{8,10},{10,8},{12,14},{14,12},{16,18},{18,... | collective-permute-start | bytes 1179656 | tf_op jit(solution)/shard_map/ppermute | solution.py:99
  504.3 18.4 %collective-permute-start.57 = (bf16[4,32,1536]{2,1,0:T(8,128)(2,1)}, bf16[4,32,1536]{2,1,0:T(8,128)(2,1)}, u32[]{:S(2)}, u32[]{:S(2)}) collective-permute-start(bf16[4,32,1536]{2,1,0:T(8,128)(2,1)} %get-tuple-element.163), channel_id=1, source_target_pairs={{0,4},{2,6},{4,0},{6,2},{8,12},{10,14},{12,8},{14,10},{16,20},{18,... | collective-permute-start | bytes 1179656 | tf_op jit(solution)/shard_map/ppermute | solution.py:99
  505.2 19.2 %collective-permute-start.58 = (bf16[4,32,1536]{2,1,0:T(8,128)(2,1)}, bf16[4,32,1536]{2,1,0:T(8,128)(2,1)}, u32[]{:S(2)}, u32[]{:S(2)}) collective-permute-start(bf16[4,32,1536]{2,1,0:T(8,128)(2,1)} %get-tuple-element.164), channel_id=1, source_target_pairs={{0,6},{2,4},{4,2},{6,0},{8,14},{10,12},{12,10},{14,8},{16,22},{18,... | collective-permute-start | bytes 1179656 | tf_op jit(solution)/shard_map/ppermute | solution.py:99
  544.3 30.6 %collective-permute-start.62 = (bf16[4,32,1536]{2,1,0:T(8,128)(2,1)}, bf16[4,32,1536]{2,1,0:T(8,128)(2,1)S(1)}, u32[]{:S(2)}, u32[]{:S(2)}) collective-permute-start(bf16[4,32,1536]{2,1,0:T(8,128)(2,1)} %get-tuple-element.174), channel_id=1, source_target_pairs={{0,2},{2,0},{4,6},{6,4},{8,10},{10,8},{12,14},{14,12},{16,18},{18,... | collective-permute-start | bytes 1179656 | tf_op jit(solution)/shard_map/ppermute | solution.py:99
  545.0 29.9 %collective-permute-start.63 = (bf16[4,32,1536]{2,1,0:T(8,128)(2,1)}, bf16[4,32,1536]{2,1,0:T(8,128)(2,1)S(1)}, u32[]{:S(2)}, u32[]{:S(2)}) collective-permute-start(bf16[4,32,1536]{2,1,0:T(8,128)(2,1)} %get-tuple-element.175), channel_id=1, source_target_pairs={{0,4},{2,6},{4,0},{6,2},{8,12},{10,14},{12,8},{14,10},{16,20},{18,... | collective-permute-start | bytes 1179656 | tf_op jit(solution)/shard_map/ppermute | solution.py:99
  546.2 28.7 %collective-permute-start.64 = (bf16[4,32,1536]{2,1,0:T(8,128)(2,1)}, bf16[4,32,1536]{2,1,0:T(8,128)(2,1)}, u32[]{:S(2)}, u32[]{:S(2)}) collective-permute-start(bf16[4,32,1536]{2,1,0:T(8,128)(2,1)} %get-tuple-element.176), channel_id=1, source_target_pairs={{0,6},{2,4},{4,2},{6,0},{8,14},{10,12},{12,10},{14,8},{16,22},{18,... | collective-permute-start | bytes 1179656 | tf_op jit(solution)/shard_map/ppermute | solution.py:99
  572.2 13.0 %collective-permute-start.54 = (f32[24,1024]{1,0:T(8,128)S(1)}, f32[24,1024]{1,0:T(8,128)S(1)}, u32[]{:S(2)}, u32[]{:S(2)}) collective-permute-start(f32[24,1024]{1,0:T(8,128)S(1)} %add.333), channel_id=1, source_target_pairs={{0,8},{2,10},{4,12},{6,14},{8,0},{10,2},{12,4},{14,6},{16,24},{18,... | collective-permute-start | bytes 294920 | tf_op jit(solution)/shard_map/ppermute | solution.py:358
  (119 other events, 2113.9 us)

commit v3 on v2

--- a/solution.py
+++ b/solution.py
@@ -68,15 +68,14 @@
     return pairs
 
 
-def crossing(dims, place, flip):
-    stride = 1
-    for size in dims[place + 1 :]:
-        stride *= size
-    count = dims[0] * dims[1] * dims[2]
+def crossing(dims, flips):
     pairs = []
-    for source in range(count):
-        digit = (source // stride) % dims[place]
-        pairs.append((source, source + ((digit ^ flip) - digit) * stride))
+    for a in range(dims[0]):
+        for b in range(dims[1]):
+            for c in range(dims[2]):
+                other = [d ^ f for d, f in zip((a, b, c), flips)]
+                source = (a * dims[1] + b) * dims[2] + c
+                pairs.append((source, (other[0] * dims[1] + other[1]) * dims[2] + other[2]))
     return pairs
 
 
@@ -257,91 +256,136 @@
     return body
 
 
-def outer_fold_kernel(dims, n):
+def outer_fold_kernel(dims, counts):
+    n = sum(counts)
+
     def body(where, *refs):
         for step in range(dims[0]):
             spot = lax.rem(where[0] + step, dims[0])
-            refs[n + step][...] = total_of([r[spot] for r in refs[:n]]).astype(BF)
+            at, start = 0, 0
+            for count in counts:
+                width = refs[at].shape[2]
+                total = total_of([r[spot] for r in refs[at : at + count]]).astype(BF)
+                refs[n + step][:, start : start + width] = total
+                at += count
+                start += width
 
     return body
 
 
+def prefetched(wires, body, grid, in_specs, out_specs, out_shape, args, name):
+    return pl.pallas_call(
+        body,
+        out_shape=out_shape,
+        grid_spec=pltpu.PrefetchScalarGridSpec(
+            num_scalar_prefetch=1, grid=grid, in_specs=in_specs, out_specs=out_specs
+        ),
+        name=name,
+    )(wires.where, *args)
+
+
 class Scatter:
-    def __init__(self, wires, products):
+    def __init__(self, wires):
         self.wires = wires
-        self.widths = [p[3].shape[1] for p in products]
-        self.m = products[0][0].shape[1] // (wires.count * 2)
-        self.plain = bool(self.m % 32 or sum(self.widths) % 128)
-        self.stage = 0
-        self.sends = ()
+        self.widths, self.kept, self.got, self.whole, self.terms = [], [], [], [], ()
+
+    def add(self, left, stay, go, right):
+        wires = self.wires
+        width = right.shape[1]
+        self.m = left.shape[1] // (wires.count * 2)
+        self.plain = bool(self.m % 32 or width % 512)
+        self.widths.append(width)
         if self.plain:
-            self.whole = [dot_first(p[0], p[3]) for p in products]
+            self.whole.append(dot_first(left, right))
+            return ()
+        shape = (*wires.dims, self.m, width)
+        send = dot_first(go, right).astype(BF).reshape(shape)
+        kept = dot_first(stay, gate(right, send)).astype(BF).reshape(shape)
+        self.kept.append(kept)
+        self.got.append(wires.swap(send))
+        return send, kept
+
+    def inner(self):
+        if self.plain:
+            return ()
+        wires, m = self.wires, self.m
+        k0, k1, k2 = wires.dims
+        n = sum(self.widths)
+        outs = prefetched(
+            wires,
+            inner_fold_kernel(wires.dims, self.widths),
+            (k0,),
+            [pl.BlockSpec((1, k1, k2, m, w), lambda z, p: (z, 0, 0, 0, 0)) for w in self.widths] * 2,
+            [pl.BlockSpec((1, m, n), lambda z, p: (z, 0, 0))] * (k1 * k2),
+            [jax.ShapeDtypeStruct((k0, m, n), BF)] * (k1 * k2),
+            [*self.kept, *self.got],
+            "fold_inner",
+        )
+        self.terms = [outs[0]] + [
+            wires.turn(o, 0, y, x) for o, (y, x) in zip(outs[1:], wires.planes[1:])
+        ]
+        return outs
+
+
+class Outer:
+    def __init__(self, wires, groups, after=()):
+        self.wires, self.groups = wires, groups
+        self.plain = groups[0].plain
+        if self.plain:
+            self.sends = ()
             return
-        shape = (*wires.dims, self.m)
-        self.sends = [
-            dot_first(p[2], p[3]).astype(BF).reshape(*shape, p[3].shape[1]) for p in products
-        ]
-        right = gate([p[3] for p in products], self.sends)
-        self.kept = [
-            dot_first(p[1], r).astype(BF).reshape(*shape, r.shape[1])
-            for p, r in zip(products, right)
-        ]
-        self.got = [wires.swap(s) for s in self.sends]
-
-    def call(self, body, grid, in_specs, out_specs, out_shape, args, name):
-        return pl.pallas_call(
-            body,
-            out_shape=out_shape,
-            grid_spec=pltpu.PrefetchScalarGridSpec(
-                num_scalar_prefetch=1, grid=grid, in_specs=in_specs, out_specs=out_specs
-            ),
-            name=name,
-        )(self.wires.where, *args)
-
-    def step(self):
-        if self.plain:
-            return
-        wires, stage, m = self.wires, self.stage, self.m
-        dims = wires.dims
-        k0, k1, k2 = dims
-        self.stage += 1
-        n = sum(self.widths)
-        if stage == 0:
-            outs = self.call(
-                inner_fold_kernel(dims, self.widths),
-                (k0,),
-                [pl.BlockSpec((1, k1, k2, m, w), lambda z, p: (z, 0, 0, 0, 0)) for w in self.widths]
-                * 2,
-                [pl.BlockSpec((1, m, n), lambda z, p: (z, 0, 0))] * (k1 * k2),
-                [jax.ShapeDtypeStruct((k0, m, n), BF)] * (k1 * k2),
-                [*self.kept, *self.got],
-                "fold_inner",
-            )
-            self.sends = outs[1:]
-            self.terms = [outs[0]] + [
-                wires.turn(o, 0, y, x) for o, (y, x) in zip(outs[1:], wires.planes[1:])
-            ]
-        elif stage == 1:
-            outs = self.call(
-                outer_fold_kernel(dims, len(self.terms)),
-                (1,),
-                [pl.BlockSpec((k0, m, n), lambda z, p: (0, 0, 0))] * len(self.terms),
-                [pl.BlockSpec((m, n), lambda z, p: (0, 0))] * k0,
-                [jax.ShapeDtypeStruct((m, n), BF)] * k0,
-                self.terms,
-                "fold_outer",
-            )
-            self.sends = outs[1:]
-            self.terms = [outs[0]] + [wires.turn(outs[r], r, 0, 0) for r in range(1, k0)]
-
-    def result(self):
+        k0 = wires.dims[0]
+        self.tall = max(g.m for g in groups)
+        self.steps = 4
+        self.rows = min(g.m for g in groups)
+        terms = [g.terms for g in groups]
+        if after:
+            terms = gate(terms, after)
+        specs, self.blocks = [], []
+        for g in groups:
+            width = sum(g.widths)
+            if g.m == self.rows:
+                self.blocks.append(width // self.steps)
+                spec = pl.BlockSpec((k0, g.m, width // self.steps), lambda j, p: (0, 0, j))
+            else:
+                self.blocks.append(width)
+                spec = pl.BlockSpec((k0, self.rows, width), lambda j, p: (0, j, 0))
+            specs += [spec] * len(g.terms)
+        n = sum(self.blocks)
+        outs = prefetched(
+            wires,
+            outer_fold_kernel(wires.dims, [len(t) for t in terms]),
+            (self.steps,),
+            specs,
+            [pl.BlockSpec((self.rows, n), lambda j, p: (0, j))] * k0,
+            [jax.ShapeDtypeStruct((self.rows, n * self.steps), BF)] * k0,
+            [t for group in terms for t in group],
+            "fold_outer",
+        )
+        self.sends = outs
+        self.terms = [outs[0]] + [wires.turn(outs[r], r, 0, 0) for r in range(1, k0)]
+
+    def result(self, after=()):
         if self.plain:
             both = ("rows", "seq")
-            return [lax.psum_scatter(g, both, scatter_dimension=0, tiled=True) for g in self.whole]
-        done, outs, start = total_of(self.terms), [], 0
-        for w in self.widths:
-            outs.append(done[:, start : start + w])
-            start += w
+            return [
+                lax.psum_scatter(w, both, scatter_dimension=0, tiled=True)
+                for g in self.groups
+                for w in g.whole
+            ]
+        terms = gate(self.terms, after) if after else self.terms
+        done = total_of(terms).reshape(self.rows, self.steps, sum(self.blocks))
+        outs, start = [], 0
+        for g, block in zip(self.groups, self.blocks):
+            part = done[:, :, start : start + block]
+            start += block
+            if g.m != self.rows:
+                outs.append(part.transpose(1, 0, 2).reshape(g.m, block))
+                continue
+            part, at = part.reshape(self.rows, block * self.steps), 0
+            for width in g.widths:
+                outs.append(part[:, at : at + width])
+                at += width
         return outs
 
 
@@ -351,12 +395,15 @@
 
 def sum_everywhere(wires, value):
     value = value + wires.swap(value)
-    for place in (2, 1, 0):
-        size = wires.dims[place]
-        step = 1
-        while step < size:
-            value = value + lax.ppermute(value, "rows", crossing(wires.dims, place, step))
-            step *= 2
+    dims = wires.dims
+    planes = [(0, y, x) for y, x in wires.planes]
+    for flips in (planes, [(z, 0, 0) for z in range(dims[0])]):
+        terms = [value] + [
+            lax.ppermute(value, "rows", crossing(dims, flip)) for flip in flips[1:]
+        ]
+        while len(terms) > 1:
+            terms = [a + b for a, b in zip(terms[::2], terms[1::2])]
+        (value,) = terms
     return value
 
 
@@ -584,19 +631,9 @@
     records = rows_here * IMG_ROW
     capacity = out_grad.shape[1]
 
-    small = jnp.concatenate(
-        [
-            ln1_gain[None],
-            ln1_bias[None],
-            qv_bias,
-            out_bias[None],
-            ln2_gain[None],
-            ln2_bias[None],
-            fc2_bias[None],
-            fc1_bias.reshape(wide, m),
-        ],
-        axis=0,
-    )
+    vectors = [ln1_gain, ln1_bias, qv_bias[0], qv_bias[1], out_bias]
+    vectors += [ln2_gain, ln2_bias, fc2_bias, fc1_bias]
+    small = jnp.concatenate(vectors).reshape(8 + wide, m)
     n_small = small.shape[0]
     pad_cols = 256
     small_cols = jnp.pad(small.T, ((0, 0), (0, pad_cols - n_small)))
@@ -699,15 +736,14 @@
     )
     grad_resid2 = grad_resid2 + back_three
     grad_branch2 = grad_resid2.astype(BF)
-    s_fc2 = Scatter(wires, [(activated_low, act_stay, act_go, grad_branch2)])
-    grad_branch2 = gate(grad_branch2, s_fc2.sends)
+    s_fc2 = Scatter(wires)
+    grad_branch2 = gate(grad_branch2, s_fc2.add(activated_low, act_stay, act_go, grad_branch2))
     grad_fc2_shift = jnp.sum(grad_branch2.astype(F32), axis=0)
     grad_activ = dot_second(grad_branch2, fc2_full).astype(BF)
     grad_hidden = (grad_activ.astype(F32) * slope.astype(F32)).astype(BF)
-    s_fc2.step()
-    grad_hidden = gate(grad_hidden, s_fc2.sends)
-    s_fc1 = Scatter(wires, [(mlp_in, *halves(wires, mlp_in), grad_hidden)])
-    grad_hidden = gate(grad_hidden, s_fc1.sends)
+    grad_hidden = gate(grad_hidden, s_fc2.inner())
+    s_fc1 = Scatter(wires)
+    grad_hidden = gate(grad_hidden, s_fc1.add(mlp_in, *halves(wires, mlp_in), grad_hidden)[:1])
     grad_fc1_shift = jnp.sum(grad_hidden.astype(F32), axis=0)
     grad_normed2 = dot_second(grad_hidden, fc1_full)
     back_two, grad_norm2_gain, grad_norm2_shift = norm_backward(
@@ -715,37 +751,35 @@
     )
     grad_resid1 = grad_resid2 + back_two
     grad_branch1 = grad_resid1.astype(BF)
-    s_fc1.step()
-    s_fc2.step()
-    grad_branch1 = gate(grad_branch1, (s_fc1.sends, s_fc2.sends))
-    s_out = Scatter(wires, [(mixed, *halves(wires, mixed), grad_branch1)])
+    grad_branch1 = gate(grad_branch1, s_fc1.inner())
+    s_a = Scatter(wires)
+    sent = s_a.add(mixed, *halves(wires, mixed), grad_branch1)
     grad_out_shift = jnp.sum(grad_branch1.astype(F32), axis=0)
-    grad_branch1 = gate(grad_branch1, s_out.sends)
+    grad_branch1 = gate(grad_branch1, sent)
     grad_mixed = dot_second(grad_branch1, out_full).astype(BF)
-    s_out.step()
-    grad_mixed = gate(grad_mixed, s_out.sends)
+    grad_mixed = gate(grad_mixed, s_fc2.terms)
     dq_a, dk_a, dv_a = attend_back(joined, logs[:, :pairs], grad_mixed, seg, 0, pairs)
     grad_a = jnp.concatenate([dq_a, dk_a, dv_a], axis=1)
     attn_stay, attn_go = halves(wires, attn_in)
-    s_a = Scatter(wires, [(attn_in, attn_stay, attn_go, grad_a)])
-    s_fc1.step()
-    grad_mixed = gate(grad_mixed, (s_a.sends, s_fc1.sends))
+    sent = s_a.add(attn_in, attn_stay, attn_go, grad_a)
+    grad_mixed = gate(grad_mixed, (sent, s_fc1.terms))
     dq_b, dk_b, dv_b = attend_back(joined, logs[:, pairs:], grad_mixed, seg, pairs, pairs)
     grad_b = jnp.concatenate([dq_b, dk_b, dv_b], axis=1)
-    s_a.step()
-    s_out.step()
-    (done_fc2,) = s_fc2.result()
-    grad_b = gate(grad_b, (s_a.sends, s_out.sends, done_fc2))
-    s_b = Scatter(wires, [(attn_in, attn_stay, attn_go, grad_b)])
-    grad_a, grad_b = gate((grad_a, grad_b), s_b.sends)
+    z_one = Outer(wires, [s_fc2, s_fc1], (grad_b,))
+    grad_b = gate(grad_b, (s_a.inner(), z_one.sends))
+    s_b = Scatter(wires)
+    sent = s_b.add(attn_in, attn_stay, attn_go, grad_b)
+    grad_a, grad_b = gate((grad_a, grad_b), sent)
     half = pairs * 2 * HEAD_DIM
-    cuts = [slice(i * width + c * half, i * width + (c + 1) * half) for c in (0, 1) for i in range(3)]
-    grad_normed1 = sum(
-        dot_second(g, jnp.concatenate([qkv_full[:, c] for c in cuts[3 * i : 3 * i + 3]], axis=1))
-        for i, g in enumerate((grad_a, grad_b))
-    )
-    s_b.step()
-    grad_normed1 = gate(grad_normed1, s_b.sends)
+
+    def normed1_part(grads, c):
+        cuts = [slice(i * width + c * half, i * width + (c + 1) * half) for i in range(3)]
+        return dot_second(grads, jnp.concatenate([qkv_full[:, cut] for cut in cuts], axis=1))
+
+    grad_normed1 = normed1_part(grad_a, 0)
+    grad_b = gate(grad_b, (s_b.inner(), grad_normed1))
+    grad_normed1 = grad_normed1 + normed1_part(grad_b, 1)
+    grad_normed1 = gate(grad_normed1, s_a.terms)
     back_one, grad_norm1_gain, grad_norm1_shift = norm_backward(
         grad_normed1, normed1, inverse1, norm1_gain
     )
@@ -778,10 +812,9 @@
         axis=0,
     )
     little = sum_everywhere(wires, jnp.pad(little, ((0, -little.shape[0] % 8), (0, 0))))
-    s_a.step()
-    s_b.step()
-    (done_a,), (done_b,) = s_a.result(), s_b.result()
-    (done_fc1,), (done_out,) = s_fc1.result(), s_out.result()
+    z_two = Outer(wires, [s_a, s_b], (back_one,))
+    done_fc2, done_fc1 = z_one.result(z_two.sends)
+    done_out, done_a, done_b = z_two.result()
     done_qkv = jnp.concatenate(
         [d[:, i * half : (i + 1) * half] for i in range(3) for d in (done_a, done_b)], axis=1
     )

time: 610 us -> 565 us (0.926)
  the two profiles are of different devices: /device:TPU:0 before, /device:TPU:8 now
where the time goes in v3:
time: 565 us; the launch traced here: 555 us
  matrix products  166 us (29%)
  Pallas kernels  155 us (27%)
  waiting for transfers between devices  68.7 us (12%)
  starting transfers between devices  64.3 us (11%)
  local copies, waits for them, and re-layouts  57.6 us (10%)
  other arithmetic  41.8 us (7%)
    dot_general x13, matrix products, dot_first(): lax.dot_general(a, b, (((0,), (0,)), ((), ())), precision=precision, pref...  64.9 us
    ppermute x36, waiting for transfers between devices, turn(): return lax.ppermute(value, 'rows', rotation(self.dims, (z, y, x)))  53.7 us
    ppermute x36, starting transfers between devices, turn(): return lax.ppermute(value, 'rows', rotation(self.dims, (z, y, x)))  51.6 us
    dot_general x7, matrix products, dot_second(): lax.dot_general(a, b, (((1,), (1,)), ((), ())), precision=precision, pref...  51.1 us
    dot_general x9, matrix products, dot_plain(): return jnp.dot(a, b, precision=precision, preferred_element_type=F32)  49.7 us
    pallas_call x2, Pallas kernels, attend_back(): pl.pallas_call(attend_back_kernel, grid=(rows, pairs), in_specs=[pl.Block...  35.3 us
    pallas_call x6, Pallas kernels, prefetched(): pl.pallas_call(body, out_shape=out_shape, grid_spec=pltpu.PrefetchScalarG...  33.5 us
    pallas_call x1, Pallas kernels, widen(): pl.pallas_call(widen_kernel(128, chunk), out_shape=[out, out, part, part]...  30.5 us
  transfers between devices with their start and end apart: 64, of which 18 were waited for; matrix products, arithmetic and copies ran while one was open for 37% of the time, Pallas kernels for 24%

profile of v3, /device:TPU:8, one launch (start us, length us, event | category | flops | bytes accessed | tf_op | source)
XLA Modules:
  0.0 555.4 jit_solution(8239606486081627165)
XLA Ops:
  1.4 4.8 concatenate.52
  39.4 12.1 %collective-permute-done.8.refs_2_ = bf16[32,5120]{1,0:T(8,128)(2,1)S(1)} collective-permute-done((bf16[32,5120]{1,0:T(8,128)(2,1)S(1)}, bf16[32,5120]{1,0:T(8,128)(2,1)S(1)}, u32[]{:S(2)}, u32[]{:S(2)}) %collective-permute-start.8) | collective-permute-done | bytes 327712 | tf_op jit(solution)/shard_map/ppermute | solution.py:98
  55.5 6.2 %collective-permute-done.7.refs_1_ = bf16[32,5120]{1,0:T(8,128)(2,1)} collective-permute-done((bf16[32,5120]{1,0:T(8,128)(2,1)S(1)}, bf16[32,5120]{1,0:T(8,128)(2,1)}, u32[]{:S(2)}, u32[]{:S(2)}) %collective-permute-start.7) | collective-permute-done | bytes 327712 | tf_op jit(solution)/shard_map/ppermute | solution.py:98
  66.6 6.7 %collective-permute-done.5.refs_2_ = bf16[4,32,3328]{2,1,0:T(8,128)(2,1)} collective-permute-done((bf16[4,32,3328]{2,1,0:T(8,128)(2,1)}, bf16[4,32,3328]{2,1,0:T(8,128)(2,1)}, u32[]{:S(2)}, u32[]{:S(2)}) %collective-permute-start.5) | collective-permute-done | bytes 852000 | tf_op jit(solution)/shard_map/ppermute | solution.py:98
  85.4 6.9 %place.3 = (bf16[1024,3072]{1,0:T(8,128)(2,1)}, bf16[1024,256]{1,0:T(8,128)(2,1)}) custom-call(s32[4]{0:T(128)} %pad_add_fusion.where, bf16[4,32,3328]{2,1,0:T(8,128)(2,1)} %stack.67.refs_0_, bf16[4,32,3328]{2,1,0:T(8,128)(2,1)} %collective-permute-done.4.refs_1_, bf16[4,32,3328]{2,1,0:T(8,128)(2,1)} %collective-permute-done.5.refs_2_, ...), custom_call_target="tpu_custom_call" | custom-call | tf_op jit(solution)/shard_map/place/pallas_call | solution.py:206
  100.8 8.6 %add_convert_fusion.q_ref.k_ref.v_ref = bf16[1024,3072]{1,0:T(8,128)(2,1)} fusion(f32[3072]{0:T(1024)S(1)} %pad_maximum_fusion.1, bf16[1024,1024]{1,0:T(8,128)(2,1)S(1)} %fusion.11, bf16[1024,3072]{1,0:T(8,128)(2,1)S(1)} %copy-done.12), kind=kOutput, calls=%fused_computation.2 | convolution fusion | flops 6448742400 | bytes 14692352 | tf_op jit(solution)/shard_map/dot_general | solution.py:21
  109.4 24.8 %attend.1 = (bf16[1024,1024]{1,0:T(8,128)(2,1)}, f32[2,8,2,512]{3,2,1,0:T(2,128)}) custom-call(s32[2,512,1]{2,1,0:T(8,128)} %copy.43.seg_col, s32[2,1,512]{2,1,0:T(1,128)} %broadcast_in_dim.19.seg_row, bf16[1024,3072]{1,0:T(8,128)(2,1)} %add_convert_fusion.q_ref.k_ref.v_ref, bf16[1024,3072]{1,0:T(8,128)(2,1)} %add_convert_fusion.q_ref.k_ref.v_ref, ...), custom_call_target="tpu_custom_call" | custom-call | tf_op jit(solution)/shard_map/attend/pallas_call | solution.py:438
  144.1 5.8 %fusion.124 = (bf16[1024,512]{1,0:T(8,128)(2,1)}, bf16[1024,512]{1,0:T(8,128)(2,1)}, bf16[1024,512]{1,0:T(8,128)(2,1)}, bf16[1024,512]{1,0:T(8,128)(2,1)}, bf16[...) fusion(bf16[1024,3072]{1,0:T(8,128)(2,1)} %get-tuple-element.118), kind=kLoop, calls=%fused_computation.251 | loop fusion | bytes 12582912 | tf_op jit(solution)/shard_map/slice | solution.py:777
  149.9 3.7 fusion.50
  155.6 9.2 %place.4 = (bf16[1024,1024]{1,0:T(8,128)(2,1)}, bf16[1024,4096]{1,0:T(8,128)(2,1)}) custom-call(s32[4]{0:T(128)} %pad_add_fusion.where, bf16[4,32,5120]{2,1,0:T(8,128)(2,1)} %stack.68.refs_0_, bf16[4,32,5120]{2,1,0:T(8,128)(2,1)} %collective-permute-done.17.refs_1_, bf16[4,32,5120]{2,1,0:T(8,128)(2,1)} %collective-permute-done.18.refs_2_, ...), custom_call_target="tpu_custom_call" | custom-call | tf_op jit(solution)/shard_map/place/pallas_call | solution.py:206
  164.8 4.7 fusion.128
  172.3 30.5 %widen.1 = (bf16[1024,4096]{1,0:T(8,128)(2,1)}, bf16[1024,4096]{1,0:T(8,128)(2,1)}, bf16[1024,2048]{1,0:T(8,128)(2,1)}, bf16[1024,2048]{1,0:T(8,128)(2,1)}) custom-call(s32[4]{0:T(128)} %pad_add_fusion.where, bf16[1024,1024]{1,0:T(8,128)(2,1)} %add_convert_fusion.1.x_ref, bf16[1024,4096]{1,0:T(8,128)(2,1)} %get-tuple-element.128.w_ref, ...), custom_call_target="tpu_custom_call" | custom-call | tf_op jit(solution)/shard_map/widen/pallas_call | solution.py:580
  204.6 5.6 fusion.49
  210.1 3.7 fusion.48
  215.2 7.7 %place.5 = bf16[4096,1024]{1,0:T(8,128)(2,1)} custom-call(s32[4]{0:T(128)} %pad_add_fusion.where, bf16[4,128,1024]{2,1,0:T(8,128)(2,1)} %stack.69.refs_0_, bf16[4,128,1024]{2,1,0:T(8,128)(2,1)} %collective-permute-done.24.refs_1_, bf16[4,128,1024]{2,1,0:T(8,128)(2,1)} %collective-permute-done.25.refs_2_, ...), custom_call_target="tpu_custom_call" | custom-call | tf_op jit(solution)/shard_map/place/pallas_call | solution.py:206
  222.9 14.9 %fusion.129 = (f32[1024]{0:T(1024)S(1)}, f32[1024,1024]{1,0:T(8,128)S(1)}) fusion(f32[1024]{0:T(1024)S(1)} %get-tuple-element.221, f32[1024,1024]{1,0:T(8,128)} %copy-done.7, bf16[1024,4096]{1,0:T(8,128)(2,1)} %get-tuple-element.129, bf16[4096,1024]{1,0:T(8,128)(2,1)} %place.5), kind=kOutput, calls=%fused_computation.256 | convolution fusion | flops 8593079296 | bytes 25174016 | tf_op jit(solution)/shard_map/dot_general | solution.py:21
  244.2 3.1 multiply_reduce_fusion
  247.4 4.2 fusion.130
  251.7 6.4 %convolution_convert_fusion.4 = bf16[2048,1024]{1,0:T(8,128)(2,1)} fusion(bf16[1024,2048]{1,0:T(8,128)(2,1)S(1)} %copy-done.74, bf16[1024,1024]{1,0:T(8,128)(2,1)S(1)} %get-tuple-element.138), kind=kOutput, calls=%fused_computation.49 | convolution fusion | flops 4297064448 | bytes 10485760 | tf_op jit(solution)/shard_map/dot_general | solution.py:25
  260.8 8.4 %convolution_convert_fusion.3 = bf16[2048,1024]{1,0:T(8,128)(2,1)} fusion(bf16[1024,2048]{1,0:T(8,128)(2,1)} %get-tuple-element.136, bf16[1024,1024]{1,0:T(8,128)(2,1)S(1)} %get-tuple-element.138), kind=kOutput, calls=%fused_computation.48 | convolution fusion | flops 4297064448 | bytes 10485760 | tf_op jit(solution)/shard_map/dot_general | solution.py:25
  271.4 15.2 %multiply_convert_fusion = bf16[1024,4096]{1,0:T(8,128)(2,1)} fusion(bf16[1024,4096]{1,0:T(8,128)(2,1)} %get-tuple-element.130, bf16[1024,1024]{1,0:T(8,128)(2,1)S(1)} %get-tuple-element.138, bf16[4096,1024]{1,0:T(8,128)(2,1)} %place.5), kind=kOutput, calls=%fused_computation.1 | convolution fusion | flops 8610906112 | bytes 27262976 | tf_op jit(solution)/shard_map/dot_general | solution.py:31
  286.6 4.4 fusion.20
  292.4 6.6 %fold_inner.4 = (bf16[4,128,1024]{2,1,0:T(8,128)(2,1)}, bf16[4,128,1024]{2,1,0:T(8,128)(2,1)}, bf16[4,128,1024]{2,1,0:T(8,128)(2,1)}, bf16[4,128,1024]{2,1,0:T(8,128)(2,1)}) custom-call(s32[4]{0:T(128)} %pad_add_fusion.where, bf16[4,2,2,128,1024]{4,3,2,1,0:T(8,128)(2,1)} %bitcast.175, bf16[4,2,2,128,1024]{4,3,2,1,0:T(8,128)(2,1)} %collective-permute-done.33.refs_1_), custom_call_target="tpu_custom_call" | custom-call | tf_op jit(solution)/shard_map/fold_inner/pallas_call | solution.py:277
  302.5 9.7 %convolution_convert_fusion.2 = bf16[512,4096]{1,0:T(8,128)(2,1)} fusion(bf16[1024,4096]{1,0:T(8,128)(2,1)} %multiply_convert_fusion, bf16[1024,1024]{1,0:T(8,128)(2,1)S(1)} %copy-done.84), kind=kOutput, calls=%fused_computation.7 | convolution fusion | flops 4297064448 | bytes 13631488 | tf_op jit(solution)/shard_map/dot_general | solution.py:25
  312.2 15.9 %multiply_reduce_fusion.1 = (f32[1024]{0:T(1024)}, f32[1024]{0:T(1024)S(1)}, f32[1024]{0:T(1024)S(1)}, f32[1024]{0:T(1024)}, f32[1024,1024]{1,0:T(8,128)S(1)}) fusion(f32[1024,1024]{1,0:T(8,128)S(1)} %copy-done.8, f32[1024]{0:T(1024)S(1)} %copy-done.60, f32[1024]{0:T(1024)S(1)} %copy-done.48, f32[1024]{0:T(1024)S(1)} %copy-done.62, ...), kind=kOutput, calls=%fused_computation.31 | convolution fusion | flops 8599367680 | bytes 25194496 | tf_op jit(solution)/shard_map/dot_general | solution.py:31
  331.0 9.5 %convolution_convert_fusion.1 = bf16[512,4096]{1,0:T(8,128)(2,1)} fusion(bf16[1024,4096]{1,0:T(8,128)(2,1)} %multiply_convert_fusion, bf16[1024,1024]{1,0:T(8,128)(2,1)S(1)} %copy-done.85), kind=kOutput, calls=%fused_computation.6 | convolution fusion | flops 4297064448 | bytes 13631488 | tf_op jit(solution)/shard_map/dot_general | solution.py:25
  340.5 6.4 %fold_inner.5 = (bf16[4,32,4096]{2,1,0:T(8,128)(2,1)}, bf16[4,32,4096]{2,1,0:T(8,128)(2,1)}, bf16[4,32,4096]{2,1,0:T(8,128)(2,1)}, bf16[4,32,4096]{2,1,0:T(8,128)(2,1)}) custom-call(s32[4]{0:T(128)} %pad_add_fusion.where, bf16[4,2,2,32,4096]{4,3,2,1,0:T(8,128)(2,1)} %bitcast.176, bf16[4,2,2,32,4096]{4,3,2,1,0:T(8,128)(2,1)} %collective-permute-done.34.refs_1_), custom_call_target="tpu_custom_call" | custom-call | tf_op jit(solution)/shard_map/fold_inner/pallas_call | solution.py:277
  349.0 3.7 convolution_convert_fusion.11
  354.9 3.7 convolution_convert_fusion.9.do_ref
  360.0 17.8 %attend_back.2 = (bf16[1024,512]{1,0:T(8,128)(2,1)}, bf16[1024,512]{1,0:T(8,128)(2,1)}, bf16[1024,512]{1,0:T(8,128)(2,1)}) custom-call(s32[2,512,1]{2,1,0:T(8,128)} %copy.43.seg_col, s32[2,1,512]{2,1,0:T(1,128)} %broadcast_in_dim.19.seg_row, bf16[1024,3072]{1,0:T(8,128)(2,1)} %add_convert_fusion.q_ref.k_ref.v_ref, ...), custom_call_target="tpu_custom_call" | custom-call | tf_op jit(solution)/shard_map/attend_back/pallas_call | solution.py:492
  386.6 4.6 convert_reduce_fusion
  391.8 5.2 convolution_convert_fusion.7
  397.0 17.5 %attend_back.3 = (bf16[1024,512]{1,0:T(8,128)(2,1)}, bf16[1024,512]{1,0:T(8,128)(2,1)}, bf16[1024,512]{1,0:T(8,128)(2,1)}) custom-call(s32[2,512,1]{2,1,0:T(8,128)} %copy.43.seg_col, s32[2,1,512]{2,1,0:T(1,128)} %broadcast_in_dim.19.seg_row, bf16[1024,3072]{1,0:T(8,128)(2,1)} %add_convert_fusion.q_ref.k_ref.v_ref, ...), custom_call_target="tpu_custom_call" | custom-call | tf_op jit(solution)/shard_map/attend_back/pallas_call | solution.py:492
  420.4 6.0 %fold_outer.2 = (bf16[32,8192]{1,0:T(8,128)(2,1)}, bf16[32,8192]{1,0:T(8,128)(2,1)}, bf16[32,8192]{1,0:T(8,128)(2,1)}, bf16[32,8192]{1,0:T(8,128)(2,1)}) custom-call(s32[4]{0:T(128)} %pad_add_fusion.where, bf16[4,128,1024]{2,1,0:T(8,128)(2,1)} %get-tuple-element.166.refs_0_, bf16[4,128,1024]{2,1,0:T(8,128)(2,1)} %copy-done.24, ...), custom_call_target="tpu_custom_call" | custom-call | tf_op jit(solution)/shard_map/fold_outer/pallas_call | solution.py:277
  426.4 5.2 fold_inner.6
  431.6 4.2 convolution_convert_fusion.6
  441.7 4.9 convolution_convert_fusion.5
  447.0 5.0 fusion.22
  453.4 4.5 fold_inner.7
  459.8 7.3 %fusion.45 = f32[1024,1024]{1,0:T(8,128)S(1)} fusion(f32[1024,1024]{1,0:T(8,128)} %fusion.22, bf16[1024,1536]{1,0:T(8,128)(2,1)} %constant_dynamic-update-slice_fusion.5, bf16[1024,512]{1,0:T(8,128)(2,1)} %get-tuple-element.235, bf16[1024,512]{1,0:T(8,128)(2,1)} %get-tuple-element.236, bf16[1024,512]{1,0:T(8,128)(2,1)S(1)} %copy-done.19), kind=kOutput, calls=%fused_computation.87 | convolution fusion | flops 3231711232 | bytes 14680064 | tf_op jit(solution)/shard_map/dot_general | solution.py:31
  479.6 4.2 fusion.121
  484.6 3.5 collective-permute-start.53
  493.3 11.1 %collective-permute-done.53 = f32[24,1024]{1,0:T(8,128)S(1)} collective-permute-done((f32[24,1024]{1,0:T(8,128)S(1)}, f32[24,1024]{1,0:T(8,128)S(1)}, u32[]{:S(2)}, u32[]{:S(2)}) %collective-permute-start.53) | collective-permute-done | bytes 98336 | tf_op jit(solution)/shard_map/ppermute | solution.py:402
  515.0 5.9 %collective-permute-done.57.refs_7_ = bf16[4,32,1536]{2,1,0:T(8,128)(2,1)} collective-permute-done((bf16[4,32,1536]{2,1,0:T(8,128)(2,1)S(1)}, bf16[4,32,1536]{2,1,0:T(8,128)(2,1)}, u32[]{:S(2)}, u32[]{:S(2)}) %collective-permute-start.57) | collective-permute-done | bytes 393248 | tf_op jit(solution)/shard_map/ppermute | solution.py:98
  521.0 4.8 fold_outer.3
  525.8 3.4 collective-permute-start.59
  544.0 3.5 collective-permute-done.60
  549.9 5.3 maximum_select_fusion
  (422 shorter events, 176.3 us)
Async XLA Ops:
  7.3 18.2 %collective-permute-start.3 = (bf16[32,3328]{1,0:T(8,128)(2,1)S(1)}, bf16[32,3328]{1,0:T(8,128)(2,1)S(1)}, u32[]{:S(2)}, u32[]{:S(2)}) collective-permute-start(bf16[32,3328]{1,0:T(8,128)(2,1)S(1)} %fusion.85.refs_0_), channel_id=1, source_target_pairs={{0,24},{2,26},{4,28},{6,30},{8,0},{10,2},{12,4},{14,6},{16,8},{18,... | collective-permute-start | bytes 638984 | tf_op jit(solution)/shard_map/ppermute | solution.py:98
  7.4 18.1 %collective-permute-start.2 = (bf16[32,3328]{1,0:T(8,128)(2,1)S(1)}, bf16[32,3328]{1,0:T(8,128)(2,1)}, u32[]{:S(2)}, u32[]{:S(2)}) collective-permute-start(bf16[32,3328]{1,0:T(8,128)(2,1)S(1)} %fusion.85.refs_0_), channel_id=1, source_target_pairs={{0,16},{2,18},{4,20},{6,22},{8,24},{10,26},{12,28},{14,30},{16,0},... | collective-permute-start | bytes 638984 | tf_op jit(solution)/shard_map/ppermute | solution.py:98
  10.4 18.0 %collective-permute-start.1 = (bf16[32,3328]{1,0:T(8,128)(2,1)S(1)}, bf16[32,3328]{1,0:T(8,128)(2,1)}, u32[]{:S(2)}, u32[]{:S(2)}) collective-permute-start(bf16[32,3328]{1,0:T(8,128)(2,1)S(1)} %fusion.85.refs_0_), channel_id=1, source_target_pairs={{0,8},{2,10},{4,12},{6,14},{8,16},{10,18},{12,20},{14,22},{16,24},... | collective-permute-start | bytes 638984 | tf_op jit(solution)/shard_map/ppermute | solution.py:98
  12.9 22.1 %collective-permute-start.32 = (bf16[1,20,8,1024]{3,2,1,0:T(8,128)(2,1)}, bf16[1,20,8,1024]{3,2,1,0:T(8,128)(2,1)}, u32[]{:S(2)}, u32[]{:S(2)}) collective-permute-start(bf16[1,20,8,1024]{3,2,1,0:T(8,128)(2,1)} %param.42), channel_id=1, source_target_pairs={{0,1},{1,0},{2,3},{3,2},{4,5},{5,4},{6,7},{7,6},{8,9},{9,8},{10,11... | collective-permute-start | bytes 983048 | tf_op jit(solution)/shard_map/ppermute | solution.py:101
  14.2 59.7 %collective-permute-start = (bf16[2,256,1024]{2,1,0:T(8,128)(2,1)S(1)}, bf16[2,256,1024]{2,1,0:T(8,128)(2,1)S(1)}, u32[]{:S(2)}, u32[]{:S(2)}) collective-permute-start(bf16[2,256,1024]{2,1,0:T(8,128)(2,1)S(1)} %constant_dynamic-slice_fusion.3), channel_id=1, source_target_pairs={{0,1},{1,0},{2,3},{3,2},{4,5},{5,4},{6,7},{7,6},{8,9},{9,8},{10,11... | collective-permute-start | bytes 3145736 | tf_op jit(solution)/shard_map/ppermute | solution.py:101
  32.0 34.6 %collective-permute-start.6 = (bf16[4,32,3328]{2,1,0:T(8,128)(2,1)}, bf16[4,32,3328]{2,1,0:T(8,128)(2,1)}, u32[]{:S(2)}, u32[]{:S(2)}) collective-permute-start(bf16[4,32,3328]{2,1,0:T(8,128)(2,1)} %stack.67.refs_0_), channel_id=1, source_target_pairs={{0,6},{2,4},{4,2},{6,0},{8,14},{10,12},{12,10},{14,8},{16,22},{18,... | collective-permute-start | bytes 2555912 | tf_op jit(solution)/shard_map/ppermute | solution.py:98
  34.5 38.8 %collective-permute-start.5 = (bf16[4,32,3328]{2,1,0:T(8,128)(2,1)}, bf16[4,32,3328]{2,1,0:T(8,128)(2,1)}, u32[]{:S(2)}, u32[]{:S(2)}) collective-permute-start(bf16[4,32,3328]{2,1,0:T(8,128)(2,1)} %stack.67.refs_0_), channel_id=1, source_target_pairs={{0,4},{2,6},{4,0},{6,2},{8,12},{10,14},{12,8},{14,10},{16,20},{18,... | collective-permute-start | bytes 2555912 | tf_op jit(solution)/shard_map/ppermute | solution.py:98
  35.0 38.4 %collective-permute-start.4 = (bf16[4,32,3328]{2,1,0:T(8,128)(2,1)}, bf16[4,32,3328]{2,1,0:T(8,128)(2,1)}, u32[]{:S(2)}, u32[]{:S(2)}) collective-permute-start(bf16[4,32,3328]{2,1,0:T(8,128)(2,1)} %stack.67.refs_0_), channel_id=1, source_target_pairs={{0,2},{2,0},{4,6},{6,4},{8,10},{10,8},{12,14},{14,12},{16,18},{18,... | collective-permute-start | bytes 2555912 | tf_op jit(solution)/shard_map/ppermute | solution.py:98
  38.1 13.3 %collective-permute-start.8 = (bf16[32,5120]{1,0:T(8,128)(2,1)S(1)}, bf16[32,5120]{1,0:T(8,128)(2,1)S(1)}, u32[]{:S(2)}, u32[]{:S(2)}) collective-permute-start(bf16[32,5120]{1,0:T(8,128)(2,1)S(1)} %constant_dynamic-update-slice_fusion.refs_0_), channel_id=1, source_target_pairs={{0,16},{2,18},{4,20},{6,22},{8,24},{10,26},{12,28},{14,30},{16,0},... | collective-permute-start | bytes 983048 | tf_op jit(solution)/shard_map/ppermute | solution.py:98
  64.2 35.1 %collective-permute-start.19 = (bf16[4,32,5120]{2,1,0:T(8,128)(2,1)}, bf16[4,32,5120]{2,1,0:T(8,128)(2,1)}, u32[]{:S(2)}, u32[]{:S(2)}) collective-permute-start(bf16[4,32,5120]{2,1,0:T(8,128)(2,1)} %stack.68.refs_0_), channel_id=1, source_target_pairs={{0,6},{2,4},{4,2},{6,0},{8,14},{10,12},{12,10},{14,8},{16,22},{18,... | collective-permute-start | bytes 3932168 | tf_op jit(solution)/shard_map/ppermute | solution.py:98
  78.2 56.6 %collective-permute-start.16 = (bf16[128,1024]{1,0:T(8,128)(2,1)}, bf16[128,1024]{1,0:T(8,128)(2,1)S(1)}, u32[]{:S(2)}, u32[]{:S(2)}) collective-permute-start(bf16[128,1024]{1,0:T(8,128)(2,1)} %refs_0_.1), channel_id=1, source_target_pairs={{0,24},{2,26},{4,28},{6,30},{8,0},{10,2},{12,4},{14,6},{16,8},{18,... | collective-permute-start | bytes 786440 | tf_op jit(solution)/shard_map/ppermute | solution.py:98
  78.3 56.6 %collective-permute-start.15 = (bf16[128,1024]{1,0:T(8,128)(2,1)}, bf16[128,1024]{1,0:T(8,128)(2,1)}, u32[]{:S(2)}, u32[]{:S(2)}) collective-permute-start(bf16[128,1024]{1,0:T(8,128)(2,1)} %refs_0_.1), channel_id=1, source_target_pairs={{0,16},{2,18},{4,20},{6,22},{8,24},{10,26},{12,28},{14,30},{16,0},... | collective-permute-start | bytes 786440 | tf_op jit(solution)/shard_map/ppermute | solution.py:98
  81.2 56.5 %collective-permute-start.14 = (bf16[128,1024]{1,0:T(8,128)(2,1)}, bf16[128,1024]{1,0:T(8,128)(2,1)}, u32[]{:S(2)}, u32[]{:S(2)}) collective-permute-start(bf16[128,1024]{1,0:T(8,128)(2,1)} %refs_0_.1), channel_id=1, source_target_pairs={{0,8},{2,10},{4,12},{6,14},{8,16},{10,18},{12,20},{14,22},{16,24},... | collective-permute-start | bytes 786440 | tf_op jit(solution)/shard_map/ppermute | solution.py:98
  84.0 50.2 %collective-permute-start.18 = (bf16[4,32,5120]{2,1,0:T(8,128)(2,1)}, bf16[4,32,5120]{2,1,0:T(8,128)(2,1)}, u32[]{:S(2)}, u32[]{:S(2)}) collective-permute-start(bf16[4,32,5120]{2,1,0:T(8,128)(2,1)} %stack.68.refs_0_), channel_id=1, source_target_pairs={{0,4},{2,6},{4,0},{6,2},{8,12},{10,14},{12,8},{14,10},{16,20},{18,... | collective-permute-start | bytes 3932168 | tf_op jit(solution)/shard_map/ppermute | solution.py:98
  99.3 35.0 %collective-permute-start.17 = (bf16[4,32,5120]{2,1,0:T(8,128)(2,1)}, bf16[4,32,5120]{2,1,0:T(8,128)(2,1)}, u32[]{:S(2)}, u32[]{:S(2)}) collective-permute-start(bf16[4,32,5120]{2,1,0:T(8,128)(2,1)} %stack.68.refs_0_), channel_id=1, source_target_pairs={{0,2},{2,0},{4,6},{6,4},{8,10},{10,8},{12,14},{14,12},{16,18},{18,... | collective-permute-start | bytes 3932168 | tf_op jit(solution)/shard_map/ppermute | solution.py:98
  134.2 19.4 %collective-permute-start.20 = (bf16[4,32,5120]{2,1,0:T(8,128)(2,1)}, bf16[4,32,5120]{2,1,0:T(8,128)(2,1)}, u32[]{:S(2)}, u32[]{:S(2)}) collective-permute-start(bf16[4,32,5120]{2,1,0:T(8,128)(2,1)} %stack.68.refs_0_), channel_id=1, source_target_pairs={{0,1},{1,0},{2,3},{3,2},{4,5},{5,4},{6,7},{7,6},{8,9},{9,8},{10,11... | collective-permute-start | bytes 3932168 | tf_op jit(solution)/shard_map/ppermute | solution.py:101
  134.3 19.8 %collective-permute-start.21 = (bf16[4,32,5120]{2,1,0:T(8,128)(2,1)}, bf16[4,32,5120]{2,1,0:T(8,128)(2,1)}, u32[]{:S(2)}, u32[]{:S(2)}) collective-permute-start(bf16[4,32,5120]{2,1,0:T(8,128)(2,1)} %collective-permute-done.17.refs_1_), channel_id=1, source_target_pairs={{0,1},{1,0},{2,3},{3,2},{4,5},{5,4},{6,7},{7,6},{8,9},{9,8},{10,11... | collective-permute-start | bytes 3932168 | tf_op jit(solution)/shard_map/ppermute | solution.py:101
  134.8 20.8 %collective-permute-start.22 = (bf16[4,32,5120]{2,1,0:T(8,128)(2,1)}, bf16[4,32,5120]{2,1,0:T(8,128)(2,1)}, u32[]{:S(2)}, u32[]{:S(2)}) collective-permute-start(bf16[4,32,5120]{2,1,0:T(8,128)(2,1)} %collective-permute-done.18.refs_2_), channel_id=1, source_target_pairs={{0,1},{1,0},{2,3},{3,2},{4,5},{5,4},{6,7},{7,6},{8,9},{9,8},{10,11... | collective-permute-start | bytes 3932168 | tf_op jit(solution)/shard_map/ppermute | solution.py:101
  134.9 20.7 %collective-permute-start.23 = (bf16[4,32,5120]{2,1,0:T(8,128)(2,1)}, bf16[4,32,5120]{2,1,0:T(8,128)(2,1)}, u32[]{:S(2)}, u32[]{:S(2)}) collective-permute-start(bf16[4,32,5120]{2,1,0:T(8,128)(2,1)} %collective-permute-done.19.refs_3_), channel_id=1, source_target_pairs={{0,1},{1,0},{2,3},{3,2},{4,5},{5,4},{6,7},{7,6},{8,9},{9,8},{10,11... | collective-permute-start | bytes 3932168 | tf_op jit(solution)/shard_map/ppermute | solution.py:101
  141.6 61.2 %collective-permute-start.26 = (bf16[4,128,1024]{2,1,0:T(8,128)(2,1)}, bf16[4,128,1024]{2,1,0:T(8,128)(2,1)}, u32[]{:S(2)}, u32[]{:S(2)}) collective-permute-start(bf16[4,128,1024]{2,1,0:T(8,128)(2,1)} %stack.69.refs_0_), channel_id=1, source_target_pairs={{0,6},{2,4},{4,2},{6,0},{8,14},{10,12},{12,10},{14,8},{16,22},{18,... | collective-permute-start | bytes 3145736 | tf_op jit(solution)/shard_map/ppermute | solution.py:98
  153.6 49.2 %collective-permute-start.25 = (bf16[4,128,1024]{2,1,0:T(8,128)(2,1)}, bf16[4,128,1024]{2,1,0:T(8,128)(2,1)}, u32[]{:S(2)}, u32[]{:S(2)}) collective-permute-start(bf16[4,128,1024]{2,1,0:T(8,128)(2,1)} %stack.69.refs_0_), channel_id=1, source_target_pairs={{0,4},{2,6},{4,0},{6,2},{8,12},{10,14},{12,8},{14,10},{16,20},{18,... | collective-permute-start | bytes 3145736 | tf_op jit(solution)/shard_map/ppermute | solution.py:98
  154.1 48.7 %collective-permute-start.24 = (bf16[4,128,1024]{2,1,0:T(8,128)(2,1)}, bf16[4,128,1024]{2,1,0:T(8,128)(2,1)}, u32[]{:S(2)}, u32[]{:S(2)}) collective-permute-start(bf16[4,128,1024]{2,1,0:T(8,128)(2,1)} %stack.69.refs_0_), channel_id=1, source_target_pairs={{0,2},{2,0},{4,6},{6,4},{8,10},{10,8},{12,14},{14,12},{16,18},{18,... | collective-permute-start | bytes 3145736 | tf_op jit(solution)/shard_map/ppermute | solution.py:98
  202.8 11.0 %collective-permute-start.27 = (bf16[4,128,1024]{2,1,0:T(8,128)(2,1)}, bf16[4,128,1024]{2,1,0:T(8,128)(2,1)S(1)}, u32[]{:S(2)}, u32[]{:S(2)}) collective-permute-start(bf16[4,128,1024]{2,1,0:T(8,128)(2,1)} %stack.69.refs_0_), channel_id=1, source_target_pairs={{0,1},{1,0},{2,3},{3,2},{4,5},{5,4},{6,7},{7,6},{8,9},{9,8},{10,11... | collective-permute-start | bytes 3145736 | tf_op jit(solution)/shard_map/ppermute | solution.py:101
  202.9 10.9 %collective-permute-start.28 = (bf16[4,128,1024]{2,1,0:T(8,128)(2,1)}, bf16[4,128,1024]{2,1,0:T(8,128)(2,1)S(1)}, u32[]{:S(2)}, u32[]{:S(2)}) collective-permute-start(bf16[4,128,1024]{2,1,0:T(8,128)(2,1)} %collective-permute-done.24.refs_1_), channel_id=1, source_target_pairs={{0,1},{1,0},{2,3},{3,2},{4,5},{5,4},{6,7},{7,6},{8,9},{9,8},{10,11... | collective-permute-start | bytes 3145736 | tf_op jit(solution)/shard_map/ppermute | solution.py:101
  258.0 34.3 %collective-permute-start.33 = (bf16[4,2,2,128,1024]{4,3,2,1,0:T(8,128)(2,1)}, bf16[4,2,2,128,1024]{4,3,2,1,0:T(8,128)(2,1)}, u32[]{:S(2)}, u32[]{:S(2)}) collective-permute-start(bf16[4,2,2,128,1024]{4,3,2,1,0:T(8,128)(2,1)} %bitcast.16), channel_id=1, source_target_pairs={{0,1},{1,0},{2,3},{3,2},{4,5},{5,4},{6,7},{7,6},{8,9},{9,8},{10,11... | collective-permute-start | bytes 12582920 | tf_op jit(solution)/shard_map/ppermute | solution.py:101
  270.9 20.2 %collective-permute-start.31 = (bf16[20,8192]{1,0:T(8,128)(2,1)S(1)}, bf16[20,8192]{1,0:T(8,128)(2,1)}, u32[]{:S(2)}, u32[]{:S(2)}) collective-permute-start(bf16[20,8192]{1,0:T(8,128)(2,1)S(1)} %dynamic-slice_bitcast_fusion), channel_id=1, source_target_pairs={{0,1},{1,0},{2,3},{3,2},{4,5},{5,4},{6,7},{7,6},{8,9},{9,8},{10,11... | collective-permute-start | bytes 983048 | tf_op jit(solution)/shard_map/ppermute | solution.py:101
  299.0 59.6 %collective-permute-start.35 = (bf16[4,128,1024]{2,1,0:T(8,128)(2,1)}, bf16[4,128,1024]{2,1,0:T(8,128)(2,1)S(1)}, u32[]{:S(2)}, u32[]{:S(2)}) collective-permute-start(bf16[4,128,1024]{2,1,0:T(8,128)(2,1)} %get-tuple-element.140), channel_id=1, source_target_pairs={{0,2},{2,0},{4,6},{6,4},{8,10},{10,8},{12,14},{14,12},{16,18},{18,... | collective-permute-start | bytes 3145736 | tf_op jit(solution)/shard_map/ppermute | solution.py:98
  299.5 60.5 %collective-permute-start.36 = (bf16[4,128,1024]{2,1,0:T(8,128)(2,1)}, bf16[4,128,1024]{2,1,0:T(8,128)(2,1)}, u32[]{:S(2)}, u32[]{:S(2)}) collective-permute-start(bf16[4,128,1024]{2,1,0:T(8,128)(2,1)} %get-tuple-element.141), channel_id=1, source_target_pairs={{0,4},{2,6},{4,0},{6,2},{8,12},{10,14},{12,8},{14,10},{16,20},{18,... | collective-permute-start | bytes 3145736 | tf_op jit(solution)/shard_map/ppermute | solution.py:98
  301.0 59.0 %collective-permute-start.37 = (bf16[4,128,1024]{2,1,0:T(8,128)(2,1)}, bf16[4,128,1024]{2,1,0:T(8,128)(2,1)}, u32[]{:S(2)}, u32[]{:S(2)}) collective-permute-start(bf16[4,128,1024]{2,1,0:T(8,128)(2,1)} %get-tuple-element.142), channel_id=1, source_target_pairs={{0,6},{2,4},{4,2},{6,0},{8,14},{10,12},{12,10},{14,8},{16,22},{18,... | collective-permute-start | bytes 3145736 | tf_op jit(solution)/shard_map/ppermute | solution.py:98
  312.2 28.3 %collective-permute-start.34 = (bf16[4,2,2,32,4096]{4,3,2,1,0:T(8,128)(2,1)}, bf16[4,2,2,32,4096]{4,3,2,1,0:T(8,128)(2,1)}, u32[]{:S(2)}, u32[]{:S(2)}) collective-permute-start(bf16[4,2,2,32,4096]{4,3,2,1,0:T(8,128)(2,1)} %bitcast.18), channel_id=1, source_target_pairs={{0,1},{1,0},{2,3},{3,2},{4,5},{5,4},{6,7},{7,6},{8,9},{9,8},{10,11... | collective-permute-start | bytes 12582920 | tf_op jit(solution)/shard_map/ppermute | solution.py:101
  346.9 50.1 %collective-permute-start.38 = (bf16[4,32,4096]{2,1,0:T(8,128)(2,1)}, bf16[4,32,4096]{2,1,0:T(8,128)(2,1)}, u32[]{:S(2)}, u32[]{:S(2)}) collective-permute-start(bf16[4,32,4096]{2,1,0:T(8,128)(2,1)} %get-tuple-element.147), channel_id=1, source_target_pairs={{0,2},{2,0},{4,6},{6,4},{8,10},{10,8},{12,14},{14,12},{16,18},{18,... | collective-permute-start | bytes 3145736 | tf_op jit(solution)/shard_map/ppermute | solution.py:98
  347.5 49.5 %collective-permute-start.39 = (bf16[4,32,4096]{2,1,0:T(8,128)(2,1)}, bf16[4,32,4096]{2,1,0:T(8,128)(2,1)}, u32[]{:S(2)}, u32[]{:S(2)}) collective-permute-start(bf16[4,32,4096]{2,1,0:T(8,128)(2,1)} %get-tuple-element.148), channel_id=1, source_target_pairs={{0,4},{2,6},{4,0},{6,2},{8,12},{10,14},{12,8},{14,10},{16,20},{18,... | collective-permute-start | bytes 3145736 | tf_op jit(solution)/shard_map/ppermute | solution.py:98
  358.6 38.4 %collective-permute-start.40 = (bf16[4,32,4096]{2,1,0:T(8,128)(2,1)}, bf16[4,32,4096]{2,1,0:T(8,128)(2,1)}, u32[]{:S(2)}, u32[]{:S(2)}) collective-permute-start(bf16[4,32,4096]{2,1,0:T(8,128)(2,1)} %get-tuple-element.149), channel_id=1, source_target_pairs={{0,6},{2,4},{4,2},{6,0},{8,14},{10,12},{12,10},{14,8},{16,22},{18,... | collective-permute-start | bytes 3145736 | tf_op jit(solution)/shard_map/ppermute | solution.py:98
  385.4 41.0 %collective-permute-start.42 = (bf16[4,2,2,32,1536]{4,3,2,1,0:T(8,128)(2,1)}, bf16[4,2,2,32,1536]{4,3,2,1,0:T(8,128)(2,1)}, u32[]{:S(2)}, u32[]{:S(2)}) collective-permute-start(bf16[4,2,2,32,1536]{4,3,2,1,0:T(8,128)(2,1)} %bitcast.22), channel_id=1, source_target_pairs={{0,1},{1,0},{2,3},{3,2},{4,5},{5,4},{6,7},{7,6},{8,9},{9,8},{10,11... | collective-permute-start | bytes 4718600 | tf_op jit(solution)/shard_map/ppermute | solution.py:101
  386.1 40.3 %collective-permute-start.41 = (bf16[4,2,2,32,1024]{4,3,2,1,0:T(8,128)(2,1)S(1)}, bf16[4,2,2,32,1024]{4,3,2,1,0:T(8,128)(2,1)}, u32[]{:S(2)}, u32[]{:S(2)}) collective-permute-start(bf16[4,2,2,32,1024]{4,3,2,1,0:T(8,128)(2,1)S(1)} %bitcast.193), channel_id=1, source_target_pairs={{0,1},{1,0},{2,3},{3,2},{4,5},{5,4},{6,7},{7,6},{8,9},{9,8},{10,11... | collective-permute-start | bytes 3145736 | tf_op jit(solution)/shard_map/ppermute | solution.py:101
  435.7 16.2 %collective-permute-start.43 = (bf16[4,2,2,32,1536]{4,3,2,1,0:T(8,128)(2,1)S(1)}, bf16[4,2,2,32,1536]{4,3,2,1,0:T(8,128)(2,1)}, u32[]{:S(2)}, u32[]{:S(2)}) collective-permute-start(bf16[4,2,2,32,1536]{4,3,2,1,0:T(8,128)(2,1)S(1)} %bitcast.227), channel_id=1, source_target_pairs={{0,1},{1,0},{2,3},{3,2},{4,5},{5,4},{6,7},{7,6},{8,9},{9,8},{10,11... | collective-permute-start | bytes 4718600 | tf_op jit(solution)/shard_map/ppermute | solution.py:101
  436.2 89.6 %collective-permute-start.61 = (bf16[32,8192]{1,0:T(8,128)(2,1)}, bf16[32,8192]{1,0:T(8,128)(2,1)}, u32[]{:S(2)}, u32[]{:S(2)}) collective-permute-start(bf16[32,8192]{1,0:T(8,128)(2,1)} %get-tuple-element.175), channel_id=1, source_target_pairs={{0,8},{2,10},{4,12},{6,14},{8,16},{10,18},{12,20},{14,22},{16,24},... | collective-permute-start | bytes 1572872 | tf_op jit(solution)/shard_map/ppermute | solution.py:98
  438.4 90.8 %collective-permute-start.62 = (bf16[32,8192]{1,0:T(8,128)(2,1)}, bf16[32,8192]{1,0:T(8,128)(2,1)}, u32[]{:S(2)}, u32[]{:S(2)}) collective-permute-start(bf16[32,8192]{1,0:T(8,128)(2,1)} %get-tuple-element.176), channel_id=1, source_target_pairs={{0,16},{2,18},{4,20},{6,22},{8,24},{10,26},{12,28},{14,30},{16,0},... | collective-permute-start | bytes 1572872 | tf_op jit(solution)/shard_map/ppermute | solution.py:98
  439.7 27.6 %collective-permute-start.44 = (bf16[4,32,2560]{2,1,0:T(8,128)(2,1)}, bf16[4,32,2560]{2,1,0:T(8,128)(2,1)}, u32[]{:S(2)}, u32[]{:S(2)}) collective-permute-start(bf16[4,32,2560]{2,1,0:T(8,128)(2,1)} %get-tuple-element.163), channel_id=1, source_target_pairs={{0,2},{2,0},{4,6},{6,4},{8,10},{10,8},{12,14},{14,12},{16,18},{18,... | collective-permute-start | bytes 1966088 | tf_op jit(solution)/shard_map/ppermute | solution.py:98
  440.2 30.0 %collective-permute-start.45 = (bf16[4,32,2560]{2,1,0:T(8,128)(2,1)}, bf16[4,32,2560]{2,1,0:T(8,128)(2,1)}, u32[]{:S(2)}, u32[]{:S(2)}) collective-permute-start(bf16[4,32,2560]{2,1,0:T(8,128)(2,1)} %get-tuple-element.164), channel_id=1, source_target_pairs={{0,4},{2,6},{4,0},{6,2},{8,12},{10,14},{12,8},{14,10},{16,20},{18,... | collective-permute-start | bytes 1966088 | tf_op jit(solution)/shard_map/ppermute | solution.py:98
  452.0 19.9 %collective-permute-start.46 = (bf16[4,32,2560]{2,1,0:T(8,128)(2,1)}, bf16[4,32,2560]{2,1,0:T(8,128)(2,1)}, u32[]{:S(2)}, u32[]{:S(2)}) collective-permute-start(bf16[4,32,2560]{2,1,0:T(8,128)(2,1)} %get-tuple-element.165), channel_id=1, source_target_pairs={{0,6},{2,4},{4,2},{6,0},{8,14},{10,12},{12,10},{14,8},{16,22},{18,... | collective-permute-start | bytes 1966088 | tf_op jit(solution)/shard_map/ppermute | solution.py:98
  484.6 19.8 %collective-permute-start.53 = (f32[24,1024]{1,0:T(8,128)S(1)}, f32[24,1024]{1,0:T(8,128)S(1)}, u32[]{:S(2)}, u32[]{:S(2)}) collective-permute-start(f32[24,1024]{1,0:T(8,128)S(1)} %add_add_fusion.2), channel_id=1, source_target_pairs={{0,16},{2,18},{4,20},{6,22},{8,24},{10,26},{12,28},{14,30},{16,0},... | collective-permute-start | bytes 294920 | tf_op jit(solution)/shard_map/ppermute | solution.py:402
  488.1 17.1 %collective-permute-start.52 = (f32[24,1024]{1,0:T(8,128)S(1)}, f32[24,1024]{1,0:T(8,128)S(1)}, u32[]{:S(2)}, u32[]{:S(2)}) collective-permute-start(f32[24,1024]{1,0:T(8,128)S(1)} %add_add_fusion.2), channel_id=1, source_target_pairs={{0,8},{2,10},{4,12},{6,14},{8,0},{10,2},{12,4},{14,6},{16,24},{18,... | collective-permute-start | bytes 294920 | tf_op jit(solution)/shard_map/ppermute | solution.py:402
  492.4 39.0 %collective-permute-start.63 = (bf16[32,8192]{1,0:T(8,128)(2,1)}, bf16[32,8192]{1,0:T(8,128)(2,1)S(1)}, u32[]{:S(2)}, u32[]{:S(2)}) collective-permute-start(bf16[32,8192]{1,0:T(8,128)(2,1)} %get-tuple-element.177), channel_id=1, source_target_pairs={{0,24},{2,26},{4,28},{6,30},{8,0},{10,2},{12,4},{14,6},{16,8},{18,... | collective-permute-start | bytes 1572872 | tf_op jit(solution)/shard_map/ppermute | solution.py:98
  515.0 34.9 %collective-permute-start.47 = (f32[2,256,1024]{2,1,0:T(8,128)}, f32[2,256,1024]{2,1,0:T(8,128)}, u32[]{:S(2)}, u32[]{:S(2)}) collective-permute-start(f32[2,256,1024]{2,1,0:T(8,128)} %get-tuple-element.241), channel_id=1, source_target_pairs={{0,1},{1,0},{2,3},{3,2},{4,5},{5,4},{6,7},{7,6},{8,9},{9,8},{10,11... | collective-permute-start | bytes 6291464 | tf_op jit(solution)/shard_map/ppermute | solution.py:101
  525.7 15.4 %collective-permute-start.58 = (bf16[32,4096]{1,0:T(8,128)(2,1)}, bf16[32,4096]{1,0:T(8,128)(2,1)}, u32[]{:S(2)}, u32[]{:S(2)}) collective-permute-start(bf16[32,4096]{1,0:T(8,128)(2,1)} %get-tuple-element.197), channel_id=1, source_target_pairs={{0,8},{2,10},{4,12},{6,14},{8,16},{10,18},{12,20},{14,22},{16,24},... | collective-permute-start | bytes 786440 | tf_op jit(solution)/shard_map/ppermute | solution.py:98
  525.8 18.2 %collective-permute-start.59 = (bf16[32,4096]{1,0:T(8,128)(2,1)}, bf16[32,4096]{1,0:T(8,128)(2,1)}, u32[]{:S(2)}, u32[]{:S(2)}) collective-permute-start(bf16[32,4096]{1,0:T(8,128)(2,1)} %get-tuple-element.198), channel_id=1, source_target_pairs={{0,16},{2,18},{4,20},{6,22},{8,24},{10,26},{12,28},{14,30},{16,0},... | collective-permute-start | bytes 786440 | tf_op jit(solution)/shard_map/ppermute | solution.py:98
  529.2 18.2 %collective-permute-start.60 = (bf16[32,4096]{1,0:T(8,128)(2,1)}, bf16[32,4096]{1,0:T(8,128)(2,1)}, u32[]{:S(2)}, u32[]{:S(2)}) collective-permute-start(bf16[32,4096]{1,0:T(8,128)(2,1)} %get-tuple-element.199), channel_id=1, source_target_pairs={{0,24},{2,26},{4,28},{6,30},{8,0},{10,2},{12,4},{14,6},{16,8},{18,... | collective-permute-start | bytes 786440 | tf_op jit(solution)/shard_map/ppermute | solution.py:98
  (102 other events, 1762.2 us)

commit v4 on v3

--- a/solution.py
+++ b/solution.py
@@ -105,19 +105,23 @@
     return lax.optimization_barrier((values, hold))[0]
 
 
-def spans(widths, low, high):
-    found, start = [], 0
-    for i, width in enumerate(widths):
-        a, b = max(low, start), min(high, start + width)
-        if a < b:
-            found.append((i, a - start, b - start, a))
-        start += width
-    return found
-
-
 def stack_kernel(*refs):
     for i, ref in enumerate(refs[:-1]):
         refs[-1][i] = ref[...]
+
+
+def regroup(weight):
+    lane = 2 * HEAD_DIM
+    pairs = weight.shape[1] // (3 * lane)
+
+    def body(x_ref, out_ref):
+        for pair in range(pairs):
+            for i in range(3):
+                at, source = (pair * 3 + i) * lane, (i * pairs + pair) * lane
+                out_ref[:, at : at + lane] = x_ref[:, source : source + lane]
+
+    out = jax.ShapeDtypeStruct(weight.shape, weight.dtype)
+    return pl.pallas_call(body, out_shape=out, name="regroup")(weight)
 
 
 def place_kernel(n_parts, dims, chunk, widths):
@@ -242,16 +246,45 @@
     n = len(widths)
 
     def body(where, *refs):
-        for at, (up, right) in enumerate(
-            (a, b) for a in range(dims[1]) for b in range(dims[2])
-        ):
+        kept, came, outs = refs[:n], refs[n : 2 * n], refs[2 * n :]
+        early = pl.program_id(0) < dims[0] // 2
+
+        def write(out, up, right):
             y = lax.rem(where[1] + up, dims[1])
             x = lax.rem(where[2] + right, dims[2])
             start = 0
-            for i, width in enumerate(widths):
-                kept, came = refs[i][0, y, x], refs[n + i][0, y, x]
-                refs[2 * n + at][0, :, start : start + width] = kept + came
+            for a, b, width in zip(kept, came, widths):
+                out[0, :, start : start + width] = a[0, y, x] + b[0, y, x]
                 start += width
+
+        write(outs[0], 0, 0)
+        write(outs[1], 0, 1)
+        write(outs[2], 1, 0)
+
+        @pl.when(early)
+        def _():
+            write(outs[3], 1, 1)
+
+        @pl.when(jnp.logical_not(early))
+        def _():
+            write(outs[4], 1, 1)
+
+    return body
+
+
+def relay_kernel(k0):
+    def body(where, x_ref, y_ref, over_x, over_y, x_out, y_out):
+        early = pl.program_id(0) < k0 // 2
+
+        @pl.when(early)
+        def _():
+            x_out[...] = x_ref[...]
+            y_out[...] = y_ref[...] + over_x[...]
+
+        @pl.when(jnp.logical_not(early))
+        def _():
+            x_out[...] = x_ref[...] + over_y[...]
+            y_out[...] = y_ref[...]
 
     return body
 
@@ -278,7 +311,10 @@
         body,
         out_shape=out_shape,
         grid_spec=pltpu.PrefetchScalarGridSpec(
-            num_scalar_prefetch=1, grid=grid, in_specs=in_specs, out_specs=out_specs
+            num_scalar_prefetch=1,
+            grid=grid,
+            in_specs=in_specs,
+            out_specs=out_specs,
         ),
         name=name,
     )(wires.where, *args)
@@ -289,18 +325,19 @@
         self.wires = wires
         self.widths, self.kept, self.got, self.whole, self.terms = [], [], [], [], ()
 
-    def add(self, left, stay, go, right):
+    def add(self, left, stay, go, right, hold=()):
         wires = self.wires
         width = right.shape[1]
         self.m = left.shape[1] // (wires.count * 2)
-        self.plain = bool(self.m % 32 or width % 512)
+        square = wires.dims[1:] == (2, 2)
+        self.plain = bool(self.m % 32 or width % 512) or not square
         self.widths.append(width)
         if self.plain:
             self.whole.append(dot_first(left, right))
             return ()
         shape = (*wires.dims, self.m, width)
         send = dot_first(go, right).astype(BF).reshape(shape)
-        kept = dot_first(stay, gate(right, send)).astype(BF).reshape(shape)
+        kept = dot_first(stay, gate(right, (send, hold))).astype(BF).reshape(shape)
         self.kept.append(kept)
         self.got.append(wires.swap(send))
         return send, kept
@@ -311,19 +348,42 @@
         wires, m = self.wires, self.m
         k0, k1, k2 = wires.dims
         n = sum(self.widths)
+        half = k0 // 2
+        whole = pl.BlockSpec((1, m, n), lambda z, p: (z, 0, 0))
+        self.low = pl.BlockSpec((1, m, n), lambda z, p: (jnp.minimum(z, half - 1), 0, 0))
+        self.high = pl.BlockSpec((1, m, n), lambda z, p: (jnp.maximum(z - half, 0), 0, 0))
+        self.shape = jax.ShapeDtypeStruct((k0, m, n), BF)
+        part = jax.ShapeDtypeStruct((half, m, n), BF)
         outs = prefetched(
             wires,
             inner_fold_kernel(wires.dims, self.widths),
             (k0,),
             [pl.BlockSpec((1, k1, k2, m, w), lambda z, p: (z, 0, 0, 0, 0)) for w in self.widths] * 2,
-            [pl.BlockSpec((1, m, n), lambda z, p: (z, 0, 0))] * (k1 * k2),
-            [jax.ShapeDtypeStruct((k0, m, n), BF)] * (k1 * k2),
+            [whole, whole, whole, self.low, self.high],
+            [self.shape, self.shape, self.shape, part, part],
             [*self.kept, *self.got],
             "fold_inner",
         )
-        self.terms = [outs[0]] + [
-            wires.turn(o, 0, y, x) for o, (y, x) in zip(outs[1:], wires.planes[1:])
-        ]
+        self.parts = [*outs[:3], wires.turn(outs[3], 0, 0, 1), wires.turn(outs[4], 0, 1, 0)]
+        return outs
+
+    def relay(self):
+        if self.plain:
+            return ()
+        wires = self.wires
+        own, *rest = self.parts
+        whole = pl.BlockSpec((1, *self.shape.shape[1:]), lambda z, p: (z, 0, 0))
+        outs = prefetched(
+            wires,
+            relay_kernel(wires.dims[0]),
+            (wires.dims[0],),
+            [whole, whole, self.low, self.high],
+            [whole, whole],
+            [self.shape, self.shape],
+            rest,
+            "relay",
+        )
+        self.terms = [own, wires.turn(outs[0], 0, 0, 1), wires.turn(outs[1], 0, 1, 0)]
         return outs
 
 
@@ -332,7 +392,7 @@
         self.wires, self.groups = wires, groups
         self.plain = groups[0].plain
         if self.plain:
-            self.sends = ()
+            self.sends = self.terms = ()
             return
         k0 = wires.dims[0]
         self.tall = max(g.m for g in groups)
@@ -365,7 +425,7 @@
         self.sends = outs
         self.terms = [outs[0]] + [wires.turn(outs[r], r, 0, 0) for r in range(1, k0)]
 
-    def result(self, after=()):
+    def result(self, shapes, spots):
         if self.plain:
             both = ("rows", "seq")
             return [
@@ -373,20 +433,31 @@
                 for g in self.groups
                 for w in g.whole
             ]
-        terms = gate(self.terms, after) if after else self.terms
-        done = total_of(terms).reshape(self.rows, self.steps, sum(self.blocks))
-        outs, start = [], 0
-        for g, block in zip(self.groups, self.blocks):
-            part = done[:, :, start : start + block]
-            start += block
-            if g.m != self.rows:
-                outs.append(part.transpose(1, 0, 2).reshape(g.m, block))
-                continue
-            part, at = part.reshape(self.rows, block * self.steps), 0
-            for width in g.widths:
-                outs.append(part[:, at : at + width])
-                at += width
-        return outs
+        terms = self.terms
+        moves, lane = [], 2 * HEAD_DIM
+        for j in range(self.steps):
+            start, product = j * sum(self.blocks), 0
+            for g, block in zip(self.groups, self.blocks):
+                for c in range(0, block, lane):
+                    row, column, at = j * self.rows, c, product
+                    if g.m == self.rows:
+                        row, column = 0, j * block + c
+                        while column >= g.widths[at - product]:
+                            column -= g.widths[at - product]
+                            at += 1
+                    array, spot = spots[at]
+                    moves.append((start + c, array, row, spot(column)))
+                start += block
+                product += len(g.widths)
+
+        def body(*refs):
+            for source, array, row, column in moves:
+                piece = total_of([r[:, source : source + lane] for r in refs[: len(terms)]])
+                refs[len(terms) + array][row : row + self.rows, column : column + lane] = piece
+
+        return pl.pallas_call(
+            body, out_shape=[jax.ShapeDtypeStruct(x, F32) for x in shapes], name="finish"
+        )(*terms)
 
 
 def pick(value, index, axis):
@@ -407,7 +478,12 @@
     return value
 
 
-def attend_kernel(seg_col, seg_row, q_ref, k_ref, v_ref, mixed_ref, log_ref, bias_ref):
+def head_of(joined_ref, h):
+    starts = [(2 * i + h) * HEAD_DIM for i in range(3)]
+    return [joined_ref[:, start : start + HEAD_DIM] for start in starts]
+
+
+def attend_kernel(seg_col, seg_row, joined_ref, mixed_ref, log_ref, bias_ref):
     @pl.when(pl.program_id(1) == 0)
     def _():
         bias_ref[...] = jnp.where(seg_col[0] == seg_row[0], 0.0, NEGATIVE)
@@ -415,14 +491,13 @@
     scale = HEAD_DIM ** (-0.5)
     mixed = []
     for h in (0, 1):
-        span = slice(h * HEAD_DIM, (h + 1) * HEAD_DIM)
-        q = q_ref[:, span] * BF(scale)
-        scores = dot_second(k_ref[:, span], q) + bias_ref[...]
+        q, k, v = head_of(joined_ref, h)
+        scores = dot_second(k, q * BF(scale)) + bias_ref[...]
         largest = jnp.max(scores, axis=0, keepdims=True)
         exponent = jnp.exp(scores - largest)
         summed = jnp.sum(exponent, axis=0, keepdims=True)
         probs = (exponent * (1.0 / summed)).astype(BF)
-        mixed.append(dot_first(v_ref[:, span], probs))
+        mixed.append(dot_first(v, probs))
         log_ref[0, 0, h : h + 1, :] = largest + jnp.log(summed)
     mixed_ref[...] = jnp.concatenate(mixed, axis=0).T.astype(BF)
 
@@ -430,10 +505,6 @@
 def attend(joined, segments, first, pairs):
     rows, length = segments.shape
     lane = 2 * HEAD_DIM
-    all_pairs = joined.shape[1] // (3 * lane)
-
-    def block(start):
-        return pl.BlockSpec((length, lane), lambda r, h: (r, start + h))
 
     return pl.pallas_call(
         attend_kernel,
@@ -441,22 +512,23 @@
         in_specs=[
             pl.BlockSpec((1, length, 1), lambda r, h: (r, 0, 0)),
             pl.BlockSpec((1, 1, length), lambda r, h: (r, 0, 0)),
-            block(first),
-            block(all_pairs + first),
-            block(2 * all_pairs + first),
+            pl.BlockSpec((length, 3 * lane), lambda r, h: (r, first + h)),
         ],
-        out_specs=[block(0), pl.BlockSpec((1, 1, 2, length), lambda r, h: (r, h, 0, 0))],
+        out_specs=[
+            pl.BlockSpec((length, lane), lambda r, h: (r, h)),
+            pl.BlockSpec((1, 1, 2, length), lambda r, h: (r, h, 0, 0)),
+        ],
         out_shape=[
             jax.ShapeDtypeStruct((rows * length, pairs * lane), BF),
             jax.ShapeDtypeStruct((rows, pairs, 2, length), F32),
         ],
         scratch_shapes=[pltpu.VMEM((length, length), F32)],
         name="attend",
-    )(segments[:, :, None], segments[:, None, :], joined, joined, joined)
+    )(segments[:, :, None], segments[:, None, :], joined)
 
 
 def attend_back_kernel(
-    seg_col, seg_row, q_ref, k_ref, v_ref, log_ref, do_ref, dq_ref, dk_ref, dv_ref, bias_ref
+    seg_col, seg_row, joined_ref, log_ref, do_ref, grad_ref, bias_ref
 ):
     @pl.when(pl.program_id(1) == 0)
     def _():
@@ -466,46 +538,46 @@
     grads = []
     for h in (0, 1):
         span = slice(h * HEAD_DIM, (h + 1) * HEAD_DIM)
-        q = q_ref[:, span] * BF(scale)
-        k = k_ref[:, span]
+        q, k, v = head_of(joined_ref, h)
+        q = q * BF(scale)
         do = do_ref[:, span]
         scores = dot_second(k, q) + bias_ref[...]
         probs = jnp.exp(scores - log_ref[0, 0, h : h + 1, :])
-        grad_probs = dot_second(v_ref[:, span], do)
+        grad_probs = dot_second(v, do)
         inner = jnp.sum(probs * grad_probs, axis=0, keepdims=True)
         grad_scores = (probs * (grad_probs - inner)).astype(BF)
-        dv_ref[:, span] = dot_plain(probs.astype(BF), do).astype(BF)
-        dk_ref[:, span] = dot_plain(grad_scores, q).astype(BF)
+        lane = 2 * HEAD_DIM
+        k_span = slice(lane + h * HEAD_DIM, lane + (h + 1) * HEAD_DIM)
+        v_span = slice(2 * lane + h * HEAD_DIM, 2 * lane + (h + 1) * HEAD_DIM)
+        grad_ref[:, v_span] = dot_plain(probs.astype(BF), do).astype(BF)
+        grad_ref[:, k_span] = dot_plain(grad_scores, q).astype(BF)
         grads.append(dot_first(k, grad_scores) * scale)
-    dq_ref[...] = jnp.concatenate(grads, axis=0).T.astype(BF)
+    grad_ref[:, : 2 * HEAD_DIM] = jnp.concatenate(grads, axis=0).T.astype(BF)
 
 
 def attend_back(joined, logs, grad_mixed, segments, first, pairs):
     rows, length = segments.shape
     lane = 2 * HEAD_DIM
-    all_pairs = joined.shape[1] // (3 * lane)
-
-    def block(start):
-        return pl.BlockSpec((length, lane), lambda r, h: (r, start + h))
-
-    out = jax.ShapeDtypeStruct((rows * length, pairs * lane), BF)
     return pl.pallas_call(
         attend_back_kernel,
         grid=(rows, pairs),
         in_specs=[
             pl.BlockSpec((1, length, 1), lambda r, h: (r, 0, 0)),
             pl.BlockSpec((1, 1, length), lambda r, h: (r, 0, 0)),
-            block(first),
-            block(all_pairs + first),
-            block(2 * all_pairs + first),
+            pl.BlockSpec((length, 3 * lane), lambda r, h: (r, first + h)),
             pl.BlockSpec((1, 1, 2, length), lambda r, h: (r, h, 0, 0)),
-            block(first),
+            pl.BlockSpec((length, lane), lambda r, h: (r, first + h)),
         ],
-        out_specs=[block(0), block(0), block(0)],
-        out_shape=[out, out, out],
+        out_specs=pl.BlockSpec((length, 3 * lane), lambda r, h: (r, h)),
+        out_shape=jax.ShapeDtypeStruct((rows * length, 3 * pairs * lane), BF),
         scratch_shapes=[pltpu.VMEM((length, length), F32)],
         name="attend_back",
-    )(segments[:, :, None], segments[:, None, :], joined, joined, joined, logs, grad_mixed)
+        cost_estimate=pl.CostEstimate(
+            flops=3 * 40 * rows * pairs * length * length * HEAD_DIM,
+            transcendentals=3 * 2 * rows * pairs * length * length,
+            bytes_accessed=3 * 16 * rows * length * pairs * lane,
+        ),
+    )(segments[:, :, None], segments[:, None, :], joined, logs, grad_mixed)
 
 
 ERF_TOP = (
@@ -635,7 +707,7 @@
     vectors += [ln2_gain, ln2_bias, fc2_bias, fc1_bias]
     small = jnp.concatenate(vectors).reshape(8 + wide, m)
     n_small = small.shape[0]
-    pad_cols = 256
+    pad_cols = 128
     small_cols = jnp.pad(small.T, ((0, 0), (0, pad_cols - n_small)))
 
     def other_rows(value):
@@ -650,7 +722,7 @@
     second = jnp.where(seq == 0, came, mine)
     inputs_low = jnp.concatenate([first, second], axis=1).reshape(count_tok, width)
     grad_came = wires.swap(out_grad)
-    ga = Gather(wires, [qkv_weight, small_cols])
+    ga = Gather(wires, [regroup(qkv_weight), small_cols])
     gc = Gather(wires, [out_weight, fc1_weight])
     gd = Gather(wires, [fc2_weight])
     ga.step()
@@ -660,11 +732,12 @@
     gc.step(ga.sends)
     ga.step(gc.sends)
     qkv_full, small_all = ga.result()
-    small_full = small_all[:, :128].T[:n_small].astype(F32)
+    small_full = small_all.T[:n_small].astype(F32)
     norm1_gain, norm1_shift, q_shift, v_shift, out_shift, norm2_gain, norm2_shift, fc2_shift = [
         small_full[i] for i in range(8)
     ]
     fc1_shift = small_full[8:n_small].reshape(wide, devices, m).transpose(1, 0, 2).reshape(ff)
+    inputs_low = gate(inputs_low, grad_came)
     seg = own_rows(segments)
     seg_flat = seg.reshape(count_tok)
     mask = (seg_flat >= 0).astype(F32)
@@ -672,10 +745,12 @@
     inputs = inputs_low.astype(F32)
     normed1, inverse1 = norm_stats(inputs)
     attn_in = (normed1 * norm1_gain + norm1_shift).astype(BF)
+    attn_in = gate(attn_in, gd.flight)
     qkv_out = dot_plain(attn_in, qkv_full)
-    joined_shift = jnp.concatenate([q_shift, jnp.zeros_like(q_shift), v_shift])
+    pairs = width // (4 * HEAD_DIM)
+    joined_shift = jnp.stack([q_shift, jnp.zeros_like(q_shift), v_shift])
+    joined_shift = joined_shift.reshape(3, 2 * pairs, 2 * HEAD_DIM).transpose(1, 0, 2).reshape(3 * width)
     joined = (qkv_out + joined_shift).astype(BF)
-    pairs = width // (4 * HEAD_DIM)
     mixed, logs = attend(joined, seg, 0, 2 * pairs)
     gc.step((mixed,))
     gd.step(gc.sends)
@@ -741,54 +816,46 @@
     grad_fc2_shift = jnp.sum(grad_branch2.astype(F32), axis=0)
     grad_activ = dot_second(grad_branch2, fc2_full).astype(BF)
     grad_hidden = (grad_activ.astype(F32) * slope.astype(F32)).astype(BF)
-    grad_hidden = gate(grad_hidden, s_fc2.inner())
+    grad_hidden = gate(grad_hidden, (s_fc2.inner(), pooled, grad_fc2_shift, grad_maps_weight))
     s_fc1 = Scatter(wires)
     grad_hidden = gate(grad_hidden, s_fc1.add(mlp_in, *halves(wires, mlp_in), grad_hidden)[:1])
     grad_fc1_shift = jnp.sum(grad_hidden.astype(F32), axis=0)
+    grad_hidden = gate(grad_hidden, s_fc2.relay())
     grad_normed2 = dot_second(grad_hidden, fc1_full)
     back_two, grad_norm2_gain, grad_norm2_shift = norm_backward(
         grad_normed2, normed2, inverse2, norm2_gain
     )
     grad_resid1 = grad_resid2 + back_two
     grad_branch1 = grad_resid1.astype(BF)
-    grad_branch1 = gate(grad_branch1, s_fc1.inner())
+    grad_branch1 = gate(grad_branch1, (s_fc1.inner(), grad_fc1_shift))
     s_a = Scatter(wires)
     sent = s_a.add(mixed, *halves(wires, mixed), grad_branch1)
     grad_out_shift = jnp.sum(grad_branch1.astype(F32), axis=0)
     grad_branch1 = gate(grad_branch1, sent)
     grad_mixed = dot_second(grad_branch1, out_full).astype(BF)
-    grad_mixed = gate(grad_mixed, s_fc2.terms)
-    dq_a, dk_a, dv_a = attend_back(joined, logs[:, :pairs], grad_mixed, seg, 0, pairs)
-    grad_a = jnp.concatenate([dq_a, dk_a, dv_a], axis=1)
+    grad_mixed = gate(grad_mixed, (s_fc2.terms, grad_out_shift, s_fc1.relay()))
+    grad_a = attend_back(joined, logs[:, :pairs], grad_mixed, seg, 0, pairs)
     attn_stay, attn_go = halves(wires, attn_in)
     sent = s_a.add(attn_in, attn_stay, attn_go, grad_a)
     grad_mixed = gate(grad_mixed, (sent, s_fc1.terms))
-    dq_b, dk_b, dv_b = attend_back(joined, logs[:, pairs:], grad_mixed, seg, pairs, pairs)
-    grad_b = jnp.concatenate([dq_b, dk_b, dv_b], axis=1)
+    grad_b = attend_back(joined, logs[:, pairs:], grad_mixed, seg, pairs, pairs)
     z_one = Outer(wires, [s_fc2, s_fc1], (grad_b,))
     grad_b = gate(grad_b, (s_a.inner(), z_one.sends))
     s_b = Scatter(wires)
     sent = s_b.add(attn_in, attn_stay, attn_go, grad_b)
     grad_a, grad_b = gate((grad_a, grad_b), sent)
-    half = pairs * 2 * HEAD_DIM
-
-    def normed1_part(grads, c):
-        cuts = [slice(i * width + c * half, i * width + (c + 1) * half) for i in range(3)]
-        return dot_second(grads, jnp.concatenate([qkv_full[:, cut] for cut in cuts], axis=1))
-
-    grad_normed1 = normed1_part(grad_a, 0)
-    grad_b = gate(grad_b, (s_b.inner(), grad_normed1))
-    grad_normed1 = grad_normed1 + normed1_part(grad_b, 1)
-    grad_normed1 = gate(grad_normed1, s_a.terms)
+    part = 6 * pairs * HEAD_DIM
+    grad_a = gate(grad_a, s_a.relay())
+    grad_normed1 = dot_second(grad_a, qkv_full[:, :part])
+    grad_b = gate(grad_b, (s_b.inner(), grad_normed1, z_one.terms))
+    grad_normed1 = grad_normed1 + dot_second(grad_b, qkv_full[:, part:])
+    grad_normed1 = gate(grad_normed1, (s_a.terms, s_b.relay()))
     back_one, grad_norm1_gain, grad_norm1_shift = norm_backward(
         grad_normed1, normed1, inverse1, norm1_gain
     )
-    sum_q, sum_v = [
-        jnp.concatenate(
-            [jnp.sum(g[:, i * half : (i + 1) * half].astype(F32), axis=0) for g in (grad_a, grad_b)]
-        )
-        for i in (0, 2)
-    ]
+    sums_here = jnp.concatenate([jnp.sum(g.astype(F32), axis=0) for g in (grad_a, grad_b)])
+    sums_here = sums_here.reshape(2 * pairs, 3, 2 * HEAD_DIM)
+    sum_q, sum_v = sums_here[:, 0].reshape(width), sums_here[:, 2].reshape(width)
     little = jnp.concatenate(
         [
             jnp.stack(
@@ -811,18 +878,9 @@
         ],
         axis=0,
     )
-    little = sum_everywhere(wires, jnp.pad(little, ((0, -little.shape[0] % 8), (0, 0))))
-    z_two = Outer(wires, [s_a, s_b], (back_one,))
-    done_fc2, done_fc1 = z_one.result(z_two.sends)
-    done_out, done_a, done_b = z_two.result()
-    done_qkv = jnp.concatenate(
-        [d[:, i * half : (i + 1) * half] for i in range(3) for d in (done_a, done_b)], axis=1
-    )
-    place = lax.axis_index("rows") * 2 + seq
-    held = lax.dynamic_slice_in_dim(little[:8], place * m, m, 1)
-    held_fc1 = lax.dynamic_slice_in_dim(
-        little[11 + NTOK : 11 + NTOK + wide].reshape(ff), place * wide * m, wide * m, 0
-    )
+    z_two = Outer(wires, [s_a, s_b])
+    little = jnp.pad(little, ((0, -little.shape[0] % 8), (0, 0)))
+    little = sum_everywhere(wires, gate(little, z_two.sends))
     grad_rows = (grad_resid1 + back_one).reshape(rows_here, row_len, width)
     grad_away = lax.dynamic_slice_in_dim(grad_rows, (1 - seq) * slots_half, slots_half, 1)
     grad_back = wires.swap(grad_away)
@@ -831,6 +889,33 @@
         seq == 0,
         jnp.concatenate([grad_kept, grad_back], axis=0),
         jnp.concatenate([grad_back, grad_kept], axis=0),
+    )
+    z_two.terms = gate(z_two.terms, grad_held)
+    lane = 2 * HEAD_DIM
+
+    def same(column):
+        return column
+
+    def spread(first):
+        return lambda column: (
+            column // lane % 3 * width + (first + column // (3 * lane)) * lane + column % lane
+        )
+
+    z_one.terms = gate(z_one.terms, z_two.sends)
+    done_fc2, done_fc1 = z_one.result(
+        [(wide * m, width), (m, ff)], [(0, same), (1, same)]
+    )
+    done_two = z_two.result(
+        [(m, width), (m, 3 * width)], [(0, same), (1, spread(0)), (1, spread(pairs))]
+    )
+    done_out, done_qkv = done_two[0], done_two[1]
+    if z_two.plain:
+        done_qkv = jnp.concatenate(done_two[1:], axis=1).reshape(m, 2 * pairs, 3, lane)
+        done_qkv = done_qkv.transpose(0, 2, 1, 3).reshape(m, 3 * width)
+    place = lax.axis_index("rows") * 2 + seq
+    held = lax.dynamic_slice_in_dim(little[:8], place * m, m, 1)
+    held_fc1 = lax.dynamic_slice_in_dim(
+        little[11 + NTOK : 11 + NTOK + wide].reshape(ff), place * wide * m, wide * m, 0
     )
     return (
         pooled,

time: 565 us -> 570 us (level)
  the two profiles are of different devices: /device:TPU:8 before, /device:TPU:0 now
where the time goes in v4:
time: 570 us; the launch traced here: 559 us
  Pallas kernels  179 us (31%)
  matrix products  172 us (30%)
  starting transfers between devices  65 us (11%)
  waiting for transfers between devices  64.7 us (11%)
  local copies, waits for them, and re-layouts  43.7 us (8%)
  other arithmetic  33 us (6%)
    dot_general x13, matrix products, dot_first(): lax.dot_general(a, b, (((0,), (0,)), ((), ())), precision=precision, pref...  63.4 us
    dot_general x7, matrix products, dot_second(): lax.dot_general(a, b, (((1,), (1,)), ((), ())), precision=precision, pref...  54.7 us
    dot_general x9, matrix products, dot_plain(): return jnp.dot(a, b, precision=precision, preferred_element_type=F32)  53.8 us
    ppermute x40, starting transfers between devices, turn(): return lax.ppermute(value, 'rows', rotation(self.dims, (z, y, x)))  52 us
    pallas_call x10, Pallas kernels, prefetched(): pl.pallas_call(body, out_shape=out_shape, grid_spec=pltpu.PrefetchScalarG...  51 us
    ppermute x40, waiting for transfers between devices, turn(): return lax.ppermute(value, 'rows', rotation(self.dims, (z, y, x)))  46 us
    pallas_call x2, Pallas kernels, attend_back(): pl.pallas_call(attend_back_kernel, grid=(rows, pairs), in_specs=[pl.Block...  35.6 us
    pallas_call x1, Pallas kernels, widen(): pl.pallas_call(widen_kernel(128, chunk), out_shape=[out, out, part, part]...  30.7 us
  transfers between devices with their start and end apart: 68, of which 19 were waited for; matrix products, arithmetic and copies ran while one was open for 36% of the time, Pallas kernels for 29%

profile of v4, /device:TPU:0, one launch (start us, length us, event | category | flops | bytes accessed | tf_op | source)
XLA Modules:
  0.0 559.3 jit_solution(4924445602526703107)
XLA Ops:
  1.4 4.8 concatenate.36
  9.0 5.1 collective-permute-start.4
  43.8 13.4 %collective-permute-done.9.refs_2_ = bf16[32,5120]{1,0:T(8,128)(2,1)S(1)} collective-permute-done((bf16[32,5120]{1,0:T(8,128)(2,1)}, bf16[32,5120]{1,0:T(8,128)(2,1)S(1)}, u32[]{:S(2)}, u32[]{:S(2)}) %collective-permute-start.9) | collective-permute-done | bytes 327712 | tf_op jit(solution)/shard_map/ppermute | solution.py:98
  59.1 9.9 %collective-permute-done.8.refs_1_ = bf16[32,5120]{1,0:T(8,128)(2,1)} collective-permute-done((bf16[32,5120]{1,0:T(8,128)(2,1)}, bf16[32,5120]{1,0:T(8,128)(2,1)}, u32[]{:S(2)}, u32[]{:S(2)}) %collective-permute-start.8) | collective-permute-done | bytes 327712 | tf_op jit(solution)/shard_map/ppermute | solution.py:98
  83.9 6.8 %place.3 = (bf16[1024,3072]{1,0:T(8,128)(2,1)}, bf16[1024,128]{1,0:T(8,128)(2,1)}) custom-call(s32[4]{0:T(128)} %pad_add_fusion.where, bf16[4,32,3200]{2,1,0:T(8,128)(2,1)} %stack.63.refs_0_, bf16[4,32,3200]{2,1,0:T(8,128)(2,1)} %collective-permute-done.5.refs_1_, bf16[4,32,3200]{2,1,0:T(8,128)(2,1)} %collective-permute-done.6.refs_2_, ...), custom_call_target="tpu_custom_call" | custom-call | tf_op jit(solution)/shard_map/place/pallas_call | solution.py:210
  97.7 11.3 %add_convert_fusion.joined_ref = bf16[1024,3072]{1,0:T(8,128)(2,1)} fusion(f32[3072]{0:T(1024)S(1)} %add.257, bf16[1024,1024]{1,0:T(8,128)(2,1)S(1)} %fusion.8, bf16[1024,3072]{1,0:T(8,128)(2,1)} %get-tuple-element.130), kind=kOutput, calls=%fused_computation.2 | convolution fusion | flops 6448742400 | bytes 14692352 | tf_op jit(solution)/shard_map/dot_general | solution.py:21
  109.1 24.3 %attend.1 = (bf16[1024,1024]{1,0:T(8,128)(2,1)}, f32[2,8,2,512]{3,2,1,0:T(2,128)}) custom-call(s32[2,512,1]{2,1,0:T(8,128)} %copy.53.seg_col, s32[2,1,512]{2,1,0:T(1,128)} %broadcast_in_dim.17.seg_row, bf16[1024,3072]{1,0:T(8,128)(2,1)} %add_convert_fusion.joined_ref), custom_call_target="tpu_custom_call" | custom-call | tf_op jit(solution)/shard_map/attend/pallas_call | solution.py:509
  133.4 7.1 %collective-permute-done.19.refs_2_ = bf16[4,32,5120]{2,1,0:T(8,128)(2,1)} collective-permute-done((bf16[4,32,5120]{2,1,0:T(8,128)(2,1)}, bf16[4,32,5120]{2,1,0:T(8,128)(2,1)}, u32[]{:S(2)}, u32[]{:S(2)}) %collective-permute-start.19) | collective-permute-done | bytes 1310752 | tf_op jit(solution)/shard_map/ppermute | solution.py:98
  151.6 5.4 fusion.43
  158.8 9.2 %place.4 = (bf16[1024,1024]{1,0:T(8,128)(2,1)}, bf16[1024,4096]{1,0:T(8,128)(2,1)}) custom-call(s32[4]{0:T(128)} %pad_add_fusion.where, bf16[4,32,5120]{2,1,0:T(8,128)(2,1)} %stack.64.refs_0_, bf16[4,32,5120]{2,1,0:T(8,128)(2,1)} %collective-permute-done.18.refs_1_, bf16[4,32,5120]{2,1,0:T(8,128)(2,1)} %collective-permute-done.19.refs_2_, ...), custom_call_target="tpu_custom_call" | custom-call | tf_op jit(solution)/shard_map/place/pallas_call | solution.py:210
  168.0 4.7 fusion.116
  175.5 30.7 %widen.1 = (bf16[1024,4096]{1,0:T(8,128)(2,1)}, bf16[1024,4096]{1,0:T(8,128)(2,1)}, bf16[1024,2048]{1,0:T(8,128)(2,1)}, bf16[1024,2048]{1,0:T(8,128)(2,1)}) custom-call(s32[4]{0:T(128)} %pad_add_fusion.where, bf16[1024,1024]{1,0:T(8,128)(2,1)} %add_convert_fusion.1.x_ref, bf16[1024,4096]{1,0:T(8,128)(2,1)} %get-tuple-element.139.w_ref, ...), custom_call_target="tpu_custom_call" | custom-call | tf_op jit(solution)/shard_map/widen/pallas_call | solution.py:652
  207.9 5.5 fusion.42
  213.4 3.7 fusion.41
  218.4 7.7 %place.5 = bf16[4096,1024]{1,0:T(8,128)(2,1)} custom-call(s32[4]{0:T(128)} %pad_add_fusion.where, bf16[4,128,1024]{2,1,0:T(8,128)(2,1)} %stack.65.refs_0_, bf16[4,128,1024]{2,1,0:T(8,128)(2,1)} %collective-permute-done.25.refs_1_, bf16[4,128,1024]{2,1,0:T(8,128)(2,1)} %collective-permute-done.26.refs_2_, ...), custom_call_target="tpu_custom_call" | custom-call | tf_op jit(solution)/shard_map/place/pallas_call | solution.py:210
  226.2 14.6 %fusion.117 = (f32[1024]{0:T(1024)S(1)}, f32[1024,1024]{1,0:T(8,128)S(1)}) fusion(f32[1024]{0:T(1024)S(1)} %get-tuple-element.252, f32[1024,1024]{1,0:T(8,128)} %copy-done.5, bf16[1024,4096]{1,0:T(8,128)(2,1)} %get-tuple-element.140, bf16[4096,1024]{1,0:T(8,128)(2,1)} %place.5), kind=kOutput, calls=%fused_computation.225 | convolution fusion | flops 8593079296 | bytes 25174016 | tf_op jit(solution)/shard_map/dot_general | solution.py:21
  250.6 4.2 fusion.118
  254.9 6.4 %convolution_convert_fusion.4 = bf16[2048,1024]{1,0:T(8,128)(2,1)} fusion(bf16[1024,2048]{1,0:T(8,128)(2,1)S(1)} %copy-done.76, bf16[1024,1024]{1,0:T(8,128)(2,1)S(1)} %get-tuple-element.149), kind=kOutput, calls=%fused_computation.51 | convolution fusion | flops 4297064448 | bytes 10485760 | tf_op jit(solution)/shard_map/dot_general | solution.py:25
  265.9 8.4 %convolution_convert_fusion.3 = bf16[2048,1024]{1,0:T(8,128)(2,1)} fusion(bf16[1024,2048]{1,0:T(8,128)(2,1)} %get-tuple-element.147, bf16[1024,1024]{1,0:T(8,128)(2,1)S(1)} %get-tuple-element.149), kind=kOutput, calls=%fused_computation.50 | convolution fusion | flops 4297064448 | bytes 10485760 | tf_op jit(solution)/shard_map/dot_general | solution.py:25
  275.2 15.2 %multiply_convert_fusion = bf16[1024,4096]{1,0:T(8,128)(2,1)} fusion(bf16[1024,4096]{1,0:T(8,128)(2,1)} %get-tuple-element.141, bf16[1024,1024]{1,0:T(8,128)(2,1)S(1)} %get-tuple-element.149, bf16[4096,1024]{1,0:T(8,128)(2,1)} %place.5), kind=kOutput, calls=%fused_computation.1 | convolution fusion | flops 8610906112 | bytes 27262976 | tf_op jit(solution)/shard_map/dot_general | solution.py:31
  290.5 4.4 fusion.21
  296.0 6.6 %fold_inner.4 = (bf16[4,128,1024]{2,1,0:T(8,128)(2,1)}, bf16[4,128,1024]{2,1,0:T(8,128)(2,1)}, bf16[4,128,1024]{2,1,0:T(8,128)(2,1)}, bf16[2,128,1024]{2,1,0:T(8,128)(2,1)}, bf16[2,128,1024]{2,1,0:T(8,128)(2,1)}) custom-call(s32[4]{0:T(128)} %pad_add_fusion.where, bf16[4,2,2,128,1024]{4,3,2,1,0:T(8,128)(2,1)} %bitcast.148, ...), custom_call_target="tpu_custom_call" | custom-call | tf_op jit(solution)/shard_map/fold_inner/pallas_call | solution.py:310
  304.7 10.1 %convolution_convert_fusion.2 = bf16[512,4096]{1,0:T(8,128)(2,1)} fusion(bf16[1024,4096]{1,0:T(8,128)(2,1)} %multiply_convert_fusion, bf16[1024,1024]{1,0:T(8,128)(2,1)S(1)} %copy-done.86), kind=kOutput, calls=%fused_computation.12 | convolution fusion | flops 4297064448 | bytes 13631488 | tf_op jit(solution)/shard_map/dot_general | solution.py:25
  316.7 9.5 %convolution_convert_fusion.1 = bf16[512,4096]{1,0:T(8,128)(2,1)} fusion(bf16[1024,4096]{1,0:T(8,128)(2,1)} %multiply_convert_fusion, bf16[1024,1024]{1,0:T(8,128)(2,1)S(1)} %copy-done.86), kind=kOutput, calls=%fused_computation.11 | convolution fusion | flops 4297064448 | bytes 13631488 | tf_op jit(solution)/shard_map/dot_general | solution.py:25
  327.8 4.7 relay.4
  334.4 16.4 %multiply_reduce_fusion.1 = (f32[1024]{0:T(1024)}, f32[1024]{0:T(1024)S(1)}, f32[1024]{0:T(1024)S(1)}, f32[1024]{0:T(1024)}, f32[1024,1024]{1,0:T(8,128)S(1)}) fusion(f32[1024,1024]{1,0:T(8,128)} %copy-done.5, f32[1024]{0:T(1024)S(1)} %copy-done.60, f32[1024]{0:T(1024)S(1)} %copy-done.48, f32[1024]{0:T(1024)S(1)} %copy-done.58, ...), kind=kOutput, calls=%fused_computation.32 | convolution fusion | flops 8599367680 | bytes 25194496 | tf_op jit(solution)/shard_map/dot_general | solution.py:31
  353.7 6.6 %fold_inner.5 = (bf16[4,32,4096]{2,1,0:T(8,128)(2,1)}, bf16[4,32,4096]{2,1,0:T(8,128)(2,1)}, bf16[4,32,4096]{2,1,0:T(8,128)(2,1)}, bf16[2,32,4096]{2,1,0:T(8,128)(2,1)}, bf16[2,32,4096]{2,1,0:T(8,128)(2,1)}) custom-call(s32[4]{0:T(128)} %pad_add_fusion.where, bf16[4,2,2,32,4096]{4,3,2,1,0:T(8,128)(2,1)} %bitcast.147, ...), custom_call_target="tpu_custom_call" | custom-call | tf_op jit(solution)/shard_map/fold_inner/pallas_call | solution.py:310
  362.5 3.5 convolution_convert_fusion.11
  369.3 3.7 convolution_convert_fusion.9.do_ref
  375.8 4.7 relay.5
  382.4 17.6 %attend_back.2 = bf16[1024,1536]{1,0:T(8,128)(2,1)} custom-call(s32[2,512,1]{2,1,0:T(8,128)} %copy.53.seg_col, s32[2,1,512]{2,1,0:T(1,128)} %broadcast_in_dim.17.seg_row, bf16[1024,3072]{1,0:T(8,128)(2,1)} %add_convert_fusion.joined_ref, f32[2,4,2,512]{3,2,1,0:T(2,128)} %get-tuple-element.261.log_ref, bf16[1024,1024]{1,0:T(8,128)(2,1)} %convolution_convert_fusion.9.do_ref), custom_call_target="tpu_custom_call" | custom-call | flops 16106127360 | bytes 25165824 | tf_op jit(solution)/shard_map/attend_back/pallas_call | solution.py:561
  400.0 5.4 convolution_convert_fusion.8
  408.4 18.0 %attend_back.3 = bf16[1024,1536]{1,0:T(8,128)(2,1)} custom-call(s32[2,512,1]{2,1,0:T(8,128)} %copy.53.seg_col, s32[2,1,512]{2,1,0:T(1,128)} %broadcast_in_dim.17.seg_row, bf16[1024,3072]{1,0:T(8,128)(2,1)} %add_convert_fusion.joined_ref, f32[2,4,2,512]{3,2,1,0:T(2,128)} %get-tuple-element.260.log_ref, bf16[1024,1024]{1,0:T(8,128)(2,1)} %convolution_convert_fusion.9.do_ref), custom_call_target="tpu_custom_call" | custom-call | flops 16106127360 | bytes 25165824 | tf_op jit(solution)/shard_map/attend_back/pallas_call | solution.py:561
  426.5 5.4 fold_outer.2
  434.8 5.4 fold_inner.6
  442.3 4.2 convolution_convert_fusion.6
  451.5 4.4 relay.6
  459.4 8.3 %fusion.25 = f32[1024,1024]{1,0:T(8,128)} fusion(bf16[1024,1536]{1,0:T(8,128)(2,1)} %attend_back.2, bf16[1024,3072]{1,0:T(8,128)(2,1)} %get-tuple-element.130), kind=kOutput, calls=%fused_computation.59 | convolution fusion | flops 3221225472 | bytes 10485760 | tf_op jit(solution)/shard_map/dot_general | solution.py:31
  469.3 4.6 fold_inner.7
  475.9 7.6 %fusion.38 = f32[1024,1024]{1,0:T(8,128)} fusion(f32[1024,1024]{1,0:T(8,128)} %fusion.25, bf16[1024,1536]{1,0:T(8,128)(2,1)S(1)} %copy-done.11, bf16[1024,3072]{1,0:T(8,128)(2,1)} %get-tuple-element.130), kind=kOutput, calls=%fused_computation.77 | convolution fusion | flops 3222274048 | bytes 14680064 | tf_op jit(solution)/shard_map/dot_general | solution.py:31
  484.7 3.3 collective-permute-done.54.over_y
  488.7 4.1 relay.7
  495.1 3.7 fusion.13
  498.8 3.1 fusion.12
  505.7 4.6 fold_outer.3
  520.0 4.5 collective-permute-start.64
  532.1 12.9 %collective-permute-done.63 = f32[24,1024]{1,0:T(8,128)S(1)} collective-permute-done((f32[24,1024]{1,0:T(8,128)S(1)}, f32[24,1024]{1,0:T(8,128)S(1)}, u32[]{:S(2)}, u32[]{:S(2)}) %collective-permute-start.63) | collective-permute-done | bytes 98336 | tf_op jit(solution)/shard_map/ppermute | solution.py:473
  548.6 5.1 maximum_select_fusion
  (422 shorter events, 166.3 us)
Async XLA Ops:
  9.0 19.6 %collective-permute-start.4 = (bf16[32,3200]{1,0:T(8,128)(2,1)S(1)}, bf16[32,3200]{1,0:T(8,128)(2,1)}, u32[]{:S(2)}, u32[]{:S(2)}) collective-permute-start(bf16[32,3200]{1,0:T(8,128)(2,1)S(1)} %fusion.78.refs_0_), channel_id=1, source_target_pairs={{0,24},{2,26},{4,28},{6,30},{8,0},{10,2},{12,4},{14,6},{16,8},{18,... | collective-permute-start | bytes 614408 | tf_op jit(solution)/shard_map/ppermute | solution.py:98
  14.1 17.5 %collective-permute-start.3 = (bf16[32,3200]{1,0:T(8,128)(2,1)S(1)}, bf16[32,3200]{1,0:T(8,128)(2,1)}, u32[]{:S(2)}, u32[]{:S(2)}) collective-permute-start(bf16[32,3200]{1,0:T(8,128)(2,1)S(1)} %fusion.78.refs_0_), channel_id=1, source_target_pairs={{0,16},{2,18},{4,20},{6,22},{8,24},{10,26},{12,28},{14,30},{16,0},... | collective-permute-start | bytes 614408 | tf_op jit(solution)/shard_map/ppermute | solution.py:98
  14.1 17.5 %collective-permute-start.2 = (bf16[32,3200]{1,0:T(8,128)(2,1)S(1)}, bf16[32,3200]{1,0:T(8,128)(2,1)}, u32[]{:S(2)}, u32[]{:S(2)}) collective-permute-start(bf16[32,3200]{1,0:T(8,128)(2,1)S(1)} %fusion.78.refs_0_), channel_id=1, source_target_pairs={{0,8},{2,10},{4,12},{6,14},{8,16},{10,18},{12,20},{14,22},{16,24},... | collective-permute-start | bytes 614408 | tf_op jit(solution)/shard_map/ppermute | solution.py:98
  17.5 57.5 %collective-permute-start = (bf16[2,256,1024]{2,1,0:T(8,128)(2,1)}, bf16[2,256,1024]{2,1,0:T(8,128)(2,1)S(1)}, u32[]{:S(2)}, u32[]{:S(2)}) collective-permute-start(bf16[2,256,1024]{2,1,0:T(8,128)(2,1)} %constant_dynamic-slice_fusion.3), channel_id=1, source_target_pairs={{0,1},{1,0},{2,3},{3,2},{4,5},{5,4},{6,7},{7,6},{8,9},{9,8},{10,11... | collective-permute-start | bytes 3145736 | tf_op jit(solution)/shard_map/ppermute | solution.py:101
  35.5 36.0 %collective-permute-start.7 = (bf16[4,32,3200]{2,1,0:T(8,128)(2,1)}, bf16[4,32,3200]{2,1,0:T(8,128)(2,1)}, u32[]{:S(2)}, u32[]{:S(2)}) collective-permute-start(bf16[4,32,3200]{2,1,0:T(8,128)(2,1)} %stack.63.refs_0_), channel_id=1, source_target_pairs={{0,6},{2,4},{4,2},{6,0},{8,14},{10,12},{12,10},{14,8},{16,22},{18,... | collective-permute-start | bytes 2457608 | tf_op jit(solution)/shard_map/ppermute | solution.py:98
  38.0 36.4 %collective-permute-start.6 = (bf16[4,32,3200]{2,1,0:T(8,128)(2,1)}, bf16[4,32,3200]{2,1,0:T(8,128)(2,1)}, u32[]{:S(2)}, u32[]{:S(2)}) collective-permute-start(bf16[4,32,3200]{2,1,0:T(8,128)(2,1)} %stack.63.refs_0_), channel_id=1, source_target_pairs={{0,4},{2,6},{4,0},{6,2},{8,12},{10,14},{12,8},{14,10},{16,20},{18,... | collective-permute-start | bytes 2457608 | tf_op jit(solution)/shard_map/ppermute | solution.py:98
  38.5 36.0 %collective-permute-start.5 = (bf16[4,32,3200]{2,1,0:T(8,128)(2,1)}, bf16[4,32,3200]{2,1,0:T(8,128)(2,1)}, u32[]{:S(2)}, u32[]{:S(2)}) collective-permute-start(bf16[4,32,3200]{2,1,0:T(8,128)(2,1)} %stack.63.refs_0_), channel_id=1, source_target_pairs={{0,2},{2,0},{4,6},{6,4},{8,10},{10,8},{12,14},{14,12},{16,18},{18,... | collective-permute-start | bytes 2457608 | tf_op jit(solution)/shard_map/ppermute | solution.py:98
  40.5 16.6 %collective-permute-start.9 = (bf16[32,5120]{1,0:T(8,128)(2,1)}, bf16[32,5120]{1,0:T(8,128)(2,1)S(1)}, u32[]{:S(2)}, u32[]{:S(2)}) collective-permute-start(bf16[32,5120]{1,0:T(8,128)(2,1)} %constant_dynamic-update-slice_fusion.refs_0_), channel_id=1, source_target_pairs={{0,16},{2,18},{4,20},{6,22},{8,24},{10,26},{12,28},{14,30},{16,0},... | collective-permute-start | bytes 983048 | tf_op jit(solution)/shard_map/ppermute | solution.py:98
  57.2 11.9 %collective-permute-start.8 = (bf16[32,5120]{1,0:T(8,128)(2,1)}, bf16[32,5120]{1,0:T(8,128)(2,1)}, u32[]{:S(2)}, u32[]{:S(2)}) collective-permute-start(bf16[32,5120]{1,0:T(8,128)(2,1)} %constant_dynamic-update-slice_fusion.refs_0_), channel_id=1, source_target_pairs={{0,8},{2,10},{4,12},{6,14},{8,16},{10,18},{12,20},{14,22},{16,24},... | collective-permute-start | bytes 983048 | tf_op jit(solution)/shard_map/ppermute | solution.py:98
  71.5 24.7 %collective-permute-start.17 = (bf16[128,1024]{1,0:T(8,128)(2,1)}, bf16[128,1024]{1,0:T(8,128)(2,1)}, u32[]{:S(2)}, u32[]{:S(2)}) collective-permute-start(bf16[128,1024]{1,0:T(8,128)(2,1)} %refs_0_.1), channel_id=1, source_target_pairs={{0,24},{2,26},{4,28},{6,30},{8,0},{10,2},{12,4},{14,6},{16,8},{18,... | collective-permute-start | bytes 786440 | tf_op jit(solution)/shard_map/ppermute | solution.py:98
  77.1 20.6 %collective-permute-start.16 = (bf16[128,1024]{1,0:T(8,128)(2,1)S(1)}, bf16[128,1024]{1,0:T(8,128)(2,1)}, u32[]{:S(2)}, u32[]{:S(2)}) collective-permute-start(bf16[128,1024]{1,0:T(8,128)(2,1)S(1)} %copy-done.35), channel_id=1, source_target_pairs={{0,16},{2,18},{4,20},{6,22},{8,24},{10,26},{12,28},{14,30},{16,0},... | collective-permute-start | bytes 786440 | tf_op jit(solution)/shard_map/ppermute | solution.py:98
  79.2 18.5 %collective-permute-start.15 = (bf16[128,1024]{1,0:T(8,128)(2,1)S(1)}, bf16[128,1024]{1,0:T(8,128)(2,1)}, u32[]{:S(2)}, u32[]{:S(2)}) collective-permute-start(bf16[128,1024]{1,0:T(8,128)(2,1)S(1)} %copy-done.35), channel_id=1, source_target_pairs={{0,8},{2,10},{4,12},{6,14},{8,16},{10,18},{12,20},{14,22},{16,24},... | collective-permute-start | bytes 786440 | tf_op jit(solution)/shard_map/ppermute | solution.py:98
  80.9 52.5 %collective-permute-start.20 = (bf16[4,32,5120]{2,1,0:T(8,128)(2,1)}, bf16[4,32,5120]{2,1,0:T(8,128)(2,1)}, u32[]{:S(2)}, u32[]{:S(2)}) collective-permute-start(bf16[4,32,5120]{2,1,0:T(8,128)(2,1)} %stack.64.refs_0_), channel_id=1, source_target_pairs={{0,6},{2,4},{4,2},{6,0},{8,14},{10,12},{12,10},{14,8},{16,22},{18,... | collective-permute-start | bytes 3932168 | tf_op jit(solution)/shard_map/ppermute | solution.py:98
  82.6 57.9 %collective-permute-start.19 = (bf16[4,32,5120]{2,1,0:T(8,128)(2,1)}, bf16[4,32,5120]{2,1,0:T(8,128)(2,1)}, u32[]{:S(2)}, u32[]{:S(2)}) collective-permute-start(bf16[4,32,5120]{2,1,0:T(8,128)(2,1)} %stack.64.refs_0_), channel_id=1, source_target_pairs={{0,4},{2,6},{4,0},{6,2},{8,12},{10,14},{12,8},{14,10},{16,20},{18,... | collective-permute-start | bytes 3932168 | tf_op jit(solution)/shard_map/ppermute | solution.py:98
  96.2 44.3 %collective-permute-start.18 = (bf16[4,32,5120]{2,1,0:T(8,128)(2,1)}, bf16[4,32,5120]{2,1,0:T(8,128)(2,1)}, u32[]{:S(2)}, u32[]{:S(2)}) collective-permute-start(bf16[4,32,5120]{2,1,0:T(8,128)(2,1)} %stack.64.refs_0_), channel_id=1, source_target_pairs={{0,2},{2,0},{4,6},{6,4},{8,10},{10,8},{12,14},{14,12},{16,18},{18,... | collective-permute-start | bytes 3932168 | tf_op jit(solution)/shard_map/ppermute | solution.py:98
  140.5 16.4 %collective-permute-start.21 = (bf16[4,32,5120]{2,1,0:T(8,128)(2,1)}, bf16[4,32,5120]{2,1,0:T(8,128)(2,1)}, u32[]{:S(2)}, u32[]{:S(2)}) collective-permute-start(bf16[4,32,5120]{2,1,0:T(8,128)(2,1)} %stack.64.refs_0_), channel_id=1, source_target_pairs={{0,1},{1,0},{2,3},{3,2},{4,5},{5,4},{6,7},{7,6},{8,9},{9,8},{10,11... | collective-permute-start | bytes 3932168 | tf_op jit(solution)/shard_map/ppermute | solution.py:101
  140.5 17.7 %collective-permute-start.22 = (bf16[4,32,5120]{2,1,0:T(8,128)(2,1)}, bf16[4,32,5120]{2,1,0:T(8,128)(2,1)}, u32[]{:S(2)}, u32[]{:S(2)}) collective-permute-start(bf16[4,32,5120]{2,1,0:T(8,128)(2,1)} %collective-permute-done.18.refs_1_), channel_id=1, source_target_pairs={{0,1},{1,0},{2,3},{3,2},{4,5},{5,4},{6,7},{7,6},{8,9},{9,8},{10,11... | collective-permute-start | bytes 3932168 | tf_op jit(solution)/shard_map/ppermute | solution.py:101
  141.0 17.8 %collective-permute-start.23 = (bf16[4,32,5120]{2,1,0:T(8,128)(2,1)}, bf16[4,32,5120]{2,1,0:T(8,128)(2,1)}, u32[]{:S(2)}, u32[]{:S(2)}) collective-permute-start(bf16[4,32,5120]{2,1,0:T(8,128)(2,1)} %collective-permute-done.19.refs_2_), channel_id=1, source_target_pairs={{0,1},{1,0},{2,3},{3,2},{4,5},{5,4},{6,7},{7,6},{8,9},{9,8},{10,11... | collective-permute-start | bytes 3932168 | tf_op jit(solution)/shard_map/ppermute | solution.py:101
  141.0 17.8 %collective-permute-start.24 = (bf16[4,32,5120]{2,1,0:T(8,128)(2,1)}, bf16[4,32,5120]{2,1,0:T(8,128)(2,1)}, u32[]{:S(2)}, u32[]{:S(2)}) collective-permute-start(bf16[4,32,5120]{2,1,0:T(8,128)(2,1)} %collective-permute-done.20.refs_3_), channel_id=1, source_target_pairs={{0,1},{1,0},{2,3},{3,2},{4,5},{5,4},{6,7},{7,6},{8,9},{9,8},{10,11... | collective-permute-start | bytes 3932168 | tf_op jit(solution)/shard_map/ppermute | solution.py:101
  148.9 57.3 %collective-permute-start.27 = (bf16[4,128,1024]{2,1,0:T(8,128)(2,1)}, bf16[4,128,1024]{2,1,0:T(8,128)(2,1)}, u32[]{:S(2)}, u32[]{:S(2)}) collective-permute-start(bf16[4,128,1024]{2,1,0:T(8,128)(2,1)} %stack.65.refs_0_), channel_id=1, source_target_pairs={{0,6},{2,4},{4,2},{6,0},{8,14},{10,12},{12,10},{14,8},{16,22},{18,... | collective-permute-start | bytes 3145736 | tf_op jit(solution)/shard_map/ppermute | solution.py:98
  156.9 49.3 %collective-permute-start.26 = (bf16[4,128,1024]{2,1,0:T(8,128)(2,1)S(1)}, bf16[4,128,1024]{2,1,0:T(8,128)(2,1)}, u32[]{:S(2)}, u32[]{:S(2)}) collective-permute-start(bf16[4,128,1024]{2,1,0:T(8,128)(2,1)S(1)} %copy-done.10), channel_id=1, source_target_pairs={{0,4},{2,6},{4,0},{6,2},{8,12},{10,14},{12,8},{14,10},{16,20},{18,... | collective-permute-start | bytes 3145736 | tf_op jit(solution)/shard_map/ppermute | solution.py:98
  158.2 48.0 %collective-permute-start.25 = (bf16[4,128,1024]{2,1,0:T(8,128)(2,1)S(1)}, bf16[4,128,1024]{2,1,0:T(8,128)(2,1)}, u32[]{:S(2)}, u32[]{:S(2)}) collective-permute-start(bf16[4,128,1024]{2,1,0:T(8,128)(2,1)S(1)} %copy-done.10), channel_id=1, source_target_pairs={{0,2},{2,0},{4,6},{6,4},{8,10},{10,8},{12,14},{14,12},{16,18},{18,... | collective-permute-start | bytes 3145736 | tf_op jit(solution)/shard_map/ppermute | solution.py:98
  261.3 34.7 %collective-permute-start.33 = (bf16[4,2,2,128,1024]{4,3,2,1,0:T(8,128)(2,1)}, bf16[4,2,2,128,1024]{4,3,2,1,0:T(8,128)(2,1)}, u32[]{:S(2)}, u32[]{:S(2)}) collective-permute-start(bf16[4,2,2,128,1024]{4,3,2,1,0:T(8,128)(2,1)} %bitcast.18), channel_id=1, source_target_pairs={{0,1},{1,0},{2,3},{3,2},{4,5},{5,4},{6,7},{7,6},{8,9},{9,8},{10,11... | collective-permute-start | bytes 12582920 | tf_op jit(solution)/shard_map/ppermute | solution.py:101
  265.4 29.4 %collective-permute-start.32 = (bf16[20,8192]{1,0:T(8,128)(2,1)}, bf16[20,8192]{1,0:T(8,128)(2,1)S(1)}, u32[]{:S(2)}, u32[]{:S(2)}) collective-permute-start(bf16[20,8192]{1,0:T(8,128)(2,1)} %dynamic-slice_bitcast_fusion), channel_id=1, source_target_pairs={{0,1},{1,0},{2,3},{3,2},{4,5},{5,4},{6,7},{7,6},{8,9},{9,8},{10,11... | collective-permute-start | bytes 983048 | tf_op jit(solution)/shard_map/ppermute | solution.py:101
  302.5 23.6 %collective-permute-start.34 = (bf16[2,128,1024]{2,1,0:T(8,128)(2,1)}, bf16[2,128,1024]{2,1,0:T(8,128)(2,1)S(1)}, u32[]{:S(2)}, u32[]{:S(2)}) collective-permute-start(bf16[2,128,1024]{2,1,0:T(8,128)(2,1)} %get-tuple-element.153), channel_id=1, source_target_pairs={{0,2},{2,0},{4,6},{6,4},{8,10},{10,8},{12,14},{14,12},{16,18},{18,... | collective-permute-start | bytes 1572872 | tf_op jit(solution)/shard_map/ppermute | solution.py:98
  304.0 22.2 %collective-permute-start.35 = (bf16[2,128,1024]{2,1,0:T(8,128)(2,1)}, bf16[2,128,1024]{2,1,0:T(8,128)(2,1)S(1)}, u32[]{:S(2)}, u32[]{:S(2)}) collective-permute-start(bf16[2,128,1024]{2,1,0:T(8,128)(2,1)} %get-tuple-element.154), channel_id=1, source_target_pairs={{0,4},{2,6},{4,0},{6,2},{8,12},{10,14},{12,8},{14,10},{16,20},{18,... | collective-permute-start | bytes 1572872 | tf_op jit(solution)/shard_map/ppermute | solution.py:98
  314.8 38.9 %collective-permute-start.36 = (bf16[4,2,2,32,4096]{4,3,2,1,0:T(8,128)(2,1)}, bf16[4,2,2,32,4096]{4,3,2,1,0:T(8,128)(2,1)}, u32[]{:S(2)}, u32[]{:S(2)}) collective-permute-start(bf16[4,2,2,32,4096]{4,3,2,1,0:T(8,128)(2,1)} %bitcast.20), channel_id=1, source_target_pairs={{0,1},{1,0},{2,3},{3,2},{4,5},{5,4},{6,7},{7,6},{8,9},{9,8},{10,11... | collective-permute-start | bytes 12582920 | tf_op jit(solution)/shard_map/ppermute | solution.py:101
  332.5 49.9 %collective-permute-start.37 = (bf16[4,128,1024]{2,1,0:T(8,128)(2,1)}, bf16[4,128,1024]{2,1,0:T(8,128)(2,1)S(1)}, u32[]{:S(2)}, u32[]{:S(2)}) collective-permute-start(bf16[4,128,1024]{2,1,0:T(8,128)(2,1)} %get-tuple-element.157), channel_id=1, source_target_pairs={{0,2},{2,0},{4,6},{6,4},{8,10},{10,8},{12,14},{14,12},{16,18},{18,... | collective-permute-start | bytes 3145736 | tf_op jit(solution)/shard_map/ppermute | solution.py:98
  333.7 48.7 %collective-permute-start.38 = (bf16[4,128,1024]{2,1,0:T(8,128)(2,1)}, bf16[4,128,1024]{2,1,0:T(8,128)(2,1)}, u32[]{:S(2)}, u32[]{:S(2)}) collective-permute-start(bf16[4,128,1024]{2,1,0:T(8,128)(2,1)} %get-tuple-element.158), channel_id=1, source_target_pairs={{0,4},{2,6},{4,0},{6,2},{8,12},{10,14},{12,8},{14,10},{16,20},{18,... | collective-permute-start | bytes 3145736 | tf_op jit(solution)/shard_map/ppermute | solution.py:98
  360.3 14.0 %collective-permute-start.39 = (bf16[2,32,4096]{2,1,0:T(8,128)(2,1)}, bf16[2,32,4096]{2,1,0:T(8,128)(2,1)}, u32[]{:S(2)}, u32[]{:S(2)}) collective-permute-start(bf16[2,32,4096]{2,1,0:T(8,128)(2,1)} %get-tuple-element.164), channel_id=1, source_target_pairs={{0,2},{2,0},{4,6},{6,4},{8,10},{10,8},{12,14},{14,12},{16,18},{18,... | collective-permute-start | bytes 1572872 | tf_op jit(solution)/shard_map/ppermute | solution.py:98
  362.1 13.7 %collective-permute-start.40 = (bf16[2,32,4096]{2,1,0:T(8,128)(2,1)}, bf16[2,32,4096]{2,1,0:T(8,128)(2,1)}, u32[]{:S(2)}, u32[]{:S(2)}) collective-permute-start(bf16[2,32,4096]{2,1,0:T(8,128)(2,1)} %get-tuple-element.165), channel_id=1, source_target_pairs={{0,4},{2,6},{4,0},{6,2},{8,12},{10,14},{12,8},{14,10},{16,20},{18,... | collective-permute-start | bytes 1572872 | tf_op jit(solution)/shard_map/ppermute | solution.py:98
  366.0 68.8 %collective-permute-start.43 = (bf16[4,2,2,32,1024]{4,3,2,1,0:T(8,128)(2,1)}, bf16[4,2,2,32,1024]{4,3,2,1,0:T(8,128)(2,1)}, u32[]{:S(2)}, u32[]{:S(2)}) collective-permute-start(bf16[4,2,2,32,1024]{4,3,2,1,0:T(8,128)(2,1)} %bitcast.22), channel_id=1, source_target_pairs={{0,1},{1,0},{2,3},{3,2},{4,5},{5,4},{6,7},{7,6},{8,9},{9,8},{10,11... | collective-permute-start | bytes 3145736 | tf_op jit(solution)/shard_map/ppermute | solution.py:101
  380.5 27.9 %collective-permute-start.41 = (bf16[4,32,4096]{2,1,0:T(8,128)(2,1)}, bf16[4,32,4096]{2,1,0:T(8,128)(2,1)S(1)}, u32[]{:S(2)}, u32[]{:S(2)}) collective-permute-start(bf16[4,32,4096]{2,1,0:T(8,128)(2,1)} %get-tuple-element.169), channel_id=1, source_target_pairs={{0,2},{2,0},{4,6},{6,4},{8,10},{10,8},{12,14},{14,12},{16,18},{18,... | collective-permute-start | bytes 3145736 | tf_op jit(solution)/shard_map/ppermute | solution.py:98
  380.8 27.6 %collective-permute-start.42 = (bf16[4,32,4096]{2,1,0:T(8,128)(2,1)}, bf16[4,32,4096]{2,1,0:T(8,128)(2,1)S(1)}, u32[]{:S(2)}, u32[]{:S(2)}) collective-permute-start(bf16[4,32,4096]{2,1,0:T(8,128)(2,1)} %get-tuple-element.170), channel_id=1, source_target_pairs={{0,4},{2,6},{4,0},{6,2},{8,12},{10,14},{12,8},{14,10},{16,20},{18,... | collective-permute-start | bytes 3145736 | tf_op jit(solution)/shard_map/ppermute | solution.py:98
  405.4 29.4 %collective-permute-start.44 = (bf16[4,2,2,32,1536]{4,3,2,1,0:T(8,128)(2,1)}, bf16[4,2,2,32,1536]{4,3,2,1,0:T(8,128)(2,1)}, u32[]{:S(2)}, u32[]{:S(2)}) collective-permute-start(bf16[4,2,2,32,1536]{4,3,2,1,0:T(8,128)(2,1)} %bitcast.24), channel_id=1, source_target_pairs={{0,1},{1,0},{2,3},{3,2},{4,5},{5,4},{6,7},{7,6},{8,9},{9,8},{10,11... | collective-permute-start | bytes 4718600 | tf_op jit(solution)/shard_map/ppermute | solution.py:101
  431.8 42.0 %collective-permute-start.48 = (bf16[32,8192]{1,0:T(8,128)(2,1)}, bf16[32,8192]{1,0:T(8,128)(2,1)}, u32[]{:S(2)}, u32[]{:S(2)}) collective-permute-start(bf16[32,8192]{1,0:T(8,128)(2,1)} %get-tuple-element.186), channel_id=1, source_target_pairs={{0,8},{2,10},{4,12},{6,14},{8,16},{10,18},{12,20},{14,22},{16,24},... | collective-permute-start | bytes 1572872 | tf_op jit(solution)/shard_map/ppermute | solution.py:98
  432.3 41.9 %collective-permute-start.49 = (bf16[32,8192]{1,0:T(8,128)(2,1)}, bf16[32,8192]{1,0:T(8,128)(2,1)}, u32[]{:S(2)}, u32[]{:S(2)}) collective-permute-start(bf16[32,8192]{1,0:T(8,128)(2,1)} %get-tuple-element.187), channel_id=1, source_target_pairs={{0,16},{2,18},{4,20},{6,22},{8,24},{10,26},{12,28},{14,30},{16,0},... | collective-permute-start | bytes 1572872 | tf_op jit(solution)/shard_map/ppermute | solution.py:98
  446.5 21.2 %collective-permute-start.47 = (bf16[4,2,2,32,1536]{4,3,2,1,0:T(8,128)(2,1)}, bf16[4,2,2,32,1536]{4,3,2,1,0:T(8,128)(2,1)}, u32[]{:S(2)}, u32[]{:S(2)}) collective-permute-start(bf16[4,2,2,32,1536]{4,3,2,1,0:T(8,128)(2,1)} %bitcast.26), channel_id=1, source_target_pairs={{0,1},{1,0},{2,3},{3,2},{4,5},{5,4},{6,7},{7,6},{8,9},{9,8},{10,11... | collective-permute-start | bytes 4718600 | tf_op jit(solution)/shard_map/ppermute | solution.py:101
  450.0 25.9 %collective-permute-start.50 = (bf16[32,8192]{1,0:T(8,128)(2,1)}, bf16[32,8192]{1,0:T(8,128)(2,1)}, u32[]{:S(2)}, u32[]{:S(2)}) collective-permute-start(bf16[32,8192]{1,0:T(8,128)(2,1)} %get-tuple-element.188), channel_id=1, source_target_pairs={{0,24},{2,26},{4,28},{6,30},{8,0},{10,2},{12,4},{14,6},{16,8},{18,... | collective-permute-start | bytes 1572872 | tf_op jit(solution)/shard_map/ppermute | solution.py:98
  456.0 39.1 %collective-permute-start.51 = (bf16[4,32,2560]{2,1,0:T(8,128)(2,1)}, bf16[4,32,2560]{2,1,0:T(8,128)(2,1)}, u32[]{:S(2)}, u32[]{:S(2)}) collective-permute-start(bf16[4,32,2560]{2,1,0:T(8,128)(2,1)} %get-tuple-element.192), channel_id=1, source_target_pairs={{0,2},{2,0},{4,6},{6,4},{8,10},{10,8},{12,14},{14,12},{16,18},{18,... | collective-permute-start | bytes 1966088 | tf_op jit(solution)/shard_map/ppermute | solution.py:98
  467.7 27.3 %collective-permute-start.52 = (bf16[4,32,2560]{2,1,0:T(8,128)(2,1)}, bf16[4,32,2560]{2,1,0:T(8,128)(2,1)}, u32[]{:S(2)}, u32[]{:S(2)}) collective-permute-start(bf16[4,32,2560]{2,1,0:T(8,128)(2,1)} %get-tuple-element.193), channel_id=1, source_target_pairs={{0,4},{2,6},{4,0},{6,2},{8,12},{10,14},{12,8},{14,10},{16,20},{18,... | collective-permute-start | bytes 1966088 | tf_op jit(solution)/shard_map/ppermute | solution.py:98
  474.3 13.8 %collective-permute-start.54 = (bf16[2,32,1536]{2,1,0:T(8,128)(2,1)}, bf16[2,32,1536]{2,1,0:T(8,128)(2,1)S(1)}, u32[]{:S(2)}, u32[]{:S(2)}) collective-permute-start(bf16[2,32,1536]{2,1,0:T(8,128)(2,1)} %get-tuple-element.200), channel_id=1, source_target_pairs={{0,4},{2,6},{4,0},{6,2},{8,12},{10,14},{12,8},{14,10},{16,20},{18,... | collective-permute-start | bytes 589832 | tf_op jit(solution)/shard_map/ppermute | solution.py:98
  492.9 11.3 %collective-permute-start.56 = (bf16[4,32,1536]{2,1,0:T(8,128)(2,1)}, bf16[4,32,1536]{2,1,0:T(8,128)(2,1)S(1)}, u32[]{:S(2)}, u32[]{:S(2)}) collective-permute-start(bf16[4,32,1536]{2,1,0:T(8,128)(2,1)} %get-tuple-element.202), channel_id=1, source_target_pairs={{0,2},{2,0},{4,6},{6,4},{8,10},{10,8},{12,14},{14,12},{16,18},{18,... | collective-permute-start | bytes 1179656 | tf_op jit(solution)/shard_map/ppermute | solution.py:98
  503.8 44.7 %collective-permute-start.55 = (f32[2,256,1024]{2,1,0:T(8,128)}, f32[2,256,1024]{2,1,0:T(8,128)}, u32[]{:S(2)}, u32[]{:S(2)}) collective-permute-start(f32[2,256,1024]{2,1,0:T(8,128)} %get-tuple-element.245), channel_id=1, source_target_pairs={{0,1},{1,0},{2,3},{3,2},{4,5},{5,4},{6,7},{7,6},{8,9},{9,8},{10,11... | collective-permute-start | bytes 6291464 | tf_op jit(solution)/shard_map/ppermute | solution.py:101
  524.5 20.6 %collective-permute-start.63 = (f32[24,1024]{1,0:T(8,128)S(1)}, f32[24,1024]{1,0:T(8,128)S(1)}, u32[]{:S(2)}, u32[]{:S(2)}) collective-permute-start(f32[24,1024]{1,0:T(8,128)S(1)} %add_add_fusion.2), channel_id=1, source_target_pairs={{0,16},{2,18},{4,20},{6,22},{8,24},{10,26},{12,28},{14,30},{16,0},... | collective-permute-start | bytes 294920 | tf_op jit(solution)/shard_map/ppermute | solution.py:473
  524.6 20.4 %collective-permute-start.62 = (f32[24,1024]{1,0:T(8,128)S(1)}, f32[24,1024]{1,0:T(8,128)S(1)}, u32[]{:S(2)}, u32[]{:S(2)}) collective-permute-start(f32[24,1024]{1,0:T(8,128)S(1)} %add_add_fusion.2), channel_id=1, source_target_pairs={{0,8},{2,10},{4,12},{6,14},{8,0},{10,2},{12,4},{14,6},{16,24},{18,... | collective-permute-start | bytes 294920 | tf_op jit(solution)/shard_map/ppermute | solution.py:473
  525.1 28.6 %collective-permute-start.65 = (bf16[32,4096]{1,0:T(8,128)(2,1)}, bf16[32,4096]{1,0:T(8,128)(2,1)S(1)}, u32[]{:S(2)}, u32[]{:S(2)}) collective-permute-start(bf16[32,4096]{1,0:T(8,128)(2,1)} %get-tuple-element.206), channel_id=1, source_target_pairs={{0,8},{2,10},{4,12},{6,14},{8,16},{10,18},{12,20},{14,22},{16,24},... | collective-permute-start | bytes 786440 | tf_op jit(solution)/shard_map/ppermute | solution.py:98
  529.3 24.3 %collective-permute-start.66 = (bf16[32,4096]{1,0:T(8,128)(2,1)}, bf16[32,4096]{1,0:T(8,128)(2,1)S(1)}, u32[]{:S(2)}, u32[]{:S(2)}) collective-permute-start(bf16[32,4096]{1,0:T(8,128)(2,1)} %get-tuple-element.207), channel_id=1, source_target_pairs={{0,16},{2,18},{4,20},{6,22},{8,24},{10,26},{12,28},{14,30},{16,0},... | collective-permute-start | bytes 786440 | tf_op jit(solution)/shard_map/ppermute | solution.py:98
  (109 other events, 1862.2 us)

commit v5 on v4

--- a/solution.py
+++ b/solution.py
@@ -464,11 +464,13 @@
     return lax.dynamic_index_in_dim(value, index, axis, keepdims=False)
 
 
-def sum_everywhere(wires, value):
+def sum_everywhere(wires, value, hold):
     value = value + wires.swap(value)
     dims = wires.dims
     planes = [(0, y, x) for y, x in wires.planes]
     for flips in (planes, [(z, 0, 0) for z in range(dims[0])]):
+        if flips is not planes:
+            value = gate(value, hold)
         terms = [value] + [
             lax.ppermute(value, "rows", crossing(dims, flip)) for flip in flips[1:]
         ]
@@ -880,7 +882,7 @@
     )
     z_two = Outer(wires, [s_a, s_b])
     little = jnp.pad(little, ((0, -little.shape[0] % 8), (0, 0)))
-    little = sum_everywhere(wires, gate(little, z_two.sends))
+    little = sum_everywhere(wires, gate(little, z_two.sends), z_two.terms)
     grad_rows = (grad_resid1 + back_one).reshape(rows_here, row_len, width)
     grad_away = lax.dynamic_slice_in_dim(grad_rows, (1 - seq) * slots_half, slots_half, 1)
     grad_back = wires.swap(grad_away)

time: 570 us -> 574 us (level)
  starting transfers between devices: 65 us -> 72.1 us
    ppermute x6, waiting for transfers between devices: 17.6 us -> 5.27 us  [sum_everywhere(): lax.ppermute(value, 'rows', crossing(dims, flip))]
    ppermute x40, waiting for transfers between devices: 46 us -> 56.5 us  [turn(): return lax.ppermute(value, 'rows', rotation(self.dims, (z, y, x)))]
  transfers between devices with their start and end apart: 68 -> 68, of which waited for: 19 -> 17; matrix products, arithmetic and copies ran while one was open for 36% -> 35% of each run, Pallas kernels for 29% -> 28%
where the time goes in v5:
time: 574 us; the launch traced here: 564 us
  Pallas kernels  179 us (31%)
  matrix products  172 us (30%)
  starting transfers between devices  72.1 us (13%)
  waiting for transfers between devices  62.9 us (11%)
  local copies, waits for them, and re-layouts  43 us (7%)
  other arithmetic  33 us (6%)
    dot_general x13, matrix products, dot_first(): lax.dot_general(a, b, (((0,), (0,)), ((), ())), precision=precision, pref...  63.4 us
    ppermute x40, starting transfers between devices, turn(): return lax.ppermute(value, 'rows', rotation(self.dims, (z, y, x)))  56.6 us
    ppermute x40, waiting for transfers between devices, turn(): return lax.ppermute(value, 'rows', rotation(self.dims, (z, y, x)))  56.5 us
    dot_general x7, matrix products, dot_second(): lax.dot_general(a, b, (((1,), (1,)), ((), ())), precision=precision, pref...  54.7 us
    dot_general x9, matrix products, dot_plain(): return jnp.dot(a, b, precision=precision, preferred_element_type=F32)  53.8 us
    pallas_call x10, Pallas kernels, prefetched(): pl.pallas_call(body, out_shape=out_shape, grid_spec=pltpu.PrefetchScalarG...  51 us
    pallas_call x2, Pallas kernels, attend_back(): pl.pallas_call(attend_back_kernel, grid=(rows, pairs), in_specs=[pl.Block...  35.6 us
    pallas_call x1, Pallas kernels, widen(): pl.pallas_call(widen_kernel(128, chunk), out_shape=[out, out, part, part]...  30.7 us
  transfers between devices with their start and end apart: 68, of which 17 were waited for; matrix products, arithmetic and copies ran while one was open for 35% of the time, Pallas kernels for 28%

profile of v5, /device:TPU:0, one launch (start us, length us, event | category | flops | bytes accessed | tf_op | source)
XLA Modules:
  0.0 563.9 jit_solution(9004827377654139875)
XLA Ops:
  1.4 4.8 concatenate.36
  9.0 5.1 collective-permute-start.4
  43.8 13.4 %collective-permute-done.9.refs_2_ = bf16[32,5120]{1,0:T(8,128)(2,1)S(1)} collective-permute-done((bf16[32,5120]{1,0:T(8,128)(2,1)}, bf16[32,5120]{1,0:T(8,128)(2,1)S(1)}, u32[]{:S(2)}, u32[]{:S(2)}) %collective-permute-start.9) | collective-permute-done | bytes 327712 | tf_op jit(solution)/shard_map/ppermute | solution.py:98
  59.1 9.9 %collective-permute-done.8.refs_1_ = bf16[32,5120]{1,0:T(8,128)(2,1)} collective-permute-done((bf16[32,5120]{1,0:T(8,128)(2,1)}, bf16[32,5120]{1,0:T(8,128)(2,1)}, u32[]{:S(2)}, u32[]{:S(2)}) %collective-permute-start.8) | collective-permute-done | bytes 327712 | tf_op jit(solution)/shard_map/ppermute | solution.py:98
  83.9 6.8 %place.3 = (bf16[1024,3072]{1,0:T(8,128)(2,1)}, bf16[1024,128]{1,0:T(8,128)(2,1)}) custom-call(s32[4]{0:T(128)} %pad_add_fusion.where, bf16[4,32,3200]{2,1,0:T(8,128)(2,1)} %stack.63.refs_0_, bf16[4,32,3200]{2,1,0:T(8,128)(2,1)} %collective-permute-done.5.refs_1_, bf16[4,32,3200]{2,1,0:T(8,128)(2,1)} %collective-permute-done.6.refs_2_, ...), custom_call_target="tpu_custom_call" | custom-call | tf_op jit(solution)/shard_map/place/pallas_call | solution.py:210
  97.7 11.3 %add_convert_fusion.joined_ref = bf16[1024,3072]{1,0:T(8,128)(2,1)} fusion(f32[3072]{0:T(1024)S(1)} %add.257, bf16[1024,1024]{1,0:T(8,128)(2,1)S(1)} %fusion.8, bf16[1024,3072]{1,0:T(8,128)(2,1)} %get-tuple-element.131), kind=kOutput, calls=%fused_computation.2 | convolution fusion | flops 6448742400 | bytes 14692352 | tf_op jit(solution)/shard_map/dot_general | solution.py:21
  109.1 24.3 %attend.1 = (bf16[1024,1024]{1,0:T(8,128)(2,1)}, f32[2,8,2,512]{3,2,1,0:T(2,128)}) custom-call(s32[2,512,1]{2,1,0:T(8,128)} %copy.53.seg_col, s32[2,1,512]{2,1,0:T(1,128)} %broadcast_in_dim.17.seg_row, bf16[1024,3072]{1,0:T(8,128)(2,1)} %add_convert_fusion.joined_ref), custom_call_target="tpu_custom_call" | custom-call | tf_op jit(solution)/shard_map/attend/pallas_call | solution.py:511
  133.4 7.1 %collective-permute-done.19.refs_2_ = bf16[4,32,5120]{2,1,0:T(8,128)(2,1)} collective-permute-done((bf16[4,32,5120]{2,1,0:T(8,128)(2,1)}, bf16[4,32,5120]{2,1,0:T(8,128)(2,1)}, u32[]{:S(2)}, u32[]{:S(2)}) %collective-permute-start.19) | collective-permute-done | bytes 1310752 | tf_op jit(solution)/shard_map/ppermute | solution.py:98
  151.6 5.4 fusion.43
  158.8 9.2 %place.4 = (bf16[1024,1024]{1,0:T(8,128)(2,1)}, bf16[1024,4096]{1,0:T(8,128)(2,1)}) custom-call(s32[4]{0:T(128)} %pad_add_fusion.where, bf16[4,32,5120]{2,1,0:T(8,128)(2,1)} %stack.64.refs_0_, bf16[4,32,5120]{2,1,0:T(8,128)(2,1)} %collective-permute-done.18.refs_1_, bf16[4,32,5120]{2,1,0:T(8,128)(2,1)} %collective-permute-done.19.refs_2_, ...), custom_call_target="tpu_custom_call" | custom-call | tf_op jit(solution)/shard_map/place/pallas_call | solution.py:210
  168.0 4.7 fusion.116
  175.5 30.7 %widen.1 = (bf16[1024,4096]{1,0:T(8,128)(2,1)}, bf16[1024,4096]{1,0:T(8,128)(2,1)}, bf16[1024,2048]{1,0:T(8,128)(2,1)}, bf16[1024,2048]{1,0:T(8,128)(2,1)}) custom-call(s32[4]{0:T(128)} %pad_add_fusion.where, bf16[1024,1024]{1,0:T(8,128)(2,1)} %add_convert_fusion.1.x_ref, bf16[1024,4096]{1,0:T(8,128)(2,1)} %get-tuple-element.140.w_ref, ...), custom_call_target="tpu_custom_call" | custom-call | tf_op jit(solution)/shard_map/widen/pallas_call | solution.py:654
  207.9 5.5 fusion.42
  213.4 3.7 fusion.41
  218.4 7.7 %place.5 = bf16[4096,1024]{1,0:T(8,128)(2,1)} custom-call(s32[4]{0:T(128)} %pad_add_fusion.where, bf16[4,128,1024]{2,1,0:T(8,128)(2,1)} %stack.65.refs_0_, bf16[4,128,1024]{2,1,0:T(8,128)(2,1)} %collective-permute-done.25.refs_1_, bf16[4,128,1024]{2,1,0:T(8,128)(2,1)} %collective-permute-done.26.refs_2_, ...), custom_call_target="tpu_custom_call" | custom-call | tf_op jit(solution)/shard_map/place/pallas_call | solution.py:210
  226.2 14.6 %fusion.117 = (f32[1024]{0:T(1024)S(1)}, f32[1024,1024]{1,0:T(8,128)S(1)}) fusion(f32[1024]{0:T(1024)S(1)} %get-tuple-element.254, f32[1024,1024]{1,0:T(8,128)} %copy-done.5, bf16[1024,4096]{1,0:T(8,128)(2,1)} %get-tuple-element.141, bf16[4096,1024]{1,0:T(8,128)(2,1)} %place.5), kind=kOutput, calls=%fused_computation.225 | convolution fusion | flops 8593079296 | bytes 25174016 | tf_op jit(solution)/shard_map/dot_general | solution.py:21
  250.6 4.2 fusion.118
  254.9 6.4 %convolution_convert_fusion.4 = bf16[2048,1024]{1,0:T(8,128)(2,1)} fusion(bf16[1024,2048]{1,0:T(8,128)(2,1)S(1)} %copy-done.76, bf16[1024,1024]{1,0:T(8,128)(2,1)S(1)} %get-tuple-element.150), kind=kOutput, calls=%fused_computation.51 | convolution fusion | flops 4297064448 | bytes 10485760 | tf_op jit(solution)/shard_map/dot_general | solution.py:25
  265.9 8.4 %convolution_convert_fusion.3 = bf16[2048,1024]{1,0:T(8,128)(2,1)} fusion(bf16[1024,2048]{1,0:T(8,128)(2,1)} %get-tuple-element.148, bf16[1024,1024]{1,0:T(8,128)(2,1)S(1)} %get-tuple-element.150), kind=kOutput, calls=%fused_computation.50 | convolution fusion | flops 4297064448 | bytes 10485760 | tf_op jit(solution)/shard_map/dot_general | solution.py:25
  275.2 15.2 %multiply_convert_fusion = bf16[1024,4096]{1,0:T(8,128)(2,1)} fusion(bf16[1024,4096]{1,0:T(8,128)(2,1)} %get-tuple-element.142, bf16[1024,1024]{1,0:T(8,128)(2,1)S(1)} %get-tuple-element.150, bf16[4096,1024]{1,0:T(8,128)(2,1)} %place.5), kind=kOutput, calls=%fused_computation.1 | convolution fusion | flops 8610906112 | bytes 27262976 | tf_op jit(solution)/shard_map/dot_general | solution.py:31
  290.5 4.4 fusion.21
  296.0 6.6 %fold_inner.4 = (bf16[4,128,1024]{2,1,0:T(8,128)(2,1)}, bf16[4,128,1024]{2,1,0:T(8,128)(2,1)}, bf16[4,128,1024]{2,1,0:T(8,128)(2,1)}, bf16[2,128,1024]{2,1,0:T(8,128)(2,1)}, bf16[2,128,1024]{2,1,0:T(8,128)(2,1)}) custom-call(s32[4]{0:T(128)} %pad_add_fusion.where, bf16[4,2,2,128,1024]{4,3,2,1,0:T(8,128)(2,1)} %bitcast.148, ...), custom_call_target="tpu_custom_call" | custom-call | tf_op jit(solution)/shard_map/fold_inner/pallas_call | solution.py:310
  304.7 10.1 %convolution_convert_fusion.2 = bf16[512,4096]{1,0:T(8,128)(2,1)} fusion(bf16[1024,4096]{1,0:T(8,128)(2,1)} %multiply_convert_fusion, bf16[1024,1024]{1,0:T(8,128)(2,1)S(1)} %copy-done.86), kind=kOutput, calls=%fused_computation.12 | convolution fusion | flops 4297064448 | bytes 13631488 | tf_op jit(solution)/shard_map/dot_general | solution.py:25
  316.7 9.5 %convolution_convert_fusion.1 = bf16[512,4096]{1,0:T(8,128)(2,1)} fusion(bf16[1024,4096]{1,0:T(8,128)(2,1)} %multiply_convert_fusion, bf16[1024,1024]{1,0:T(8,128)(2,1)S(1)} %copy-done.86), kind=kOutput, calls=%fused_computation.11 | convolution fusion | flops 4297064448 | bytes 13631488 | tf_op jit(solution)/shard_map/dot_general | solution.py:25
  327.8 4.7 relay.4
  334.4 16.4 %multiply_reduce_fusion.1 = (f32[1024]{0:T(1024)}, f32[1024]{0:T(1024)S(1)}, f32[1024]{0:T(1024)S(1)}, f32[1024]{0:T(1024)}, f32[1024,1024]{1,0:T(8,128)S(1)}) fusion(f32[1024,1024]{1,0:T(8,128)} %copy-done.5, f32[1024]{0:T(1024)S(1)} %copy-done.60, f32[1024]{0:T(1024)S(1)} %copy-done.48, f32[1024]{0:T(1024)S(1)} %copy-done.58, ...), kind=kOutput, calls=%fused_computation.32 | convolution fusion | flops 8599367680 | bytes 25194496 | tf_op jit(solution)/shard_map/dot_general | solution.py:31
  353.7 6.6 %fold_inner.5 = (bf16[4,32,4096]{2,1,0:T(8,128)(2,1)}, bf16[4,32,4096]{2,1,0:T(8,128)(2,1)}, bf16[4,32,4096]{2,1,0:T(8,128)(2,1)}, bf16[2,32,4096]{2,1,0:T(8,128)(2,1)}, bf16[2,32,4096]{2,1,0:T(8,128)(2,1)}) custom-call(s32[4]{0:T(128)} %pad_add_fusion.where, bf16[4,2,2,32,4096]{4,3,2,1,0:T(8,128)(2,1)} %bitcast.147, ...), custom_call_target="tpu_custom_call" | custom-call | tf_op jit(solution)/shard_map/fold_inner/pallas_call | solution.py:310
  362.5 3.5 convolution_convert_fusion.11
  369.3 3.7 convolution_convert_fusion.9.do_ref
  375.8 4.7 relay.5
  382.4 17.6 %attend_back.2 = bf16[1024,1536]{1,0:T(8,128)(2,1)} custom-call(s32[2,512,1]{2,1,0:T(8,128)} %copy.53.seg_col, s32[2,1,512]{2,1,0:T(1,128)} %broadcast_in_dim.17.seg_row, bf16[1024,3072]{1,0:T(8,128)(2,1)} %add_convert_fusion.joined_ref, f32[2,4,2,512]{3,2,1,0:T(2,128)} %get-tuple-element.263.log_ref, bf16[1024,1024]{1,0:T(8,128)(2,1)} %convolution_convert_fusion.9.do_ref), custom_call_target="tpu_custom_call" | custom-call | flops 16106127360 | bytes 25165824 | tf_op jit(solution)/shard_map/attend_back/pallas_call | solution.py:563
  400.0 5.4 convolution_convert_fusion.8
  408.4 18.0 %attend_back.3 = bf16[1024,1536]{1,0:T(8,128)(2,1)} custom-call(s32[2,512,1]{2,1,0:T(8,128)} %copy.53.seg_col, s32[2,1,512]{2,1,0:T(1,128)} %broadcast_in_dim.17.seg_row, bf16[1024,3072]{1,0:T(8,128)(2,1)} %add_convert_fusion.joined_ref, f32[2,4,2,512]{3,2,1,0:T(2,128)} %get-tuple-element.262.log_ref, bf16[1024,1024]{1,0:T(8,128)(2,1)} %convolution_convert_fusion.9.do_ref), custom_call_target="tpu_custom_call" | custom-call | flops 16106127360 | bytes 25165824 | tf_op jit(solution)/shard_map/attend_back/pallas_call | solution.py:563
  426.5 5.4 fold_outer.2
  434.8 5.4 fold_inner.6
  442.3 4.2 convolution_convert_fusion.6
  451.5 4.4 relay.6
  459.4 8.3 %fusion.25 = f32[1024,1024]{1,0:T(8,128)} fusion(bf16[1024,1536]{1,0:T(8,128)(2,1)} %attend_back.2, bf16[1024,3072]{1,0:T(8,128)(2,1)} %get-tuple-element.131), kind=kOutput, calls=%fused_computation.59 | convolution fusion | flops 3221225472 | bytes 10485760 | tf_op jit(solution)/shard_map/dot_general | solution.py:31
  469.3 4.6 fold_inner.7
  475.9 7.6 %fusion.38 = f32[1024,1024]{1,0:T(8,128)} fusion(f32[1024,1024]{1,0:T(8,128)} %fusion.25, bf16[1024,1536]{1,0:T(8,128)(2,1)S(1)} %copy-done.11, bf16[1024,3072]{1,0:T(8,128)(2,1)} %get-tuple-element.131), kind=kOutput, calls=%fused_computation.77 | convolution fusion | flops 3222274048 | bytes 14680064 | tf_op jit(solution)/shard_map/dot_general | solution.py:31
  488.7 4.1 relay.7
  495.1 3.7 fusion.13
  505.7 4.6 fold_outer.3
  520.5 3.7 collective-permute-start.64
  527.1 10.1 %collective-permute-done.63.refs_2_ = bf16[32,4096]{1,0:T(8,128)(2,1)S(1)} collective-permute-done((bf16[32,4096]{1,0:T(8,128)(2,1)}, bf16[32,4096]{1,0:T(8,128)(2,1)S(1)}, u32[]{:S(2)}, u32[]{:S(2)}) %collective-permute-start.63) | collective-permute-done | bytes 262176 | tf_op jit(solution)/shard_map/ppermute | solution.py:98
  537.2 6.7 %collective-permute-start.67 = (f32[24,1024]{1,0:T(8,128)S(1)}, f32[24,1024]{1,0:T(8,128)S(1)}, u32[]{:S(2)}, u32[]{:S(2)}) collective-permute-start(f32[24,1024]{1,0:T(8,128)S(1)} %add_add_fusion.2), channel_id=1, source_target_pairs={{0,24},{2,26},{4,28},{6,30},{8,16},{10,18},{12,20},{14,22},{16,8},... | collective-permute-start | bytes 294920 | tf_op jit(solution)/shard_map/ppermute | solution.py:475
  547.4 5.3 collective-permute-done.66
  556.3 5.1 maximum_select_fusion
  (422 shorter events, 168.9 us)
Async XLA Ops:
  9.0 19.6 %collective-permute-start.4 = (bf16[32,3200]{1,0:T(8,128)(2,1)S(1)}, bf16[32,3200]{1,0:T(8,128)(2,1)}, u32[]{:S(2)}, u32[]{:S(2)}) collective-permute-start(bf16[32,3200]{1,0:T(8,128)(2,1)S(1)} %fusion.78.refs_0_), channel_id=1, source_target_pairs={{0,24},{2,26},{4,28},{6,30},{8,0},{10,2},{12,4},{14,6},{16,8},{18,... | collective-permute-start | bytes 614408 | tf_op jit(solution)/shard_map/ppermute | solution.py:98
  14.1 17.5 %collective-permute-start.3 = (bf16[32,3200]{1,0:T(8,128)(2,1)S(1)}, bf16[32,3200]{1,0:T(8,128)(2,1)}, u32[]{:S(2)}, u32[]{:S(2)}) collective-permute-start(bf16[32,3200]{1,0:T(8,128)(2,1)S(1)} %fusion.78.refs_0_), channel_id=1, source_target_pairs={{0,16},{2,18},{4,20},{6,22},{8,24},{10,26},{12,28},{14,30},{16,0},... | collective-permute-start | bytes 614408 | tf_op jit(solution)/shard_map/ppermute | solution.py:98
  14.1 17.5 %collective-permute-start.2 = (bf16[32,3200]{1,0:T(8,128)(2,1)S(1)}, bf16[32,3200]{1,0:T(8,128)(2,1)}, u32[]{:S(2)}, u32[]{:S(2)}) collective-permute-start(bf16[32,3200]{1,0:T(8,128)(2,1)S(1)} %fusion.78.refs_0_), channel_id=1, source_target_pairs={{0,8},{2,10},{4,12},{6,14},{8,16},{10,18},{12,20},{14,22},{16,24},... | collective-permute-start | bytes 614408 | tf_op jit(solution)/shard_map/ppermute | solution.py:98
  17.5 57.5 %collective-permute-start = (bf16[2,256,1024]{2,1,0:T(8,128)(2,1)}, bf16[2,256,1024]{2,1,0:T(8,128)(2,1)S(1)}, u32[]{:S(2)}, u32[]{:S(2)}) collective-permute-start(bf16[2,256,1024]{2,1,0:T(8,128)(2,1)} %constant_dynamic-slice_fusion.3), channel_id=1, source_target_pairs={{0,1},{1,0},{2,3},{3,2},{4,5},{5,4},{6,7},{7,6},{8,9},{9,8},{10,11... | collective-permute-start | bytes 3145736 | tf_op jit(solution)/shard_map/ppermute | solution.py:101
  35.5 36.0 %collective-permute-start.7 = (bf16[4,32,3200]{2,1,0:T(8,128)(2,1)}, bf16[4,32,3200]{2,1,0:T(8,128)(2,1)}, u32[]{:S(2)}, u32[]{:S(2)}) collective-permute-start(bf16[4,32,3200]{2,1,0:T(8,128)(2,1)} %stack.63.refs_0_), channel_id=1, source_target_pairs={{0,6},{2,4},{4,2},{6,0},{8,14},{10,12},{12,10},{14,8},{16,22},{18,... | collective-permute-start | bytes 2457608 | tf_op jit(solution)/shard_map/ppermute | solution.py:98
  38.0 36.4 %collective-permute-start.6 = (bf16[4,32,3200]{2,1,0:T(8,128)(2,1)}, bf16[4,32,3200]{2,1,0:T(8,128)(2,1)}, u32[]{:S(2)}, u32[]{:S(2)}) collective-permute-start(bf16[4,32,3200]{2,1,0:T(8,128)(2,1)} %stack.63.refs_0_), channel_id=1, source_target_pairs={{0,4},{2,6},{4,0},{6,2},{8,12},{10,14},{12,8},{14,10},{16,20},{18,... | collective-permute-start | bytes 2457608 | tf_op jit(solution)/shard_map/ppermute | solution.py:98
  38.5 36.0 %collective-permute-start.5 = (bf16[4,32,3200]{2,1,0:T(8,128)(2,1)}, bf16[4,32,3200]{2,1,0:T(8,128)(2,1)}, u32[]{:S(2)}, u32[]{:S(2)}) collective-permute-start(bf16[4,32,3200]{2,1,0:T(8,128)(2,1)} %stack.63.refs_0_), channel_id=1, source_target_pairs={{0,2},{2,0},{4,6},{6,4},{8,10},{10,8},{12,14},{14,12},{16,18},{18,... | collective-permute-start | bytes 2457608 | tf_op jit(solution)/shard_map/ppermute | solution.py:98
  40.5 16.6 %collective-permute-start.9 = (bf16[32,5120]{1,0:T(8,128)(2,1)}, bf16[32,5120]{1,0:T(8,128)(2,1)S(1)}, u32[]{:S(2)}, u32[]{:S(2)}) collective-permute-start(bf16[32,5120]{1,0:T(8,128)(2,1)} %constant_dynamic-update-slice_fusion.refs_0_), channel_id=1, source_target_pairs={{0,16},{2,18},{4,20},{6,22},{8,24},{10,26},{12,28},{14,30},{16,0},... | collective-permute-start | bytes 983048 | tf_op jit(solution)/shard_map/ppermute | solution.py:98
  57.2 11.9 %collective-permute-start.8 = (bf16[32,5120]{1,0:T(8,128)(2,1)}, bf16[32,5120]{1,0:T(8,128)(2,1)}, u32[]{:S(2)}, u32[]{:S(2)}) collective-permute-start(bf16[32,5120]{1,0:T(8,128)(2,1)} %constant_dynamic-update-slice_fusion.refs_0_), channel_id=1, source_target_pairs={{0,8},{2,10},{4,12},{6,14},{8,16},{10,18},{12,20},{14,22},{16,24},... | collective-permute-start | bytes 983048 | tf_op jit(solution)/shard_map/ppermute | solution.py:98
  71.5 24.7 %collective-permute-start.17 = (bf16[128,1024]{1,0:T(8,128)(2,1)}, bf16[128,1024]{1,0:T(8,128)(2,1)}, u32[]{:S(2)}, u32[]{:S(2)}) collective-permute-start(bf16[128,1024]{1,0:T(8,128)(2,1)} %refs_0_.1), channel_id=1, source_target_pairs={{0,24},{2,26},{4,28},{6,30},{8,0},{10,2},{12,4},{14,6},{16,8},{18,... | collective-permute-start | bytes 786440 | tf_op jit(solution)/shard_map/ppermute | solution.py:98
  77.1 20.6 %collective-permute-start.16 = (bf16[128,1024]{1,0:T(8,128)(2,1)S(1)}, bf16[128,1024]{1,0:T(8,128)(2,1)}, u32[]{:S(2)}, u32[]{:S(2)}) collective-permute-start(bf16[128,1024]{1,0:T(8,128)(2,1)S(1)} %copy-done.35), channel_id=1, source_target_pairs={{0,16},{2,18},{4,20},{6,22},{8,24},{10,26},{12,28},{14,30},{16,0},... | collective-permute-start | bytes 786440 | tf_op jit(solution)/shard_map/ppermute | solution.py:98
  79.2 18.5 %collective-permute-start.15 = (bf16[128,1024]{1,0:T(8,128)(2,1)S(1)}, bf16[128,1024]{1,0:T(8,128)(2,1)}, u32[]{:S(2)}, u32[]{:S(2)}) collective-permute-start(bf16[128,1024]{1,0:T(8,128)(2,1)S(1)} %copy-done.35), channel_id=1, source_target_pairs={{0,8},{2,10},{4,12},{6,14},{8,16},{10,18},{12,20},{14,22},{16,24},... | collective-permute-start | bytes 786440 | tf_op jit(solution)/shard_map/ppermute | solution.py:98
  80.9 52.5 %collective-permute-start.20 = (bf16[4,32,5120]{2,1,0:T(8,128)(2,1)}, bf16[4,32,5120]{2,1,0:T(8,128)(2,1)}, u32[]{:S(2)}, u32[]{:S(2)}) collective-permute-start(bf16[4,32,5120]{2,1,0:T(8,128)(2,1)} %stack.64.refs_0_), channel_id=1, source_target_pairs={{0,6},{2,4},{4,2},{6,0},{8,14},{10,12},{12,10},{14,8},{16,22},{18,... | collective-permute-start | bytes 3932168 | tf_op jit(solution)/shard_map/ppermute | solution.py:98
  82.6 57.9 %collective-permute-start.19 = (bf16[4,32,5120]{2,1,0:T(8,128)(2,1)}, bf16[4,32,5120]{2,1,0:T(8,128)(2,1)}, u32[]{:S(2)}, u32[]{:S(2)}) collective-permute-start(bf16[4,32,5120]{2,1,0:T(8,128)(2,1)} %stack.64.refs_0_), channel_id=1, source_target_pairs={{0,4},{2,6},{4,0},{6,2},{8,12},{10,14},{12,8},{14,10},{16,20},{18,... | collective-permute-start | bytes 3932168 | tf_op jit(solution)/shard_map/ppermute | solution.py:98
  96.2 44.3 %collective-permute-start.18 = (bf16[4,32,5120]{2,1,0:T(8,128)(2,1)}, bf16[4,32,5120]{2,1,0:T(8,128)(2,1)}, u32[]{:S(2)}, u32[]{:S(2)}) collective-permute-start(bf16[4,32,5120]{2,1,0:T(8,128)(2,1)} %stack.64.refs_0_), channel_id=1, source_target_pairs={{0,2},{2,0},{4,6},{6,4},{8,10},{10,8},{12,14},{14,12},{16,18},{18,... | collective-permute-start | bytes 3932168 | tf_op jit(solution)/shard_map/ppermute | solution.py:98
  140.5 16.4 %collective-permute-start.21 = (bf16[4,32,5120]{2,1,0:T(8,128)(2,1)}, bf16[4,32,5120]{2,1,0:T(8,128)(2,1)}, u32[]{:S(2)}, u32[]{:S(2)}) collective-permute-start(bf16[4,32,5120]{2,1,0:T(8,128)(2,1)} %stack.64.refs_0_), channel_id=1, source_target_pairs={{0,1},{1,0},{2,3},{3,2},{4,5},{5,4},{6,7},{7,6},{8,9},{9,8},{10,11... | collective-permute-start | bytes 3932168 | tf_op jit(solution)/shard_map/ppermute | solution.py:101
  140.5 17.7 %collective-permute-start.22 = (bf16[4,32,5120]{2,1,0:T(8,128)(2,1)}, bf16[4,32,5120]{2,1,0:T(8,128)(2,1)}, u32[]{:S(2)}, u32[]{:S(2)}) collective-permute-start(bf16[4,32,5120]{2,1,0:T(8,128)(2,1)} %collective-permute-done.18.refs_1_), channel_id=1, source_target_pairs={{0,1},{1,0},{2,3},{3,2},{4,5},{5,4},{6,7},{7,6},{8,9},{9,8},{10,11... | collective-permute-start | bytes 3932168 | tf_op jit(solution)/shard_map/ppermute | solution.py:101
  141.0 17.8 %collective-permute-start.23 = (bf16[4,32,5120]{2,1,0:T(8,128)(2,1)}, bf16[4,32,5120]{2,1,0:T(8,128)(2,1)}, u32[]{:S(2)}, u32[]{:S(2)}) collective-permute-start(bf16[4,32,5120]{2,1,0:T(8,128)(2,1)} %collective-permute-done.19.refs_2_), channel_id=1, source_target_pairs={{0,1},{1,0},{2,3},{3,2},{4,5},{5,4},{6,7},{7,6},{8,9},{9,8},{10,11... | collective-permute-start | bytes 3932168 | tf_op jit(solution)/shard_map/ppermute | solution.py:101
  141.0 17.8 %collective-permute-start.24 = (bf16[4,32,5120]{2,1,0:T(8,128)(2,1)}, bf16[4,32,5120]{2,1,0:T(8,128)(2,1)}, u32[]{:S(2)}, u32[]{:S(2)}) collective-permute-start(bf16[4,32,5120]{2,1,0:T(8,128)(2,1)} %collective-permute-done.20.refs_3_), channel_id=1, source_target_pairs={{0,1},{1,0},{2,3},{3,2},{4,5},{5,4},{6,7},{7,6},{8,9},{9,8},{10,11... | collective-permute-start | bytes 3932168 | tf_op jit(solution)/shard_map/ppermute | solution.py:101
  148.9 57.3 %collective-permute-start.27 = (bf16[4,128,1024]{2,1,0:T(8,128)(2,1)}, bf16[4,128,1024]{2,1,0:T(8,128)(2,1)}, u32[]{:S(2)}, u32[]{:S(2)}) collective-permute-start(bf16[4,128,1024]{2,1,0:T(8,128)(2,1)} %stack.65.refs_0_), channel_id=1, source_target_pairs={{0,6},{2,4},{4,2},{6,0},{8,14},{10,12},{12,10},{14,8},{16,22},{18,... | collective-permute-start | bytes 3145736 | tf_op jit(solution)/shard_map/ppermute | solution.py:98
  156.9 49.3 %collective-permute-start.26 = (bf16[4,128,1024]{2,1,0:T(8,128)(2,1)S(1)}, bf16[4,128,1024]{2,1,0:T(8,128)(2,1)}, u32[]{:S(2)}, u32[]{:S(2)}) collective-permute-start(bf16[4,128,1024]{2,1,0:T(8,128)(2,1)S(1)} %copy-done.10), channel_id=1, source_target_pairs={{0,4},{2,6},{4,0},{6,2},{8,12},{10,14},{12,8},{14,10},{16,20},{18,... | collective-permute-start | bytes 3145736 | tf_op jit(solution)/shard_map/ppermute | solution.py:98
  158.2 48.0 %collective-permute-start.25 = (bf16[4,128,1024]{2,1,0:T(8,128)(2,1)S(1)}, bf16[4,128,1024]{2,1,0:T(8,128)(2,1)}, u32[]{:S(2)}, u32[]{:S(2)}) collective-permute-start(bf16[4,128,1024]{2,1,0:T(8,128)(2,1)S(1)} %copy-done.10), channel_id=1, source_target_pairs={{0,2},{2,0},{4,6},{6,4},{8,10},{10,8},{12,14},{14,12},{16,18},{18,... | collective-permute-start | bytes 3145736 | tf_op jit(solution)/shard_map/ppermute | solution.py:98
  206.2 10.9 %collective-permute-start.28 = (bf16[4,128,1024]{2,1,0:T(8,128)(2,1)S(1)}, bf16[4,128,1024]{2,1,0:T(8,128)(2,1)S(1)}, u32[]{:S(2)}, u32[]{:S(2)}) collective-permute-start(bf16[4,128,1024]{2,1,0:T(8,128)(2,1)S(1)} %copy-done.10), channel_id=1, source_target_pairs={{0,1},{1,0},{2,3},{3,2},{4,5},{5,4},{6,7},{7,6},{8,9},{9,8},{10,11... | collective-permute-start | bytes 3145736 | tf_op jit(solution)/shard_map/ppermute | solution.py:101
  261.3 34.7 %collective-permute-start.33 = (bf16[4,2,2,128,1024]{4,3,2,1,0:T(8,128)(2,1)}, bf16[4,2,2,128,1024]{4,3,2,1,0:T(8,128)(2,1)}, u32[]{:S(2)}, u32[]{:S(2)}) collective-permute-start(bf16[4,2,2,128,1024]{4,3,2,1,0:T(8,128)(2,1)} %bitcast.18), channel_id=1, source_target_pairs={{0,1},{1,0},{2,3},{3,2},{4,5},{5,4},{6,7},{7,6},{8,9},{9,8},{10,11... | collective-permute-start | bytes 12582920 | tf_op jit(solution)/shard_map/ppermute | solution.py:101
  265.4 29.4 %collective-permute-start.32 = (bf16[20,8192]{1,0:T(8,128)(2,1)}, bf16[20,8192]{1,0:T(8,128)(2,1)S(1)}, u32[]{:S(2)}, u32[]{:S(2)}) collective-permute-start(bf16[20,8192]{1,0:T(8,128)(2,1)} %dynamic-slice_bitcast_fusion), channel_id=1, source_target_pairs={{0,1},{1,0},{2,3},{3,2},{4,5},{5,4},{6,7},{7,6},{8,9},{9,8},{10,11... | collective-permute-start | bytes 983048 | tf_op jit(solution)/shard_map/ppermute | solution.py:101
  302.5 23.6 %collective-permute-start.34 = (bf16[2,128,1024]{2,1,0:T(8,128)(2,1)}, bf16[2,128,1024]{2,1,0:T(8,128)(2,1)S(1)}, u32[]{:S(2)}, u32[]{:S(2)}) collective-permute-start(bf16[2,128,1024]{2,1,0:T(8,128)(2,1)} %get-tuple-element.154), channel_id=1, source_target_pairs={{0,2},{2,0},{4,6},{6,4},{8,10},{10,8},{12,14},{14,12},{16,18},{18,... | collective-permute-start | bytes 1572872 | tf_op jit(solution)/shard_map/ppermute | solution.py:98
  304.0 22.2 %collective-permute-start.35 = (bf16[2,128,1024]{2,1,0:T(8,128)(2,1)}, bf16[2,128,1024]{2,1,0:T(8,128)(2,1)S(1)}, u32[]{:S(2)}, u32[]{:S(2)}) collective-permute-start(bf16[2,128,1024]{2,1,0:T(8,128)(2,1)} %get-tuple-element.155), channel_id=1, source_target_pairs={{0,4},{2,6},{4,0},{6,2},{8,12},{10,14},{12,8},{14,10},{16,20},{18,... | collective-permute-start | bytes 1572872 | tf_op jit(solution)/shard_map/ppermute | solution.py:98
  314.8 38.9 %collective-permute-start.36 = (bf16[4,2,2,32,4096]{4,3,2,1,0:T(8,128)(2,1)}, bf16[4,2,2,32,4096]{4,3,2,1,0:T(8,128)(2,1)}, u32[]{:S(2)}, u32[]{:S(2)}) collective-permute-start(bf16[4,2,2,32,4096]{4,3,2,1,0:T(8,128)(2,1)} %bitcast.20), channel_id=1, source_target_pairs={{0,1},{1,0},{2,3},{3,2},{4,5},{5,4},{6,7},{7,6},{8,9},{9,8},{10,11... | collective-permute-start | bytes 12582920 | tf_op jit(solution)/shard_map/ppermute | solution.py:101
  332.5 49.9 %collective-permute-start.37 = (bf16[4,128,1024]{2,1,0:T(8,128)(2,1)}, bf16[4,128,1024]{2,1,0:T(8,128)(2,1)S(1)}, u32[]{:S(2)}, u32[]{:S(2)}) collective-permute-start(bf16[4,128,1024]{2,1,0:T(8,128)(2,1)} %get-tuple-element.158), channel_id=1, source_target_pairs={{0,2},{2,0},{4,6},{6,4},{8,10},{10,8},{12,14},{14,12},{16,18},{18,... | collective-permute-start | bytes 3145736 | tf_op jit(solution)/shard_map/ppermute | solution.py:98
  333.7 48.7 %collective-permute-start.38 = (bf16[4,128,1024]{2,1,0:T(8,128)(2,1)}, bf16[4,128,1024]{2,1,0:T(8,128)(2,1)}, u32[]{:S(2)}, u32[]{:S(2)}) collective-permute-start(bf16[4,128,1024]{2,1,0:T(8,128)(2,1)} %get-tuple-element.159), channel_id=1, source_target_pairs={{0,4},{2,6},{4,0},{6,2},{8,12},{10,14},{12,8},{14,10},{16,20},{18,... | collective-permute-start | bytes 3145736 | tf_op jit(solution)/shard_map/ppermute | solution.py:98
  360.3 14.0 %collective-permute-start.39 = (bf16[2,32,4096]{2,1,0:T(8,128)(2,1)}, bf16[2,32,4096]{2,1,0:T(8,128)(2,1)}, u32[]{:S(2)}, u32[]{:S(2)}) collective-permute-start(bf16[2,32,4096]{2,1,0:T(8,128)(2,1)} %get-tuple-element.165), channel_id=1, source_target_pairs={{0,2},{2,0},{4,6},{6,4},{8,10},{10,8},{12,14},{14,12},{16,18},{18,... | collective-permute-start | bytes 1572872 | tf_op jit(solution)/shard_map/ppermute | solution.py:98
  362.1 13.7 %collective-permute-start.40 = (bf16[2,32,4096]{2,1,0:T(8,128)(2,1)}, bf16[2,32,4096]{2,1,0:T(8,128)(2,1)}, u32[]{:S(2)}, u32[]{:S(2)}) collective-permute-start(bf16[2,32,4096]{2,1,0:T(8,128)(2,1)} %get-tuple-element.166), channel_id=1, source_target_pairs={{0,4},{2,6},{4,0},{6,2},{8,12},{10,14},{12,8},{14,10},{16,20},{18,... | collective-permute-start | bytes 1572872 | tf_op jit(solution)/shard_map/ppermute | solution.py:98
  366.0 68.8 %collective-permute-start.43 = (bf16[4,2,2,32,1024]{4,3,2,1,0:T(8,128)(2,1)}, bf16[4,2,2,32,1024]{4,3,2,1,0:T(8,128)(2,1)}, u32[]{:S(2)}, u32[]{:S(2)}) collective-permute-start(bf16[4,2,2,32,1024]{4,3,2,1,0:T(8,128)(2,1)} %bitcast.22), channel_id=1, source_target_pairs={{0,1},{1,0},{2,3},{3,2},{4,5},{5,4},{6,7},{7,6},{8,9},{9,8},{10,11... | collective-permute-start | bytes 3145736 | tf_op jit(solution)/shard_map/ppermute | solution.py:101
  380.5 27.9 %collective-permute-start.41 = (bf16[4,32,4096]{2,1,0:T(8,128)(2,1)}, bf16[4,32,4096]{2,1,0:T(8,128)(2,1)S(1)}, u32[]{:S(2)}, u32[]{:S(2)}) collective-permute-start(bf16[4,32,4096]{2,1,0:T(8,128)(2,1)} %get-tuple-element.170), channel_id=1, source_target_pairs={{0,2},{2,0},{4,6},{6,4},{8,10},{10,8},{12,14},{14,12},{16,18},{18,... | collective-permute-start | bytes 3145736 | tf_op jit(solution)/shard_map/ppermute | solution.py:98
  380.8 27.6 %collective-permute-start.42 = (bf16[4,32,4096]{2,1,0:T(8,128)(2,1)}, bf16[4,32,4096]{2,1,0:T(8,128)(2,1)S(1)}, u32[]{:S(2)}, u32[]{:S(2)}) collective-permute-start(bf16[4,32,4096]{2,1,0:T(8,128)(2,1)} %get-tuple-element.171), channel_id=1, source_target_pairs={{0,4},{2,6},{4,0},{6,2},{8,12},{10,14},{12,8},{14,10},{16,20},{18,... | collective-permute-start | bytes 3145736 | tf_op jit(solution)/shard_map/ppermute | solution.py:98
  405.4 29.4 %collective-permute-start.44 = (bf16[4,2,2,32,1536]{4,3,2,1,0:T(8,128)(2,1)}, bf16[4,2,2,32,1536]{4,3,2,1,0:T(8,128)(2,1)}, u32[]{:S(2)}, u32[]{:S(2)}) collective-permute-start(bf16[4,2,2,32,1536]{4,3,2,1,0:T(8,128)(2,1)} %bitcast.24), channel_id=1, source_target_pairs={{0,1},{1,0},{2,3},{3,2},{4,5},{5,4},{6,7},{7,6},{8,9},{9,8},{10,11... | collective-permute-start | bytes 4718600 | tf_op jit(solution)/shard_map/ppermute | solution.py:101
  431.8 42.0 %collective-permute-start.48 = (bf16[32,8192]{1,0:T(8,128)(2,1)}, bf16[32,8192]{1,0:T(8,128)(2,1)}, u32[]{:S(2)}, u32[]{:S(2)}) collective-permute-start(bf16[32,8192]{1,0:T(8,128)(2,1)} %get-tuple-element.187), channel_id=1, source_target_pairs={{0,8},{2,10},{4,12},{6,14},{8,16},{10,18},{12,20},{14,22},{16,24},... | collective-permute-start | bytes 1572872 | tf_op jit(solution)/shard_map/ppermute | solution.py:98
  432.3 41.9 %collective-permute-start.49 = (bf16[32,8192]{1,0:T(8,128)(2,1)}, bf16[32,8192]{1,0:T(8,128)(2,1)}, u32[]{:S(2)}, u32[]{:S(2)}) collective-permute-start(bf16[32,8192]{1,0:T(8,128)(2,1)} %get-tuple-element.188), channel_id=1, source_target_pairs={{0,16},{2,18},{4,20},{6,22},{8,24},{10,26},{12,28},{14,30},{16,0},... | collective-permute-start | bytes 1572872 | tf_op jit(solution)/shard_map/ppermute | solution.py:98
  446.5 21.2 %collective-permute-start.47 = (bf16[4,2,2,32,1536]{4,3,2,1,0:T(8,128)(2,1)}, bf16[4,2,2,32,1536]{4,3,2,1,0:T(8,128)(2,1)}, u32[]{:S(2)}, u32[]{:S(2)}) collective-permute-start(bf16[4,2,2,32,1536]{4,3,2,1,0:T(8,128)(2,1)} %bitcast.26), channel_id=1, source_target_pairs={{0,1},{1,0},{2,3},{3,2},{4,5},{5,4},{6,7},{7,6},{8,9},{9,8},{10,11... | collective-permute-start | bytes 4718600 | tf_op jit(solution)/shard_map/ppermute | solution.py:101
  450.0 25.9 %collective-permute-start.50 = (bf16[32,8192]{1,0:T(8,128)(2,1)}, bf16[32,8192]{1,0:T(8,128)(2,1)}, u32[]{:S(2)}, u32[]{:S(2)}) collective-permute-start(bf16[32,8192]{1,0:T(8,128)(2,1)} %get-tuple-element.189), channel_id=1, source_target_pairs={{0,24},{2,26},{4,28},{6,30},{8,0},{10,2},{12,4},{14,6},{16,8},{18,... | collective-permute-start | bytes 1572872 | tf_op jit(solution)/shard_map/ppermute | solution.py:98
  456.0 39.1 %collective-permute-start.51 = (bf16[4,32,2560]{2,1,0:T(8,128)(2,1)}, bf16[4,32,2560]{2,1,0:T(8,128)(2,1)}, u32[]{:S(2)}, u32[]{:S(2)}) collective-permute-start(bf16[4,32,2560]{2,1,0:T(8,128)(2,1)} %get-tuple-element.193), channel_id=1, source_target_pairs={{0,2},{2,0},{4,6},{6,4},{8,10},{10,8},{12,14},{14,12},{16,18},{18,... | collective-permute-start | bytes 1966088 | tf_op jit(solution)/shard_map/ppermute | solution.py:98
  467.7 27.3 %collective-permute-start.52 = (bf16[4,32,2560]{2,1,0:T(8,128)(2,1)}, bf16[4,32,2560]{2,1,0:T(8,128)(2,1)}, u32[]{:S(2)}, u32[]{:S(2)}) collective-permute-start(bf16[4,32,2560]{2,1,0:T(8,128)(2,1)} %get-tuple-element.194), channel_id=1, source_target_pairs={{0,4},{2,6},{4,0},{6,2},{8,12},{10,14},{12,8},{14,10},{16,20},{18,... | collective-permute-start | bytes 1966088 | tf_op jit(solution)/shard_map/ppermute | solution.py:98
  474.3 13.8 %collective-permute-start.54 = (bf16[2,32,1536]{2,1,0:T(8,128)(2,1)}, bf16[2,32,1536]{2,1,0:T(8,128)(2,1)S(1)}, u32[]{:S(2)}, u32[]{:S(2)}) collective-permute-start(bf16[2,32,1536]{2,1,0:T(8,128)(2,1)} %get-tuple-element.201), channel_id=1, source_target_pairs={{0,4},{2,6},{4,0},{6,2},{8,12},{10,14},{12,8},{14,10},{16,20},{18,... | collective-permute-start | bytes 589832 | tf_op jit(solution)/shard_map/ppermute | solution.py:98
  492.9 11.3 %collective-permute-start.56 = (bf16[4,32,1536]{2,1,0:T(8,128)(2,1)}, bf16[4,32,1536]{2,1,0:T(8,128)(2,1)S(1)}, u32[]{:S(2)}, u32[]{:S(2)}) collective-permute-start(bf16[4,32,1536]{2,1,0:T(8,128)(2,1)} %get-tuple-element.203), channel_id=1, source_target_pairs={{0,2},{2,0},{4,6},{6,4},{8,10},{10,8},{12,14},{14,12},{16,18},{18,... | collective-permute-start | bytes 1179656 | tf_op jit(solution)/shard_map/ppermute | solution.py:98
  503.8 52.5 %collective-permute-start.55 = (f32[2,256,1024]{2,1,0:T(8,128)}, f32[2,256,1024]{2,1,0:T(8,128)}, u32[]{:S(2)}, u32[]{:S(2)}) collective-permute-start(f32[2,256,1024]{2,1,0:T(8,128)} %get-tuple-element.247), channel_id=1, source_target_pairs={{0,1},{1,0},{2,3},{3,2},{4,5},{5,4},{6,7},{7,6},{8,9},{9,8},{10,11... | collective-permute-start | bytes 6291464 | tf_op jit(solution)/shard_map/ppermute | solution.py:101
  515.3 11.9 %collective-permute-start.62 = (bf16[32,4096]{1,0:T(8,128)(2,1)}, bf16[32,4096]{1,0:T(8,128)(2,1)S(1)}, u32[]{:S(2)}, u32[]{:S(2)}) collective-permute-start(bf16[32,4096]{1,0:T(8,128)(2,1)} %get-tuple-element.207), channel_id=1, source_target_pairs={{0,8},{2,10},{4,12},{6,14},{8,16},{10,18},{12,20},{14,22},{16,24},... | collective-permute-start | bytes 786440 | tf_op jit(solution)/shard_map/ppermute | solution.py:98
  518.5 18.7 %collective-permute-start.63 = (bf16[32,4096]{1,0:T(8,128)(2,1)}, bf16[32,4096]{1,0:T(8,128)(2,1)S(1)}, u32[]{:S(2)}, u32[]{:S(2)}) collective-permute-start(bf16[32,4096]{1,0:T(8,128)(2,1)} %get-tuple-element.208), channel_id=1, source_target_pairs={{0,16},{2,18},{4,20},{6,22},{8,24},{10,26},{12,28},{14,30},{16,0},... | collective-permute-start | bytes 786440 | tf_op jit(solution)/shard_map/ppermute | solution.py:98
  520.5 16.7 %collective-permute-start.64 = (bf16[32,4096]{1,0:T(8,128)(2,1)}, bf16[32,4096]{1,0:T(8,128)(2,1)S(1)}, u32[]{:S(2)}, u32[]{:S(2)}) collective-permute-start(bf16[32,4096]{1,0:T(8,128)(2,1)} %get-tuple-element.209), channel_id=1, source_target_pairs={{0,24},{2,26},{4,28},{6,30},{8,0},{10,2},{12,4},{14,6},{16,8},{18,... | collective-permute-start | bytes 786440 | tf_op jit(solution)/shard_map/ppermute | solution.py:98
  (109 other events, 1936.8 us)
